TPU v7x, 256 devices: a whole 4x4x8 slice. The times are simulated.
256 devices in a mesh: tile: 128 (over y, z, x), nrn: 2 (over core).
Axes of the slice: x: 4, y: 4, z: 8, core: 2. Of those that a mesh axis runs over, the one named last changes fastest.
Arguments:
- movie: bfloat16 [2, 128, 1024, 1024], P('nrn', 'tile'), may hold values from 0.099609375 to 2
- shifts: int32 [2, 128, 2], P('nrn', 'tile'), may hold values from -4 to 4
- footprints: bfloat16 [12288, 16, 128], P('tile'), may hold values from 0.019897461 to 1
- blocks: int32 [12288, 16], P('tile'), may hold values from 0 to 4095, as said below
- traces: float32 [2, 12288, 4], P('nrn', 'tile'), may hold values from 0.1 to 2
- counts: int32 [128], P('tile'), may hold values from 24 to 96, as said below
Outputs:
- new_traces: float32 [2, 12288, 4], P('nrn', 'tile')
- new_footprints: bfloat16 [12288, 16, 128], P('tile')
Inputs may be any that keep to these rules, and one draw needn't show every extreme that they name: Each neuron has a plane z < 29, a block row r < 1 and a block column x < 63; blocks[k, 4 a + 2 d + e] = ((z + a) * 2 + r + d) * 64 + x + e for a in 0..3 and d, e in 0..1, so a neuron covers 2 x 2 blocks on each of 4 planes and reaches at most one block row below its tile's rows. `counts`: some tile is full and some holds 24 live neurons in every draw.
All inputs are finite; a program needn't handle non-finite values.
Results may differ from a plain program's by a relative error of at most 0.00105.
Values may be sent and summed in bfloat16 or wider, within the bound.
No kernel may reach another device: no remote copies, remote signals or barrier semaphores. Data moves between devices by JAX's collectives and lax.ppermute only.
A program may use at most 128 MiB of HBM per device.

v0:
```python
import jax
import jax.numpy as jnp
from jax import lax
from jax.experimental import pallas as pl
from jax.experimental.pallas import tpu as pltpu
from jax.sharding import PartitionSpec as P

Z = 32
PR = 8
PC = 16
VOX = PR * PC
NF = 8
KT = 96
NH = 2 * KT
NA = 4
XC = 32
FIELD = Z * XC
PADF = 4 * XC
EPSILON = 1e-06
VMEM_LIMIT = 56 * 1024 * 1024

F32 = jnp.float32
BF16 = jnp.bfloat16


def iota(shape, dim):
    return lax.broadcasted_iota(jnp.int32, shape, dim)


def vmem():
    return pl.BlockSpec(memory_space=pltpu.VMEM)


def smem():
    return pl.BlockSpec(memory_space=pltpu.SMEM)


def call(kernel, out_shape, in_specs, scratch=(), name=None):
    many = isinstance(out_shape, (list, tuple))
    return pl.pallas_call(
        kernel,
        out_shape=out_shape,
        in_specs=in_specs,
        out_specs=[vmem() for _ in out_shape] if many else vmem(),
        scratch_shapes=list(scratch),
        compiler_params=pltpu.CompilerParams(vmem_limit_bytes=VMEM_LIMIT),
        name=name,
    )


def register_kernel(shift_ref, movie_ref, out_ref):
    s = shift_ref[0]
    u = shift_ref[1]
    height, width = movie_ref.shape
    band = 128
    groups = width // 256
    src = iota((512, 256), 0) - 128
    dst = iota((512, 256), 1)
    lane = dst % 128
    column = (lane // PC) * 32 + (dst // 128) * PC + lane % PC
    pick = jnp.where(src == column - u, 1.0, 0.0).astype(BF16)
    for b in range(height // band):
        lo = max(0, b * band - 16)
        hi = min(height, b * band + band + 16)
        want = iota((band, hi - lo), 0) + b * band - s
        have = iota((band, hi - lo), 1) + lo
        move = jnp.where(want == have, 1.0, 0.0).astype(BF16)
        rows = jnp.dot(move, movie_ref[lo:hi, :], preferred_element_type=F32).astype(BF16)
        parts = []
        for g in range(groups):
            left = max(0, 256 * g - 128)
            right = min(width, 256 * g + 384)
            part = pick[left - 256 * g + 128 : right - 256 * g + 128, :]
            parts.append(jnp.dot(rows[:, left:right], part, preferred_element_type=F32))
        for t in range(band // PR):
            for c in range(2):
                piece = [p[t * PR : (t + 1) * PR, c * 128 : (c + 1) * 128] for p in parts]
                start = ((b * (band // PR) + t) * 2 + c) * groups * PR
                out_ref[start : start + groups * PR, :] = jnp.concatenate(piece, axis=0).astype(BF16)


def rows_kernel(live_ref, odd_ref, foot_ref, upper_ref, lower_ref, wide):
    wide[...] = foot_ref[...].astype(F32)
    live = live_ref[...] > 0
    odd = odd_ref[...] > 0
    for a in range(NA):
        for d, ref in ((0, upper_ref), (1, lower_ref)):
            first = wide[pl.ds(4 * a + 2 * d, KT, stride=16), :]
            second = wide[pl.ds(4 * a + 2 * d + 1, KT, stride=16), :]
            value = jnp.where(live, jnp.where(odd, second, first), 0.0)
            ref[a * KT : (a + 1) * KT, :] = value.astype(BF16)


def tile_at(ref, block):
    return ref.at[pl.ds(pl.multiple_of(block * PR, PR), PR), :]


def expand(upper_ref, lower_ref, tiles_ref):
    lane_in = iota((VOX, PR * VOX), 0)
    lane_out = iota((VOX, PR * VOX), 1)
    same = (lane_in // PC == lane_out // VOX) & (lane_in % PC == lane_out % PC)
    spread = jnp.where(same, 1.0, 0.0).astype(BF16)
    for a in range(NA):
        for d, ref in ((0, upper_ref), (1, lower_ref)):
            rows = ref[a * KT : (a + 1) * KT, :]
            wide = jnp.dot(rows, spread, preferred_element_type=F32)
            base = (a * NH + d * KT) * PR
            for i in range(PR):
                tiles_ref[pl.ds(base + i, KT, stride=PR), :] = wide[:, i * VOX : (i + 1) * VOX]


def zero(ref, rows):
    step = 256

    def body(k, carry):
        ref[pl.ds(pl.multiple_of(k * step, step), step), :] = jnp.zeros((step, VOX), F32)
        return carry

    lax.fori_loop(0, rows // step, body, 0)


def rebuild(place_ref, tiles_ref, trace_ref, field_ref):
    zero(field_ref, 2 * FIELD * PR)

    def body(n, carry):
        trace = jnp.broadcast_to(trace_ref[pl.ds(n, 1), :], (PR, VOX))
        base = place_ref[n]
        for a in range(NA):
            spot = tile_at(field_ref, base + a * XC)
            spot[...] = spot[...] + tile_at(tiles_ref, a * NH + n)[...] * trace
        return carry

    lax.fori_loop(0, NH, body, 0, unroll=4)


def project(place_ref, tiles_ref, field_ref, sums_ref):
    def body(n, carry):
        base = place_ref[n]
        total = tile_at(tiles_ref, n)[...] * tile_at(field_ref, base)[...]
        for a in range(1, NA):
            total = total + tile_at(tiles_ref, a * NH + n)[...] * tile_at(field_ref, base + a * XC)[...]
        tile_at(sums_ref, n)[...] = total
        return carry

    lax.fori_loop(0, NH, body, 0, unroll=4)
    rows = sums_ref[pl.ds(0, NH, stride=PR), :]
    for i in range(1, PR):
        rows = rows + sums_ref[pl.ds(i, NH, stride=PR), :]
    group = jnp.where(iota((VOX, VOX), 0) // PC == iota((VOX, VOX), 1) // PC, 1.0, 0.0)
    return jnp.dot(rows, group, preferred_element_type=F32, precision=lax.Precision.HIGHEST)


def denom_kernel(place_ref, upper_ref, lower_ref, trace_ref, tiles_ref, denom_ref, field, sums):
    expand(upper_ref, lower_ref, tiles_ref)
    rebuild(place_ref, tiles_ref, trace_ref, field)
    denom_ref[...] = project(place_ref, tiles_ref, field, sums)


def frames_to_lanes(tiles):
    lane = iota((PR, VOX), 1)
    for k in range(3):
        step = 1 << k
        width = PC * step
        odd = (lane // width) % 2 == 1
        after = list(tiles)
        for f in range(NF):
            if f & step:
                continue
            a, b = tiles[f], tiles[f | step]
            after[f] = jnp.where(odd, pltpu.roll(b, width, 1), a)
            after[f | step] = jnp.where(odd, b, pltpu.roll(a, VOX - width, 1))
        tiles = after
    return tiles


def numer_kernel(place_ref, tiles_ref, image_ref, field_ref, numer_ref, sums):
    def body(z, carry):
        groups = XC // 8
        rows = groups * PR
        base = pl.multiple_of(z * (NF * rows), NF * rows)
        image = image_ref[pl.ds(base, NF * rows), :].astype(F32)
        for g in range(groups):
            tiles = [image[f * rows + g * PR : f * rows + (g + 1) * PR, :] for f in range(NF)]
            tiles = frames_to_lanes(tiles)
            for x in range(8):
                tile_at(field_ref, z * XC + g * 8 + x)[...] = tiles[x]
        return carry

    lax.fori_loop(0, Z, body, 0)
    field_ref[FIELD * PR : (FIELD + PADF) * PR, :] = jnp.zeros((PADF * PR, VOX), F32)
    numer_ref[...] = project(place_ref, tiles_ref, field_ref, sums)


def fold(products_ref):
    lane_in = iota((VOX, VOX), 0)
    lane_out = iota((VOX, VOX), 1)
    total = None
    for i in range(PR):
        pick = jnp.where((lane_out // PC == i) & (lane_out % PC == lane_in % PC), 1.0, 0.0).astype(BF16)
        rows = products_ref[pl.ds(i, NA * NH, stride=PR), :]
        high = rows.astype(BF16)
        low = (rows - high.astype(F32)).astype(BF16)
        part = jnp.dot(high, pick, preferred_element_type=F32) + jnp.dot(low, pick, preferred_element_type=F32)
        total = part if total is None else total + part
    return total


def update_kernel(
    place_ref, spot_ref, upper_ref, lower_ref, tiles_ref, image_ref, old_ref, numer_ref, denom_ref,
    trace_ref, upper_out, lower_out, field, product_n, product_d,
):
    trace_ref[...] = old_ref[...] * numer_ref[...] / (denom_ref[...] + EPSILON)
    rebuild(place_ref, tiles_ref, trace_ref, field)

    def body(n, carry):
        trace = jnp.broadcast_to(trace_ref[pl.ds(n, 1), :], (PR, VOX))
        base = place_ref[n]
        spot = spot_ref[n]
        for a in range(NA):
            m = a * NH + n
            tile_at(product_n, m)[...] = tile_at(image_ref, spot + a * XC)[...] * trace
            tile_at(product_d, m)[...] = tile_at(field, base + a * XC)[...] * trace
        return carry

    lax.fori_loop(0, NH, body, 0, unroll=4)
    ratio = fold(product_n) / (fold(product_d) + EPSILON)
    for a in range(NA):
        for d, ref, out in ((0, upper_ref, upper_out), (1, lower_ref, lower_out)):
            start = a * NH + d * KT
            value = ref[a * KT : (a + 1) * KT, :].astype(F32) * ratio[start : start + KT, :]
            out[a * KT : (a + 1) * KT, :] = value.astype(BF16)


def merge_kernel(odd_ref, upper_ref, lower_ref, upper_other, lower_other, out_ref, wide):
    odd = odd_ref[...] > 0
    for a in range(NA):
        rows = slice(a * KT, (a + 1) * KT)
        for d, mine_ref, other_ref in ((0, upper_ref, upper_other), (1, lower_ref, lower_other)):
            mine = mine_ref[rows, :].astype(F32)
            other = other_ref[rows, :].astype(F32)
            wide[pl.ds(4 * a + 2 * d, KT, stride=16), :] = jnp.where(odd, other, mine)
            wide[pl.ds(4 * a + 2 * d + 1, KT, stride=16), :] = jnp.where(odd, mine, other)
    out_ref[...] = wide[...].astype(BF16)


def shards(movie, shifts, footprints, blocks, traces, counts):
    tiles = lax.axis_size("tile")
    tile = lax.axis_index("tile")
    core = lax.axis_index("nrn")
    down = [(i, (i + 1) % tiles) for i in range(tiles)]
    up = [(j, i) for i, j in down]
    cross = [(0, 1), (1, 0)]

    def shape(rows, dtype):
        return jax.ShapeDtypeStruct((rows, VOX), dtype)

    sent = call(
        register_kernel, shape(tiles * 2 * XC // 8 * PR, BF16), [smem(), vmem()], name="register"
    )(shifts[0, 0], movie[0, 0])
    images = lax.all_to_all(
        sent.reshape(tiles * 2, XC // 8 * PR, VOX), ("tile", "nrn"), split_axis=0, concat_axis=0, tiled=True
    ).reshape(-1, VOX)

    first = blocks[:, 0]
    plane = first // 128
    column = first % 64
    odd = (column + core) % 2
    base = plane * XC + (column + odd) // 2
    live = (jnp.arange(KT, dtype=jnp.int32) < counts[0]).astype(jnp.int32)
    odd_rows = jnp.broadcast_to(odd[:, None], (KT, VOX))
    live_rows = jnp.broadcast_to(live[:, None], (KT, VOX))
    upper, lower = call(
        rows_kernel, [shape(NA * KT, BF16)] * 2, [vmem()] * 3,
        scratch=[pltpu.VMEM((KT * 16, VOX), F32)], name="rows",
    )(live_rows, odd_rows, footprints.reshape(-1, VOX))

    mine = traces[0]
    theirs = lax.ppermute(mine, "nrn", cross)
    even_frames = jnp.where(core == 0, mine, theirs)
    odd_frames = jnp.where(core == 0, theirs, mine)
    frames = jnp.stack([even_frames, odd_frames], axis=-1).reshape(KT, NF)
    packet = jnp.concatenate([frames, jnp.broadcast_to(base.astype(F32)[:, None], (KT, NF))], axis=1)
    packet_in = lax.ppermute(packet, "tile", down)
    lower_in = lax.ppermute(lower, "tile", down)
    base_in = packet_in[:, NF].astype(jnp.int32)
    margin = tile == 0
    place = jnp.concatenate([base, base_in + jnp.where(margin, FIELD, 0)])
    spot = jnp.concatenate([base, jnp.where(margin, FIELD, base_in)])
    both = jnp.concatenate([frames, packet_in[:, :NF]], axis=0)
    old = jnp.broadcast_to(both[:, :, None], (NH, NF, PC)).reshape(NH, VOX)

    field = pltpu.VMEM((2 * FIELD * PR, VOX), F32)
    sums = pltpu.VMEM((NH * PR, VOX), F32)
    tiles_e, denom = call(
        denom_kernel, [shape(NA * NH * PR, F32), shape(NH, F32)], [smem()] + [vmem()] * 3,
        scratch=[field, sums], name="denominator",
    )(place, upper, lower_in, old)

    def complete(partial):
        partial = partial + lax.ppermute(partial, "nrn", cross)
        from_above = lax.ppermute(partial[:KT], "tile", down)
        from_below = lax.ppermute(partial[KT:], "tile", up)
        return partial + jnp.concatenate([from_below, from_above], axis=0)

    denom = complete(denom)
    image_field, numer = call(
        numer_kernel, [shape((FIELD + PADF) * PR, F32), shape(NH, F32)], [smem()] + [vmem()] * 2,
        scratch=[sums], name="numerator",
    )(spot, tiles_e, images)
    numer = complete(numer)

    product = pltpu.VMEM((NA * NH * PR, VOX), F32)
    new, upper_new, lower_new = call(
        update_kernel, [shape(NH, F32), shape(NA * KT, BF16), shape(NA * KT, BF16)], [smem()] * 2 + [vmem()] * 7,
        scratch=[field, product, product], name="update",
    )(place, spot, upper, lower_in, tiles_e, image_field, old, numer, denom)

    lower_back = lax.ppermute(lower_new, "tile", up)
    upper_other = lax.ppermute(upper_new, "nrn", cross)
    lower_other = lax.ppermute(lower_back, "nrn", cross)
    merged = call(
        merge_kernel, shape(KT * 16, BF16), [vmem()] * 5,
        scratch=[pltpu.VMEM((KT * 16, VOX), F32)], name="merge",
    )(odd_rows, upper_new, lower_back, upper_other, lower_other)

    frames_new = new[:KT].reshape(KT, NF, PC)[:, :, 0].reshape(KT, NF // 2, 2)
    updated = jnp.where(core == 0, frames_new[:, :, 0], frames_new[:, :, 1])
    return updated[None], merged.reshape(KT, 16, VOX)


def solution(mesh):
    placed = (
        P("nrn", "tile", None, None),
        P("nrn", "tile", None),
        P("tile", None, None),
        P("tile", None),
        P("nrn", "tile", None),
        P("tile"),
    )
    return jax.shard_map(
        shards,
        mesh=mesh,
        in_specs=placed,
        out_specs=(P("nrn", "tile", None), P("tile", None, None)),
        check_vma=False,
    )
```

profile of v0, /device:TPU:1, one launch (start us, length us, event | category | flops | bytes accessed | tf_op | source)
XLA Modules:
  0.0 139.4 jit_solution(11523085600186727012)
XLA Ops:
  0.6 5.3 %register.1 = bf16[8192,128]{1,0:T(8,128)(2,1)} custom-call(s32[2]{0:T(128)} %bitcast.53, bf16[1024,1024]{1,0:T(8,128)(2,1)} %bitcast.42), custom_call_target="tpu_custom_call" | custom-call | tf_op jit(solution)/shard_map/register/pallas_call | solution.py:257
  6.0 0.0 copy-start.5
  6.0 15.7 %all-to-all-start = ((bf16[256,32,128]{2,1,0:T(8,128)(2,1)}), bf16[256,32,128]{2,1,0:T(8,128)(2,1)S(1)}, u32[]{:S(2)}, u32[]{:S(2)}) async-start(bf16[256,32,128]{2,1,0:T(8,128)(2,1)} %bitcast.41), calls=%async_computation | async-start | bytes 4194304 | tf_op jit(solution)/shard_map/all_to_all | solution.py:260
  21.6 0.0 copy-done.5
  21.6 2.2 %collective-permute-start = (f32[96,4]{0,1:T(4,128)S(1)}, f32[96,4]{0,1:T(4,128)S(1)}, u32[]{:S(2)}, u32[]{:S(2)}) collective-permute-start(f32[96,4]{0,1:T(4,128)S(1)} %bitcast.51), channel_id=1, source_target_pairs={{0,1},{1,0},{2,3},{3,2},{4,5},{5,4},{6,7},{7,6},{8,9},{9,8},{10,11... | collective-permute-start | bytes 4616 | tf_op jit(solution)/shard_map/ppermute | solution.py:278
  24.5 0.7 convert_bitcast_fusion
  25.2 0.7 broadcast_in_dim.38.odd_ref
  25.9 0.7 broadcast_in_dim.36.live_ref
  26.6 2.0 %rows.1 = (bf16[384,128]{1,0:T(8,128)(2,1)}, bf16[384,128]{1,0:T(8,128)(2,1)}) custom-call(s32[96,128]{1,0:T(8,128)} %broadcast_in_dim.36.live_ref, s32[96,128]{1,0:T(8,128)} %broadcast_in_dim.38.odd_ref, bf16[1536,128]{1,0:T(8,128)(2,1)} %bitcast.45), custom_call_target="tpu_custom_call" | custom-call | tf_op jit(solution)/shard_map/rows/pallas_call | solution.py:272
  28.6 0.0 collective-permute-start.2
  28.6 0.0 collective-permute-done
  28.7 0.8 collective-permute-start.1
  29.5 0.7 fusion.4
  30.3 46.3 %collective-permute-done.1 = f32[96,16]{0,1:T(8,128)S(1)} collective-permute-done((f32[96,16]{0,1:T(8,128)S(1)}, f32[96,16]{0,1:T(8,128)S(1)}, u32[]{:S(2)}, u32[]{:S(2)}) %collective-permute-start.1) | collective-permute-done | bytes 6176 | tf_op jit(solution)/shard_map/ppermute | solution.py:283
  76.6 0.1 pad_maximum_fusion.1
  76.7 0.7 copy.10.trace_ref.old_ref
  77.4 0.6 pad_add_fusion
  78.1 0.0 collective-permute-done.2.lower_ref
  78.1 0.0 copy-start.1
  78.1 0.6 copy-done.1
  78.7 5.7 %denominator.1 = (f32[6144,128]{1,0:T(8,128)}, f32[192,128]{1,0:T(8,128)}) custom-call(s32[192]{0:T(256)} %get-tuple-element.31.place_ref, bf16[384,128]{1,0:T(8,128)(2,1)} %get-tuple-element.11.upper_ref, bf16[384,128]{1,0:T(8,128)(2,1)} %copy-done.1, f32[192,128]{1,0:T(8,128)} %copy.10.trace_ref.old_ref), custom_call_target="tpu_custom_call" | custom-call | tf_op jit(solution)/shard_map/denominator/pallas_call | solution.py:294
  84.4 1.0 collective-permute-start.6
  85.5 1.2 collective-permute-done.6
  86.6 0.9 add.84
  87.5 0.0 all-to-all-done
  87.5 0.0 copy-start
  87.6 1.4 copy-done
  88.9 13.1 %numerator.1 = (f32[9216,128]{1,0:T(8,128)}, f32[192,128]{1,0:T(8,128)}) custom-call(s32[192]{0:T(256)} %get-tuple-element.30.place_ref.spot_ref, f32[6144,128]{1,0:T(8,128)} %get-tuple-element.13.tiles_ref, bf16[8192,128]{1,0:T(8,128)(2,1)} %bitcast.40), custom_call_target="tpu_custom_call" | custom-call | tf_op jit(solution)/shard_map/numerator/pallas_call | solution.py:306
  102.0 0.4 collective-permute-start.3
  102.4 0.1 collective-permute-start.7
  102.4 1.5 %collective-permute-start.8 = (f32[96,128]{1,0:T(8,128)S(1)}, f32[96,128]{1,0:T(8,128)S(1)}, u32[]{:S(2)}, u32[]{:S(2)}) collective-permute-start(f32[96,128]{1,0:T(8,128)S(1)} %get-tuple-element.23), channel_id=1, source_target_pairs={{0,2},{2,4},{4,6},{6,8},{8,10},{10,12},{12,14},{14,16},{16,18},{18... | collective-permute-start | bytes 147464 | tf_op jit(solution)/shard_map/ppermute | solution.py:301
  103.9 0.0 collective-permute-done.3
  103.9 0.9 add.82
  104.8 5.6 %collective-permute-start.4 = (f32[96,128]{1,0:T(8,128)S(1)}, f32[96,128]{1,0:T(8,128)S(1)}, u32[]{:S(2)}, u32[]{:S(2)}) collective-permute-start(f32[96,128]{1,0:T(8,128)S(1)} %get-tuple-element.24), channel_id=1, source_target_pairs={{2,0},{4,2},{6,4},{8,6},{10,8},{12,10},{14,12},{16,14},{18,16},{20... | collective-permute-start | bytes 147464 | tf_op jit(solution)/shard_map/ppermute | solution.py:302
  110.4 0.0 collective-permute-start.5
  110.4 0.0 collective-permute-done.7
  110.4 0.5 collective-permute-done.8
  110.9 0.6 maximum_add_fusion.1.denom_ref
  111.5 0.1 collective-permute-done.4
  111.6 7.2 %collective-permute-done.5 = f32[96,128]{1,0:T(8,128)S(1)} collective-permute-done((f32[96,128]{1,0:T(8,128)S(1)}, f32[96,128]{1,0:T(8,128)S(1)}, u32[]{:S(2)}, u32[]{:S(2)}) %collective-permute-start.5) | collective-permute-done | bytes 49184 | tf_op jit(solution)/shard_map/ppermute | solution.py:301
  118.8 0.6 maximum_add_fusion.numer_ref
  119.4 9.2 %update.1 = (f32[192,128]{1,0:T(8,128)}, bf16[384,128]{1,0:T(8,128)(2,1)}, bf16[384,128]{1,0:T(8,128)(2,1)}) custom-call(s32[192]{0:T(256)} %get-tuple-element.31.place_ref, s32[192]{0:T(256)} %get-tuple-element.30.place_ref.spot_ref, bf16[384,128]{1,0:T(8,128)(2,1)} %get-tuple-element.11.upper_ref, bf16[384,128]{1,0:T(8,128)(2,1)} %copy-done.1, ...), custom_call_target="tpu_custom_call" | custom-call | tf_op jit(solution)/shard_map/update/pallas_call | solution.py:313
  128.6 0.0 collective-permute-start.9
  128.6 0.8 slice.40
  129.4 0.1 copy.12
  129.5 2.0 %collective-permute-start.10 = (bf16[384,128]{1,0:T(8,128)(2,1)}, bf16[384,128]{1,0:T(8,128)(2,1)S(1)}, u32[]{:S(2)}, u32[]{:S(2)}) collective-permute-start(bf16[384,128]{1,0:T(8,128)(2,1)} %get-tuple-element.18.upper_ref), channel_id=1, source_target_pairs={{0,1},{1,0},{2,3},{3,2},{4,5},{5,4},{6,7},{7,6},{8,9},{9,8},{10,11... | collective-permute-start | bytes 294920 | tf_op jit(solution)/shard_map/ppermute | solution.py:319
  131.5 0.8 collective-permute-done.9.lower_ref
  132.3 0.0 copy-start.2
  132.3 3.0 %collective-permute-start.11 = (bf16[384,128]{1,0:T(8,128)(2,1)S(1)}, bf16[384,128]{1,0:T(8,128)(2,1)S(1)}, u32[]{:S(2)}, u32[]{:S(2)}) collective-permute-start(bf16[384,128]{1,0:T(8,128)(2,1)S(1)} %collective-permute-done.9.lower_ref), channel_id=1, source_target_pairs={{0,1},{1,0},{2,3},{3,2},{4,5},{5,4},{6,7},{7,6},{8,9},{9,8},{10,11... | collective-permute-start | bytes 294920 | tf_op jit(solution)/shard_map/ppermute | solution.py:320
  135.3 0.6 broadcast_select_fusion
  135.9 0.0 collective-permute-done.10.upper_other
  135.9 0.0 copy-start.3
  135.9 0.4 collective-permute-done.11.lower_other
  136.3 0.0 copy-done.2
  136.3 0.3 copy-done.3
  136.5 0.0 copy-start.4
  136.5 0.6 copy-done.4
  137.2 2.2 %merge.1 = bf16[1536,128]{1,0:T(8,128)(2,1)} custom-call(s32[96,128]{1,0:T(8,128)} %broadcast_in_dim.38.odd_ref, bf16[384,128]{1,0:T(8,128)(2,1)} %get-tuple-element.18.upper_ref, bf16[384,128]{1,0:T(8,128)(2,1)} %copy-done.2, bf16[384,128]{1,0:T(8,128)(2,1)} %copy-done.3, bf16[384,128]{1,0:T(8,128)(2,1)} %copy-done.4), custom_call_target="tpu_custom_call" | custom-call | tf_op jit(solution)/shard_map/merge/pallas_call | solution.py:321
  (12 shorter events, 0.1 us)
Async XLA Ops:
  6.0 15.7 %copy-start.5 = (f32[1,96,4]{1,2,0:T(4,128)S(1)}, f32[1,96,4]{1,2,0:T(4,128)}, u32[]{:S(2)}) copy-start(f32[1,96,4]{1,2,0:T(4,128)} %param.10) | copy-start | bytes 4612
  6.0 81.6 %all-to-all-start = ((bf16[256,32,128]{2,1,0:T(8,128)(2,1)}), bf16[256,32,128]{2,1,0:T(8,128)(2,1)S(1)}, u32[]{:S(2)}, u32[]{:S(2)}) async-start(bf16[256,32,128]{2,1,0:T(8,128)(2,1)} %bitcast.41), calls=%async_computation | async-start | bytes 4194304 | tf_op jit(solution)/shard_map/all_to_all | solution.py:260
  21.6 7.0 %collective-permute-start = (f32[96,4]{0,1:T(4,128)S(1)}, f32[96,4]{0,1:T(4,128)S(1)}, u32[]{:S(2)}, u32[]{:S(2)}) collective-permute-start(f32[96,4]{0,1:T(4,128)S(1)} %bitcast.51), channel_id=1, source_target_pairs={{0,1},{1,0},{2,3},{3,2},{4,5},{5,4},{6,7},{7,6},{8,9},{9,8},{10,11... | collective-permute-start | bytes 4616 | tf_op jit(solution)/shard_map/ppermute | solution.py:278
  28.6 49.5 %collective-permute-start.2 = (bf16[384,128]{1,0:T(8,128)(2,1)}, bf16[384,128]{1,0:T(8,128)(2,1)S(1)}, u32[]{:S(2)}, u32[]{:S(2)}) collective-permute-start(bf16[384,128]{1,0:T(8,128)(2,1)} %get-tuple-element.12), channel_id=1, source_target_pairs={{0,2},{2,4},{4,6},{6,8},{8,10},{10,12},{12,14},{14,16},{16,18},{18... | collective-permute-start | bytes 294920 | tf_op jit(solution)/shard_map/ppermute | solution.py:284
  28.7 47.9 %collective-permute-start.1 = (f32[96,16]{0,1:T(8,128)S(1)}, f32[96,16]{0,1:T(8,128)S(1)}, u32[]{:S(2)}, u32[]{:S(2)}) collective-permute-start(f32[96,16]{0,1:T(8,128)S(1)} %pad_maximum_fusion), channel_id=1, source_target_pairs={{0,2},{2,4},{4,6},{6,8},{8,10},{10,12},{12,14},{14,16},{16,18},{18... | collective-permute-start | bytes 18440 | tf_op jit(solution)/shard_map/ppermute | solution.py:283
  78.1 0.6 copy-start.1
  84.4 2.2 %collective-permute-start.6 = (f32[192,128]{1,0:T(8,128)}, f32[192,128]{1,0:T(8,128)S(1)}, u32[]{:S(2)}, u32[]{:S(2)}) collective-permute-start(f32[192,128]{1,0:T(8,128)} %get-tuple-element.16), channel_id=1, source_target_pairs={{0,1},{1,0},{2,3},{3,2},{4,5},{5,4},{6,7},{7,6},{8,9},{9,8},{10,11... | collective-permute-start | bytes 294920 | tf_op jit(solution)/shard_map/ppermute | solution.py:300
  87.5 1.4 copy-start
  102.0 1.9 %collective-permute-start.3 = (f32[192,128]{1,0:T(8,128)}, f32[192,128]{1,0:T(8,128)S(1)}, u32[]{:S(2)}, u32[]{:S(2)}) collective-permute-start(f32[192,128]{1,0:T(8,128)} %get-tuple-element.15), channel_id=1, source_target_pairs={{0,1},{1,0},{2,3},{3,2},{4,5},{5,4},{6,7},{7,6},{8,9},{9,8},{10,11... | collective-permute-start | bytes 294920 | tf_op jit(solution)/shard_map/ppermute | solution.py:300
  102.4 8.1 %collective-permute-start.7 = (f32[96,128]{1,0:T(8,128)S(1)}, f32[96,128]{1,0:T(8,128)S(1)}, u32[]{:S(2)}, u32[]{:S(2)}) collective-permute-start(f32[96,128]{1,0:T(8,128)S(1)} %get-tuple-element.22), channel_id=1, source_target_pairs={{2,0},{4,2},{6,4},{8,6},{10,8},{12,10},{14,12},{16,14},{18,16},{20... | collective-permute-start | bytes 147464 | tf_op jit(solution)/shard_map/ppermute | solution.py:302
  102.4 8.4 %collective-permute-start.8 = (f32[96,128]{1,0:T(8,128)S(1)}, f32[96,128]{1,0:T(8,128)S(1)}, u32[]{:S(2)}, u32[]{:S(2)}) collective-permute-start(f32[96,128]{1,0:T(8,128)S(1)} %get-tuple-element.23), channel_id=1, source_target_pairs={{0,2},{2,4},{4,6},{6,8},{8,10},{10,12},{12,14},{14,16},{16,18},{18... | collective-permute-start | bytes 147464 | tf_op jit(solution)/shard_map/ppermute | solution.py:301
  104.8 6.8 %collective-permute-start.4 = (f32[96,128]{1,0:T(8,128)S(1)}, f32[96,128]{1,0:T(8,128)S(1)}, u32[]{:S(2)}, u32[]{:S(2)}) collective-permute-start(f32[96,128]{1,0:T(8,128)S(1)} %get-tuple-element.24), channel_id=1, source_target_pairs={{2,0},{4,2},{6,4},{8,6},{10,8},{12,10},{14,12},{16,14},{18,16},{20... | collective-permute-start | bytes 147464 | tf_op jit(solution)/shard_map/ppermute | solution.py:302
  110.4 8.4 %collective-permute-start.5 = (f32[96,128]{1,0:T(8,128)S(1)}, f32[96,128]{1,0:T(8,128)S(1)}, u32[]{:S(2)}, u32[]{:S(2)}) collective-permute-start(f32[96,128]{1,0:T(8,128)S(1)} %get-tuple-element.25), channel_id=1, source_target_pairs={{0,2},{2,4},{4,6},{6,8},{8,10},{10,12},{12,14},{14,16},{16,18},{18... | collective-permute-start | bytes 147464 | tf_op jit(solution)/shard_map/ppermute | solution.py:301
  128.6 3.7 %collective-permute-start.9 = (bf16[384,128]{1,0:T(8,128)(2,1)}, bf16[384,128]{1,0:T(8,128)(2,1)S(1)}, u32[]{:S(2)}, u32[]{:S(2)}) collective-permute-start(bf16[384,128]{1,0:T(8,128)(2,1)} %get-tuple-element.19), channel_id=1, source_target_pairs={{2,0},{4,2},{6,4},{8,6},{10,8},{12,10},{14,12},{16,14},{18,16},{20... | collective-permute-start | bytes 294920 | tf_op jit(solution)/shard_map/ppermute | solution.py:318
  129.5 6.4 %collective-permute-start.10 = (bf16[384,128]{1,0:T(8,128)(2,1)}, bf16[384,128]{1,0:T(8,128)(2,1)S(1)}, u32[]{:S(2)}, u32[]{:S(2)}) collective-permute-start(bf16[384,128]{1,0:T(8,128)(2,1)} %get-tuple-element.18.upper_ref), channel_id=1, source_target_pairs={{0,1},{1,0},{2,3},{3,2},{4,5},{5,4},{6,7},{7,6},{8,9},{9,8},{10,11... | collective-permute-start | bytes 294920 | tf_op jit(solution)/shard_map/ppermute | solution.py:319
  132.3 4.0 %copy-start.2 = (bf16[384,128]{1,0:T(8,128)(2,1)}, bf16[384,128]{1,0:T(8,128)(2,1)S(1)}, u32[]{:S(2)}) copy-start(bf16[384,128]{1,0:T(8,128)(2,1)S(1)} %collective-permute-done.9.lower_ref) | copy-start | bytes 294916
  132.3 4.0 %collective-permute-start.11 = (bf16[384,128]{1,0:T(8,128)(2,1)S(1)}, bf16[384,128]{1,0:T(8,128)(2,1)S(1)}, u32[]{:S(2)}, u32[]{:S(2)}) collective-permute-start(bf16[384,128]{1,0:T(8,128)(2,1)S(1)} %collective-permute-done.9.lower_ref), channel_id=1, source_target_pairs={{0,1},{1,0},{2,3},{3,2},{4,5},{5,4},{6,7},{7,6},{8,9},{9,8},{10,11... | collective-permute-start | bytes 294920 | tf_op jit(solution)/shard_map/ppermute | solution.py:320
  135.9 0.6 copy-start.3
  136.5 0.6 copy-start.4
where the time goes:
time: 140 us; the launch traced here: 139 us
  waiting for transfers between devices  56.4 us (40%)
  Pallas kernels  37.5 us (27%)
  starting transfers between devices  32.2 us (23%)
  local copies, waits for them, and re-layouts  5.99 us (4%)
  other arithmetic  5.85 us (4%)
  between operations  1.43 us (1%)
    ppermute x1, waiting for transfers between devices, shards(): packet_in = lax.ppermute(packet, 'tile', down)  46.3 us
    all_to_all x1, starting transfers between devices, shards(): lax.all_to_all(sent.reshape(tiles * 2, XC // 8 * PR, VOX), ('tile', 'nrn'...  15.7 us
    pallas_call x1, Pallas kernels, shards(): call(numer_kernel, [shape((FIELD + PADF) * PR, F32), shape(NH, F32)], [sm...  13.1 us
    pallas_call x1, Pallas kernels, shards(): call(update_kernel, [shape(NH, F32), shape(NA * KT, BF16), shape(NA * KT,...  9.17 us
    ppermute x2, waiting for transfers between devices, complete(): from_above = lax.ppermute(partial[:KT], 'tile', down)  7.65 us
    pallas_call x1, Pallas kernels, shards(): call(denom_kernel, [shape(NA * NH * PR, F32), shape(NH, F32)], [smem()] +...  5.73 us
    ppermute x2, starting transfers between devices, complete(): from_below = lax.ppermute(partial[KT:], 'tile', up)  5.67 us
    pallas_call x1, Pallas kernels, shards(): call(register_kernel, shape(tiles * 2 * XC // 8 * PR, BF16), [smem(), vme...  5.32 us
  transfers between devices with their start and end apart: 13, of which 7 were waited for; matrix products, arithmetic and copies ran while one was open for 6% of the time, Pallas kernels for 6%

commit v1 on v0

v1 whole, which is shorter than its diff:
```python
import jax
import jax.numpy as jnp
from jax import lax
from jax.experimental import pallas as pl
from jax.experimental.pallas import tpu as pltpu
from jax.sharding import PartitionSpec as P

Z = 32
PR = 8
PC = 16
VOX = PR * PC
BAND = 224
NF = 8
KT = 96
NH = 2 * KT
NA = 4
XC = 32
TILES = NA * NH
FIELD = Z * XC
PADF = 4 * XC
EPSILON = 1e-06
MIB = 1024 * 1024

F32 = jnp.float32
BF16 = jnp.bfloat16


def iota(shape, dim):
    return lax.broadcasted_iota(jnp.int32, shape, dim)


def vmem():
    return pl.BlockSpec(memory_space=pltpu.VMEM)


def smem():
    return pl.BlockSpec(memory_space=pltpu.SMEM)


def call(kernel, out_shape, in_specs, scratch=(), name=None, limit=24, out_specs=None):
    if out_specs is None:
        out_specs = [vmem() for _ in out_shape] if isinstance(out_shape, (list, tuple)) else vmem()
    return pl.pallas_call(
        kernel,
        out_shape=out_shape,
        in_specs=in_specs,
        out_specs=out_specs,
        scratch_shapes=list(scratch),
        compiler_params=pltpu.CompilerParams(vmem_limit_bytes=limit * MIB),
        name=name,
    )


def rows_kernel(count_ref, block_ref, foot_ref, upper_ref, packet_ref, odd_ref, wide):
    core = lax.axis_index("nrn")
    first = block_ref[...]
    ones = jnp.where(iota((16, VOX), 0) == 0, 1.0, 0.0).astype(BF16)

    def down_rows(values):
        return lax.dot_general(
            values.astype(F32).astype(BF16), ones, (((0,), (0,)), ((), ())), preferred_element_type=F32
        )

    plane = down_rows(first // 128)
    column = down_rows(first % 64).astype(jnp.int32)
    odd = (column + core) % 2
    place = (column + odd) // 2
    live = iota((KT, VOX), 0) < count_ref[0]
    odd_ref[...] = odd
    info = jnp.where(iota((KT, VOX), 1) < 64, plane, place.astype(F32))
    packet_ref[NA * KT : NA * KT + KT, :] = info.astype(BF16)
    wide[...] = foot_ref[...].astype(F32)
    for a in range(NA):
        for d, ref in ((0, upper_ref), (1, packet_ref)):
            left = wide[pl.ds(4 * a + 2 * d, KT, stride=16), :]
            right = wide[pl.ds(4 * a + 2 * d + 1, KT, stride=16), :]
            value = jnp.where(live, jnp.where(odd > 0, right, left), 0.0)
            ref[a * KT : (a + 1) * KT, :] = value.astype(BF16)


def register_kernel(shift_ref, movie_ref, out_ref, image, laid, load_sem, store_sem):
    height, width = movie_ref.shape
    bands = [(lo, min(height, lo + BAND)) for lo in range(0, height, BAND)]
    edges = [0] + [min(height, hi + 16) for _, hi in bands]
    loads = []
    for b in range(len(bands)):
        rows = pl.ds(edges[b], edges[b + 1] - edges[b])
        loads.append(pltpu.make_async_copy(movie_ref.at[rows, :], image.at[rows, :], load_sem.at[b]))
        loads[-1].start()
    s = shift_ref[0]
    u = shift_ref[1]
    groups = width // 256
    src = iota((512, 256), 0) - 128
    lane = iota((512, 256), 1) % 128
    want_column = (lane // PC) * 32 + (iota((512, 256), 1) // 128) * PC + lane % PC
    pick = jnp.where(src == want_column - u, 1.0, 0.0).astype(BF16)
    stores = []
    for b, (first, last) in enumerate(bands):
        loads[b].wait()
        lo = max(0, first - 16)
        hi = min(height, last + 16)
        want = iota((last - first, hi - lo), 0) + first - s
        have = iota((last - first, hi - lo), 1) + lo
        move = jnp.where(want == have, 1.0, 0.0).astype(BF16)
        rows = jnp.dot(move, image[lo:hi, :], preferred_element_type=F32).astype(BF16)
        parts = []
        for g in range(groups):
            start = max(0, 256 * g - 128)
            stop = min(width, 256 * g + 384)
            part = pick[start - 256 * g + 128 : stop - 256 * g + 128, :]
            parts.append(jnp.dot(rows[:, start:stop], part, preferred_element_type=F32))
        for t in range((last - first) // PR):
            for c in range(2):
                piece = [p[t * PR : (t + 1) * PR, c * 128 : (c + 1) * 128] for p in parts]
                at = ((first // PR + t) * 2 + c) * groups * PR
                laid[at : at + groups * PR, :] = jnp.concatenate(piece, axis=0).astype(BF16)
        where = pl.ds(first * 2 * groups, (last - first) * 2 * groups)
        stores.append(pltpu.make_async_copy(laid.at[where, :], out_ref.at[where, :], store_sem.at[b]))
        stores[-1].start()
    for copy in stores:
        copy.wait()


def tile_at(ref, block):
    return ref.at[pl.ds(pl.multiple_of(block * PR, PR), PR), :]


def expand(upper_ref, lower_ref, tiles_ref):
    lane_in = iota((VOX, PR * VOX), 0)
    lane_out = iota((VOX, PR * VOX), 1)
    same = (lane_in // PC == lane_out // VOX) & (lane_in % PC == lane_out % PC)
    spread = jnp.where(same, 1.0, 0.0).astype(BF16)
    for a in range(NA):
        for d, ref in ((0, upper_ref), (1, lower_ref)):
            rows = ref[a * KT : (a + 1) * KT, :]
            wide = jnp.dot(rows, spread, preferred_element_type=F32)
            base = (a * NH + d * KT) * PR
            for i in range(PR):
                tiles_ref[pl.ds(base + i, KT, stride=PR), :] = wide[:, i * VOX : (i + 1) * VOX]


def zero(ref, start, rows):
    step = 256

    def body(k, carry):
        ref[pl.ds(pl.multiple_of(start + k * step, step), step), :] = jnp.zeros((step, VOX), F32)
        return carry

    lax.fori_loop(0, rows // step, body, 0)


def rebuild(place_ref, tiles_ref, trace_ref, field_ref):
    zero(field_ref, 0, FIELD * PR)

    @pl.when(lax.axis_index("tile") == 0)
    def _():
        zero(field_ref, FIELD * PR, FIELD * PR)

    def body(n, carry):
        trace = jnp.broadcast_to(trace_ref[pl.ds(n, 1), :], (PR, VOX))
        base = place_ref[n]
        held = [tile_at(field_ref, base + a * XC)[...] for a in range(NA)]
        added = [tile_at(tiles_ref, a * NH + n)[...] * trace for a in range(NA)]
        for a in range(NA):
            tile_at(field_ref, base + a * XC)[...] = held[a] + added[a]
        return carry

    lax.fori_loop(0, NH, body, 0, unroll=8)


def project(place_ref, tiles_ref, field_ref, sums_ref):
    def body(n, carry):
        base = place_ref[n]
        total = tile_at(tiles_ref, n)[...] * tile_at(field_ref, base)[...]
        for a in range(1, NA):
            total = total + tile_at(tiles_ref, a * NH + n)[...] * tile_at(field_ref, base + a * XC)[...]
        tile_at(sums_ref, n)[...] = total
        return carry

    lax.fori_loop(0, NH, body, 0, unroll=8)
    rows = sums_ref[pl.ds(0, NH, stride=PR), :]
    for i in range(1, PR):
        rows = rows + sums_ref[pl.ds(i, NH, stride=PR), :]
    group = jnp.where(iota((VOX, VOX), 0) // PC == iota((VOX, VOX), 1) // PC, 1.0, 0.0)
    return jnp.dot(rows, group, preferred_element_type=F32, precision=lax.Precision.HIGHEST)


def denom_kernel(place_ref, upper_ref, packet_ref, trace_ref, tiles_ref, field, sums):
    expand(upper_ref, packet_ref, tiles_ref)
    rebuild(place_ref, tiles_ref, trace_ref, field)
    tiles_ref[TILES * PR : TILES * PR + NH, :] = project(place_ref, tiles_ref, field, sums)


def numer_kernel(place_ref, tiles_ref, image_ref, field_ref, sums_ref, permute_ref, sums):
    source = iota((VOX, NF * VOX), 0)
    target = iota((VOX, NF * VOX), 1)
    same = (source // PC == target // VOX) & (source % PC == target % PC)
    frame = (target % VOX) // PC
    for f in range(NF):
        permute_ref[f * VOX : (f + 1) * VOX, :] = jnp.where(same & (frame == f), 1.0, 0.0).astype(BF16)
    groups = XC // 8
    rows = groups * PR
    step = 16

    def body(k, carry):
        base = pl.multiple_of(k * (step * NF * rows), step * NF * rows)
        image = image_ref[pl.ds(base, step * NF * rows), :]
        lhs = []
        for z in range(step):
            start = z * NF * rows
            lhs.append(jnp.concatenate([image[start + f * rows : start + (f + 1) * rows, :] for f in range(NF)], axis=1))
        out = jnp.dot(jnp.concatenate(lhs, axis=0), permute_ref[...], preferred_element_type=F32)
        for z in range(step):
            for g in range(groups):
                for x in range(8):
                    at = z * rows + g * PR
                    tile_at(field_ref, (k * step + z) * XC + g * 8 + x)[...] = out[at : at + PR, x * VOX : (x + 1) * VOX]
        return carry

    lax.fori_loop(0, Z // step, body, 0)
    field_ref[FIELD * PR : (FIELD + PADF) * PR, :] = jnp.zeros((PADF * PR, VOX), F32)
    numer = project(place_ref, tiles_ref, field_ref, sums)
    denom = tiles_ref[TILES * PR : TILES * PR + NH, :]
    value = jnp.where(iota((NH, VOX), 1) % PC < PC // 2, numer, denom)
    sums_ref[...] = value


def fold(products_ref):
    lane_in = iota((2 * VOX, VOX), 0) % VOX
    lane_out = iota((2 * VOX, VOX), 1)
    total = None
    for i in range(PR):
        pick = jnp.where((lane_out // PC == i) & (lane_out % PC == lane_in % PC), 1.0, 0.0).astype(BF16)
        rows = products_ref[pl.ds(i, NA * KT, stride=PR), :]
        high = rows.astype(BF16)
        low = (rows - high.astype(F32)).astype(BF16)
        part = jnp.dot(jnp.concatenate([high, low], axis=1), pick, preferred_element_type=F32)
        total = part if total is None else total + part
    return total


def renew(start, place_ref, spot_ref, rows_ref, image_ref, field_ref, trace_ref, product_n, product_d):
    def body(k, carry):
        n = start + k
        trace = jnp.broadcast_to(trace_ref[pl.ds(n, 1), :], (PR, VOX))
        base = place_ref[n]
        spot = spot_ref[n]
        for a in range(NA):
            m = a * KT + k
            tile_at(product_n, m)[...] = tile_at(image_ref, spot + a * XC)[...] * trace
            tile_at(product_d, m)[...] = tile_at(field_ref, base + a * XC)[...] * trace
        return carry

    lax.fori_loop(0, KT, body, 0, unroll=8)
    ratio = fold(product_n) / (fold(product_d) + EPSILON)
    return (rows_ref[0 : NA * KT, :].astype(F32) * ratio).astype(BF16)


def lower_kernel(
    place_ref, spot_ref, packet_ref, tiles_ref, image_ref, old_ref, mine_ref, below_ref, above_ref,
    trace_ref, field_ref, out_ref, product_n, product_d,
):
    sums = mine_ref[...] + jnp.concatenate([below_ref[...], above_ref[...]], axis=0)
    first = iota((NH, VOX), 1) % PC < PC // 2
    numer = jnp.where(first, sums, pltpu.roll(sums, PC // 2, 1))
    denom = jnp.where(first, pltpu.roll(sums, VOX - PC // 2, 1), sums)
    trace_ref[...] = old_ref[...] * numer / (denom + EPSILON)
    rebuild(place_ref, tiles_ref, trace_ref, field_ref)
    out_ref[...] = renew(
        KT, place_ref, spot_ref, packet_ref, image_ref, field_ref, trace_ref, product_n, product_d
    )


def upper_kernel(
    place_ref, spot_ref, upper_ref, image_ref, field_ref, trace_ref, out_ref, sent_ref, product_n, product_d
):
    value = renew(0, place_ref, spot_ref, upper_ref, image_ref, field_ref, trace_ref, product_n, product_d)
    out_ref[...] = value
    sent_ref[...] = value


def merge_kernel(odd_ref, upper_ref, lower_ref, upper_other, lower_other, out_ref, wide):
    odd = odd_ref[...] > 0
    for a in range(NA):
        rows = slice(a * KT, (a + 1) * KT)
        for d, mine_ref, other_ref in ((0, upper_ref, upper_other), (1, lower_ref, lower_other)):
            mine = mine_ref[rows, :].astype(F32)
            other = other_ref[rows, :].astype(F32)
            wide[pl.ds(4 * a + 2 * d, KT, stride=16), :] = jnp.where(odd, other, mine)
            wide[pl.ds(4 * a + 2 * d + 1, KT, stride=16), :] = jnp.where(odd, mine, other)
    out_ref[...] = wide[...].astype(BF16)


def shards(movie, shifts, footprints, blocks, traces, counts):
    tiles = lax.axis_size("tile")
    tile = lax.axis_index("tile")
    core = lax.axis_index("nrn")
    down = [(i, (i + 1) % tiles) for i in range(tiles)]
    up = [(j, i) for i, j in down]
    cross = [(0, 1), (1, 0)]

    def shape(rows, dtype):
        return jax.ShapeDtypeStruct((rows, VOX), dtype)

    mine = traces[0]
    above = lax.ppermute(mine, "tile", down)
    theirs = lax.ppermute(mine, "nrn", cross)

    upper, packet, odd = call(
        rows_kernel,
        [shape(NA * KT, BF16), shape(NA * KT + KT, BF16), shape(KT, jnp.int32)],
        [smem(), vmem(), vmem()],
        scratch=[pltpu.VMEM((KT * 16, VOX), F32)], name="rows", limit=4,
    )(
        counts, pltpu.with_memory_space_constraint(blocks.T, pltpu.HBM),
        pltpu.with_memory_space_constraint(footprints.reshape(-1, VOX), pltpu.HBM),
    )
    packet_in = lax.ppermute(packet, "tile", down)

    height, width = movie.shape[2:]
    outside = pl.BlockSpec(memory_space=pltpu.HBM)
    sent = call(
        register_kernel, shape(tiles * 2 * XC, BF16), [smem(), outside],
        scratch=[
            pltpu.VMEM((height, width), BF16), pltpu.VMEM((tiles * 2 * XC, VOX), BF16),
            pltpu.SemaphoreType.DMA((5,)), pltpu.SemaphoreType.DMA((5,)),
        ],
        out_specs=outside, name="register", limit=12,
    )(shifts[0, 0], pltpu.with_memory_space_constraint(movie[0, 0], pltpu.HBM))
    sent, packet_in, above, theirs = lax.optimization_barrier((sent, packet_in, above, theirs))
    images = lax.all_to_all(
        sent.reshape(tiles * 2, XC, VOX), ("tile", "nrn"), split_axis=0, concat_axis=0, tiled=True
    ).reshape(-1, VOX)

    both = jnp.concatenate([mine, above], axis=0)
    other = jnp.concatenate([theirs, lax.ppermute(above, "nrn", cross)], axis=0)
    frames = jnp.stack([jnp.where(core == 0, both, other), jnp.where(core == 0, other, both)], axis=-1)
    old = jnp.broadcast_to(frames.reshape(NH, NF)[:, :, None], (NH, NF, PC)).reshape(NH, VOX)

    def base_of(info):
        return info[NA * KT :, 0].astype(jnp.int32) * XC + info[NA * KT :, 64].astype(jnp.int32)

    base, base_in = base_of(packet), base_of(packet_in)
    margin = tile == 0
    place = jnp.concatenate([base, base_in + jnp.where(margin, FIELD, 0)])
    spot = jnp.concatenate([base, jnp.where(margin, FIELD, base_in)])

    field = pltpu.VMEM((2 * FIELD * PR, VOX), F32)
    sums = pltpu.VMEM((NH * PR, VOX), F32)
    in_vmem = pltpu.with_memory_space_constraint
    tiles_e = call(
        denom_kernel, pltpu.VMEM((TILES * PR + NH, VOX), F32), [smem()] + [vmem()] * 3,
        scratch=[field, sums], name="denominator", limit=14,
    )(place, upper, packet_in, old)
    tiles_e = in_vmem(tiles_e, pltpu.VMEM)
    image_field, partial = call(
        numer_kernel, [pltpu.VMEM(((FIELD + PADF) * PR, VOX), F32), shape(NH, F32)],
        [smem()] + [vmem()] * 2,
        scratch=[pltpu.VMEM((NF * VOX, NF * VOX), BF16), sums], name="numerator", limit=12,
    )(spot, tiles_e, images)
    image_field = in_vmem(image_field, pltpu.VMEM)

    everyone = ("tile", "nrn")

    def other_core(pairs):
        return [(2 * i + c, 2 * j + 1 - c) for i, j in pairs for c in (0, 1)]

    partial = partial + lax.ppermute(partial, "nrn", cross)
    from_above = lax.ppermute(partial[:KT], "tile", down)
    from_below = lax.ppermute(partial[KT:], "tile", up)

    product = pltpu.VMEM((NA * KT * PR, VOX), F32)
    new, rebuilt, lower_new = call(
        lower_kernel,
        [shape(NH, F32), pltpu.VMEM((2 * FIELD * PR, VOX), F32), shape(NA * KT, BF16)],
        [smem()] * 2 + [vmem()] * 7,
        scratch=[product, product], name="lower", limit=8,
    )(place, spot, packet_in, tiles_e, image_field, old, partial, from_below, from_above)
    lower_back = lax.ppermute(lower_new, "tile", up)
    lower_other = lax.ppermute(lower_new, everyone, other_core(up))
    upper_new, upper_sent = call(
        upper_kernel, [shape(NA * KT, BF16)] * 2, [smem()] * 2 + [vmem()] * 4,
        scratch=[product, product], name="upper", limit=8,
    )(place, spot, upper, image_field, in_vmem(rebuilt, pltpu.VMEM), new)
    upper_other = lax.ppermute(upper_sent, "nrn", cross)
    merged = call(
        merge_kernel, shape(KT * 16, BF16), [vmem()] * 5,
        scratch=[pltpu.VMEM((KT * 16, VOX), F32)], name="merge", limit=4,
    )(odd, upper_new, lower_back, upper_other, lower_other)

    frames_new = new[:KT].reshape(KT, NF, PC)[:, :, 0].reshape(KT, NF // 2, 2)
    updated = jnp.where(core == 0, frames_new[:, :, 0], frames_new[:, :, 1])
    return updated[None], merged.reshape(KT, 16, VOX)


def solution(mesh):
    placed = (
        P("nrn", "tile", None, None),
        P("nrn", "tile", None),
        P("tile", None, None),
        P("tile", None),
        P("nrn", "tile", None),
        P("tile"),
    )
    return jax.shard_map(
        shards,
        mesh=mesh,
        in_specs=placed,
        out_specs=(P("nrn", "tile", None), P("tile", None, None)),
        check_vma=False,
    )
```

time: 140 us -> 114 us (0.81)
  Pallas kernels: 37.5 us -> 23.1 us
  other arithmetic: 5.85 us -> 1.12 us
  waiting for transfers between devices: 56.4 us -> 52.4 us
  local copies, waits for them, and re-layouts: 5.99 us -> 2.41 us
    ppermute x1, waiting for transfers between devices: 46.3 us -> 0.01 us  [shards(): packet_in = lax.ppermute(packet, 'tile', down)]
    all_to_all x1, waiting for transfers between devices: 0.01 us -> 44.3 us  [shards(): lax.all_to_all(sent.reshape(tiles * 2, XC, VOX), ('tile', 'nrn'), split_a...]
    pallas_call x5 -> x6, Pallas kernels: 35.3 us -> 22 us  [the longest x1 5.28 us: shards(): call(numer_kernel, [pltpu.VMEM(((FIELD + PADF) * PR, VOX), F32), shape(NH...]
    ppermute x9 -> x7, starting transfers between devices: 13.5 us -> 19.9 us  [the longest x1 8.26 us: shards(): lower_other = lax.ppermute(lower_new, everyone, other_core(up))]
    all_to_all x1, starting transfers between devices: 15.7 us -> 10.3 us  [shards(): lax.all_to_all(sent.reshape(tiles * 2, XC, VOX), ('tile', 'nrn'), split_a...]
    add x5 -> x2, other arithmetic: 3.81 us -> 0.19 us  [the longest x1 0.17 us: base_of(): info[NA * KT:, 0].astype(jnp.int32) * XC]
    ppermute x9 -> x7, waiting for transfers between devices: 9.24 us -> 7.7 us  [the longest x1 4.36 us: shards(): above = lax.ppermute(mine, 'tile', down)]
    unnamed x12 -> x10, local copies, waits for them, and re-layouts: 2.93 us -> 2.19 us
  transfers between devices with their start and end apart: 13 -> 11, of which waited for: 7 -> 7; matrix products, arithmetic and copies ran while one was open for 6% -> 1% of each run, Pallas kernels for 6% -> 9%
where the time goes in v1:
time: 114 us
  waiting for transfers between devices  52.4 us (46%)
  starting transfers between devices  33.4 us (29%)
  Pallas kernels  23.1 us (20%)
  local copies, waits for them, and re-layouts  2.41 us (2%)
  between operations  1.42 us (1%)
    all_to_all x1, waiting for transfers between devices, shards(): lax.all_to_all(sent.reshape(tiles * 2, XC, VOX), ('tile', 'nrn'), split_a...  44.3 us
    all_to_all x1, starting transfers between devices, shards(): lax.all_to_all(sent.reshape(tiles * 2, XC, VOX), ('tile', 'nrn'), split_a...  10.3 us
    ppermute x1, starting transfers between devices, shards(): lower_other = lax.ppermute(lower_new, everyone, other_core(up))  8.26 us
    ppermute x1, starting transfers between devices, shards(): from_below = lax.ppermute(partial[KT:], 'tile', up)  5.65 us
    pallas_call x1, Pallas kernels, shards(): call(numer_kernel, [pltpu.VMEM(((FIELD + PADF) * PR, VOX), F32), shape(NH...  5.28 us
    pallas_call x1, Pallas kernels, shards(): call(register_kernel, shape(tiles * 2 * XC, BF16), [smem(), outside], scr...  4.9 us
    pallas_call x1, Pallas kernels, shards(): call(lower_kernel, [shape(NH, F32), pltpu.VMEM((2 * FIELD * PR, VOX), F32...  4.54 us
    ppermute x1, waiting for transfers between devices, shards(): above = lax.ppermute(mine, 'tile', down)  4.36 us
  transfers between devices with their start and end apart: 11, of which 7 were waited for; matrix products, arithmetic and copies ran while one was open for 1% of the time, Pallas kernels for 9%

profile of v1, /device:TPU:1, one launch (start us, length us, event | category | flops | bytes accessed | tf_op | source)
XLA Modules:
  0.0 113.9 jit_solution(12933804033171740101)
XLA Ops:
  1.3 1.4 %rows.1 = (bf16[384,128]{1,0:T(8,128)(2,1)S(1)}, bf16[480,128]{1,0:T(8,128)(2,1)S(1)}, s32[96,128]{1,0:T(8,128)S(1)}) custom-call(s32[1]{0:T(128)S(6)} %copy.12.count_ref, s32[16,96]{1,0:T(8,128)} %bitcast.25, bf16[1536,128]{1,0:T(8,128)(2,1)} %bitcast.21), custom_call_target="tpu_custom_call" | custom-call | tf_op jit(solution)/shard_map/rows/pallas_call | solution.py:309
  2.7 0.0 copy-start
  2.7 0.6 copy-done
  3.4 2.0 %collective-permute-start = (bf16[480,128]{1,0:T(8,128)(2,1)S(1)}, bf16[480,128]{1,0:T(8,128)(2,1)S(1)}, u32[]{:S(2)}, u32[]{:S(2)}) collective-permute-start(bf16[480,128]{1,0:T(8,128)(2,1)S(1)} %get-tuple-element.16), channel_id=1, source_target_pairs={{0,2},{2,4},{4,6},{6,8},{8,10},{10,12},{12,14},{14,16},{16,18},{18... | collective-permute-start | bytes 368648 | tf_op jit(solution)/shard_map/ppermute | solution.py:318
  5.4 1.2 %collective-permute-start.2 = (f32[96,4]{0,1:T(4,128)}, f32[96,4]{0,1:T(4,128)S(1)}, u32[]{:S(2)}, u32[]{:S(2)}) collective-permute-start(f32[96,4]{0,1:T(4,128)} %bitcast.26), channel_id=1, source_target_pairs={{0,1},{1,0},{2,3},{3,2},{4,5},{5,4},{6,7},{7,6},{8,9},{9,8},{10,11... | collective-permute-start | bytes 4616 | tf_op jit(solution)/shard_map/ppermute | solution.py:307
  6.6 1.0 collective-permute-start.1
  7.6 0.0 copy-start.3
  7.6 0.7 copy-done.3
  8.2 0.0 copy-start.4
  8.2 4.9 %register.1 = bf16[8192,128]{1,0:T(8,128)(2,1)} custom-call(s32[2]{0:T(128)S(1)} %bitcast.18, bf16[1024,1024]{1,0:T(8,128)(2,1)} %bitcast.19), custom_call_target="tpu_custom_call" | custom-call | tf_op jit(solution)/shard_map/register/pallas_call | solution.py:322
  13.1 0.0 collective-permute-done.2
  13.1 4.4 %collective-permute-done.1 = f32[96,4]{0,1:T(4,128)S(1)} collective-permute-done((f32[96,4]{0,1:T(4,128)}, f32[96,4]{0,1:T(4,128)S(1)}, u32[]{:S(2)}, u32[]{:S(2)}) %collective-permute-start.1) | collective-permute-done | bytes 1568 | tf_op jit(solution)/shard_map/ppermute | solution.py:306
  17.5 0.0 collective-permute-done.packet_ref
  17.5 10.3 %all-to-all-start = ((bf16[256,32,128]{2,1,0:T(8,128)(2,1)}), bf16[256,32,128]{2,1,0:T(8,128)(2,1)}, u32[]{:S(2)}, u32[]{:S(2)}) async-start(bf16[256,32,128]{2,1,0:T(8,128)(2,1)} %bitcast.10), calls=%async_computation | async-start | bytes 4194304 | tf_op jit(solution)/shard_map/all_to_all | solution.py:331
  27.8 0.2 add_reduce_fusion.1
  28.0 2.3 %collective-permute-start.3 = (f32[96,4]{0,1:T(4,128)S(1)}, f32[96,4]{0,1:T(4,128)S(1)}, u32[]{:S(2)}, u32[]{:S(2)}) collective-permute-start(f32[96,4]{0,1:T(4,128)S(1)} %collective-permute-done.1), channel_id=1, source_target_pairs={{0,1},{1,0},{2,3},{3,2},{4,5},{5,4},{6,7},{7,6},{8,9},{9,8},{10,11... | collective-permute-start | bytes 4616 | tf_op jit(solution)/shard_map/ppermute | solution.py:336
  30.3 0.2 select_reduce_fusion
  30.5 0.1 pad_add_fusion
  30.5 0.6 collective-permute-done.3
  31.1 0.0 copy-done.4
  31.1 0.1 fusion.1
  31.2 0.1 copy.9.trace_ref.old_ref
  31.3 0.0 copy-start.1
  31.3 0.9 copy-done.1
  32.2 3.8 %denominator.1.tiles_ref = f32[6336,128]{1,0:T(8,128)S(1)} custom-call(s32[192]{0:T(256)S(1)} %get-tuple-element.37.place_ref, bf16[384,128]{1,0:T(8,128)(2,1)S(1)} %copy-done.1, bf16[480,128]{1,0:T(8,128)(2,1)S(1)} %collective-permute-done.packet_ref, f32[192,128]{1,0:T(8,128)S(1)} %copy.9.trace_ref.old_ref), custom_call_target="tpu_custom_call" | custom-call | tf_op jit(solution)/shard_map/denominator/pallas_call | solution.py:351
  36.0 44.3 %all-to-all-done = bf16[256,32,128]{2,1,0:T(8,128)(2,1)} async-done(((bf16[256,32,128]{2,1,0:T(8,128)(2,1)}), bf16[256,32,128]{2,1,0:T(8,128)(2,1)}, u32[]{:S(2)}, u32[]{:S(2)}) %all-to-all-start) | async-done | bytes 2097184 | tf_op jit(solution)/shard_map/all_to_all | solution.py:331
  80.3 5.3 %numerator.1 = (f32[9216,128]{1,0:T(8,128)S(1)}, f32[192,128]{1,0:T(8,128)S(1)}) custom-call(s32[192]{0:T(256)S(1)} %get-tuple-element.36.place_ref.spot_ref, f32[6336,128]{1,0:T(8,128)S(1)} %denominator.1.tiles_ref, bf16[8192,128]{1,0:T(8,128)(2,1)} %bitcast.11.image_ref), custom_call_target="tpu_custom_call" | custom-call | tf_op jit(solution)/shard_map/numerator/pallas_call | solution.py:356
  85.6 0.9 collective-permute-start.4
  86.5 0.9 collective-permute-done.4
  87.5 1.3 %collective-permute-start.6 = (f32[96,128]{1,0:T(8,128)S(1)}, f32[96,128]{1,0:T(8,128)S(1)}, u32[]{:S(2)}, u32[]{:S(2)}) collective-permute-start(f32[96,128]{1,0:T(8,128)S(1)} %get-tuple-element.32), channel_id=1, source_target_pairs={{0,2},{2,4},{4,6},{6,8},{8,10},{10,12},{12,14},{14,16},{16,18},{18... | collective-permute-start | bytes 147464 | tf_op jit(solution)/shard_map/ppermute | solution.py:369
  88.8 5.6 %collective-permute-start.5 = (f32[96,128]{1,0:T(8,128)S(1)}, f32[96,128]{1,0:T(8,128)S(1)}, u32[]{:S(2)}, u32[]{:S(2)}) collective-permute-start(f32[96,128]{1,0:T(8,128)S(1)} %get-tuple-element.33), channel_id=1, source_target_pairs={{2,0},{4,2},{6,4},{8,6},{10,8},{12,10},{14,12},{16,14},{18,16},{20... | collective-permute-start | bytes 147464 | tf_op jit(solution)/shard_map/ppermute | solution.py:370
  94.5 1.5 %collective-permute-done.6.above_ref = f32[96,128]{1,0:T(8,128)S(1)} collective-permute-done((f32[96,128]{1,0:T(8,128)S(1)}, f32[96,128]{1,0:T(8,128)S(1)}, u32[]{:S(2)}, u32[]{:S(2)}) %collective-permute-start.6) | collective-permute-done | bytes 49184 | tf_op jit(solution)/shard_map/ppermute | solution.py:369
  95.9 0.0 collective-permute-done.5.below_ref
  95.9 0.0 copy-start.2
  95.9 4.5 %lower.1 = (f32[192,128]{1,0:T(8,128)S(1)}, f32[16384,128]{1,0:T(8,128)S(1)}, bf16[384,128]{1,0:T(8,128)(2,1)}) custom-call(s32[192]{0:T(256)S(1)} %get-tuple-element.37.place_ref, s32[192]{0:T(256)S(1)} %get-tuple-element.36.place_ref.spot_ref, bf16[480,128]{1,0:T(8,128)(2,1)S(1)} %collective-permute-done.packet_ref, f32[6336,128]{1,0:T(8,128)S(1)} %denominator.1.tiles_ref, ...), custom_call_target="tpu_custom_call" | custom-call | tf_op jit(solution)/shard_map/lower/pallas_call | solution.py:373
  100.5 8.3 %collective-permute-start.9 = (bf16[384,128]{1,0:T(8,128)(2,1)}, bf16[384,128]{1,0:T(8,128)(2,1)S(1)}, u32[]{:S(2)}, u32[]{:S(2)}) collective-permute-start(bf16[384,128]{1,0:T(8,128)(2,1)} %get-tuple-element.28), channel_id=1, source_target_pairs={{2,1},{3,0},{4,3},{5,2},{6,5},{7,4},{8,7},{9,6},{10,9},{11,8},{12,... | collective-permute-start | bytes 294920 | tf_op jit(solution)/shard_map/ppermute | solution.py:380
  108.7 0.0 collective-permute-start.7
  108.7 0.0 copy-done.2
  108.7 2.1 %upper.1 = (bf16[384,128]{1,0:T(8,128)(2,1)S(1)}, bf16[384,128]{1,0:T(8,128)(2,1)S(1)}) custom-call(s32[192]{0:T(256)S(1)} %get-tuple-element.37.place_ref, s32[192]{0:T(256)S(1)} %get-tuple-element.36.place_ref.spot_ref, bf16[384,128]{1,0:T(8,128)(2,1)S(1)} %copy-done.2, f32[9216,128]{1,0:T(8,128)S(1)} %get-tuple-element.22.image_ref, ...), custom_call_target="tpu_custom_call" | custom-call | tf_op jit(solution)/shard_map/upper/pallas_call | solution.py:381
  110.8 0.1 copy.11
  110.9 0.5 collective-permute-start.8
  111.4 0.6 broadcast_select_fusion
  112.0 0.4 collective-permute-done.8.upper_other
  112.4 0.0 collective-permute-done.9.lower_other
  112.4 0.3 collective-permute-done.7.lower_ref
  112.7 1.2 %merge.1 = bf16[1536,128]{1,0:T(8,128)(2,1)} custom-call(s32[96,128]{1,0:T(8,128)S(1)} %get-tuple-element.25.odd_ref, bf16[384,128]{1,0:T(8,128)(2,1)S(1)} %get-tuple-element.27.upper_ref, bf16[384,128]{1,0:T(8,128)(2,1)S(1)} %collective-permute-done.7.lower_ref, bf16[384,128]{1,0:T(8,128)(2,1)S(1)} %collective-permute-done.8.upper_other, ...), custom_call_target="tpu_custom_call" | custom-call | tf_op jit(solution)/shard_map/merge/pallas_call | solution.py:386
  (8 shorter events, 0.1 us)
Async XLA Ops:
  2.7 0.6 copy-start
  3.4 14.1 %collective-permute-start = (bf16[480,128]{1,0:T(8,128)(2,1)S(1)}, bf16[480,128]{1,0:T(8,128)(2,1)S(1)}, u32[]{:S(2)}, u32[]{:S(2)}) collective-permute-start(bf16[480,128]{1,0:T(8,128)(2,1)S(1)} %get-tuple-element.16), channel_id=1, source_target_pairs={{0,2},{2,4},{4,6},{6,8},{8,10},{10,12},{12,14},{14,16},{16,18},{18... | collective-permute-start | bytes 368648 | tf_op jit(solution)/shard_map/ppermute | solution.py:318
  5.4 7.7 %collective-permute-start.2 = (f32[96,4]{0,1:T(4,128)}, f32[96,4]{0,1:T(4,128)S(1)}, u32[]{:S(2)}, u32[]{:S(2)}) collective-permute-start(f32[96,4]{0,1:T(4,128)} %bitcast.26), channel_id=1, source_target_pairs={{0,1},{1,0},{2,3},{3,2},{4,5},{5,4},{6,7},{7,6},{8,9},{9,8},{10,11... | collective-permute-start | bytes 4616 | tf_op jit(solution)/shard_map/ppermute | solution.py:307
  6.6 10.9 %collective-permute-start.1 = (f32[96,4]{0,1:T(4,128)}, f32[96,4]{0,1:T(4,128)S(1)}, u32[]{:S(2)}, u32[]{:S(2)}) collective-permute-start(f32[96,4]{0,1:T(4,128)} %bitcast.27), channel_id=1, source_target_pairs={{0,2},{2,4},{4,6},{6,8},{8,10},{10,12},{12,14},{14,16},{16,18},{18... | collective-permute-start | bytes 4616 | tf_op jit(solution)/shard_map/ppermute | solution.py:306
  7.6 0.7 copy-start.3
  8.2 22.9 %copy-start.4 = (f32[1,96,4]{1,2,0:T(4,128)S(1)}, f32[1,96,4]{1,2,0:T(4,128)}, u32[]{:S(2)}) copy-start(f32[1,96,4]{1,2,0:T(4,128)} %param.10) | copy-start | bytes 4612
  17.5 62.8 %all-to-all-start = ((bf16[256,32,128]{2,1,0:T(8,128)(2,1)}), bf16[256,32,128]{2,1,0:T(8,128)(2,1)}, u32[]{:S(2)}, u32[]{:S(2)}) async-start(bf16[256,32,128]{2,1,0:T(8,128)(2,1)} %bitcast.10), calls=%async_computation | async-start | bytes 4194304 | tf_op jit(solution)/shard_map/all_to_all | solution.py:331
  28.0 3.1 %collective-permute-start.3 = (f32[96,4]{0,1:T(4,128)S(1)}, f32[96,4]{0,1:T(4,128)S(1)}, u32[]{:S(2)}, u32[]{:S(2)}) collective-permute-start(f32[96,4]{0,1:T(4,128)S(1)} %collective-permute-done.1), channel_id=1, source_target_pairs={{0,1},{1,0},{2,3},{3,2},{4,5},{5,4},{6,7},{7,6},{8,9},{9,8},{10,11... | collective-permute-start | bytes 4616 | tf_op jit(solution)/shard_map/ppermute | solution.py:336
  31.3 0.9 copy-start.1
  85.6 1.9 %collective-permute-start.4 = (f32[192,128]{1,0:T(8,128)S(1)}, f32[192,128]{1,0:T(8,128)S(1)}, u32[]{:S(2)}, u32[]{:S(2)}) collective-permute-start(f32[192,128]{1,0:T(8,128)S(1)} %get-tuple-element.23), channel_id=1, source_target_pairs={{0,1},{1,0},{2,3},{3,2},{4,5},{5,4},{6,7},{7,6},{8,9},{9,8},{10,11... | collective-permute-start | bytes 294920 | tf_op jit(solution)/shard_map/ppermute | solution.py:368
  87.5 8.4 %collective-permute-start.6 = (f32[96,128]{1,0:T(8,128)S(1)}, f32[96,128]{1,0:T(8,128)S(1)}, u32[]{:S(2)}, u32[]{:S(2)}) collective-permute-start(f32[96,128]{1,0:T(8,128)S(1)} %get-tuple-element.32), channel_id=1, source_target_pairs={{0,2},{2,4},{4,6},{6,8},{8,10},{10,12},{12,14},{14,16},{16,18},{18... | collective-permute-start | bytes 147464 | tf_op jit(solution)/shard_map/ppermute | solution.py:369
  88.8 7.1 %collective-permute-start.5 = (f32[96,128]{1,0:T(8,128)S(1)}, f32[96,128]{1,0:T(8,128)S(1)}, u32[]{:S(2)}, u32[]{:S(2)}) collective-permute-start(f32[96,128]{1,0:T(8,128)S(1)} %get-tuple-element.33), channel_id=1, source_target_pairs={{2,0},{4,2},{6,4},{8,6},{10,8},{12,10},{14,12},{16,14},{18,16},{20... | collective-permute-start | bytes 147464 | tf_op jit(solution)/shard_map/ppermute | solution.py:370
  95.9 12.8 %copy-start.2 = (bf16[384,128]{1,0:T(8,128)(2,1)S(1)}, bf16[384,128]{1,0:T(8,128)(2,1)}, u32[]{:S(2)}) copy-start(bf16[384,128]{1,0:T(8,128)(2,1)} %copy-done) | copy-start | bytes 294916
  100.5 11.9 %collective-permute-start.9 = (bf16[384,128]{1,0:T(8,128)(2,1)}, bf16[384,128]{1,0:T(8,128)(2,1)S(1)}, u32[]{:S(2)}, u32[]{:S(2)}) collective-permute-start(bf16[384,128]{1,0:T(8,128)(2,1)} %get-tuple-element.28), channel_id=1, source_target_pairs={{2,1},{3,0},{4,3},{5,2},{6,5},{7,4},{8,7},{9,6},{10,9},{11,8},{12,... | collective-permute-start | bytes 294920 | tf_op jit(solution)/shard_map/ppermute | solution.py:380
  108.7 4.0 %collective-permute-start.7 = (bf16[384,128]{1,0:T(8,128)(2,1)}, bf16[384,128]{1,0:T(8,128)(2,1)S(1)}, u32[]{:S(2)}, u32[]{:S(2)}) collective-permute-start(bf16[384,128]{1,0:T(8,128)(2,1)} %get-tuple-element.28), channel_id=1, source_target_pairs={{2,0},{4,2},{6,4},{8,6},{10,8},{12,10},{14,12},{16,14},{18,16},{20... | collective-permute-start | bytes 294920 | tf_op jit(solution)/shard_map/ppermute | solution.py:379
  110.9 1.5 %collective-permute-start.8 = (bf16[384,128]{1,0:T(8,128)(2,1)S(1)}, bf16[384,128]{1,0:T(8,128)(2,1)S(1)}, u32[]{:S(2)}, u32[]{:S(2)}) collective-permute-start(bf16[384,128]{1,0:T(8,128)(2,1)S(1)} %get-tuple-element.29), channel_id=1, source_target_pairs={{0,1},{1,0},{2,3},{3,2},{4,5},{5,4},{6,7},{7,6},{8,9},{9,8},{10,11... | collective-permute-start | bytes 294920 | tf_op jit(solution)/shard_map/ppermute | solution.py:385

commit v2 on v1

--- a/solution.py
+++ b/solution.py
@@ -51,8 +51,7 @@
     )
 
 
-def rows_kernel(count_ref, block_ref, foot_ref, upper_ref, packet_ref, odd_ref, wide):
-    core = lax.axis_index("nrn")
+def places(block_ref):
     first = block_ref[...]
     ones = jnp.where(iota((16, VOX), 0) == 0, 1.0, 0.0).astype(BF16)
 
@@ -63,19 +62,27 @@
 
     plane = down_rows(first // 128)
     column = down_rows(first % 64).astype(jnp.int32)
-    odd = (column + core) % 2
-    place = (column + odd) // 2
+    odd = (column + lax.axis_index("nrn")) % 2
+    return plane, (column + odd) // 2, odd
+
+
+def pick_rows(d, count_ref, odd, foot_ref, out_ref, wide):
+    wide[...] = foot_ref[...].astype(F32)
     live = iota((KT, VOX), 0) < count_ref[0]
-    odd_ref[...] = odd
+    for a in range(NA):
+        left = wide[pl.ds(4 * a + 2 * d, KT, stride=16), :]
+        right = wide[pl.ds(4 * a + 2 * d + 1, KT, stride=16), :]
+        value = jnp.where(live, jnp.where(odd > 0, right, left), 0.0)
+        out_ref[a * KT : (a + 1) * KT, :] = value.astype(BF16)
+
+
+def rows_kernel(count_ref, block_ref, foot_ref, packet_ref, upper_ref, odd_ref, wide):
+    plane, place, odd = places(block_ref)
     info = jnp.where(iota((KT, VOX), 1) < 64, plane, place.astype(F32))
     packet_ref[NA * KT : NA * KT + KT, :] = info.astype(BF16)
-    wide[...] = foot_ref[...].astype(F32)
-    for a in range(NA):
-        for d, ref in ((0, upper_ref), (1, packet_ref)):
-            left = wide[pl.ds(4 * a + 2 * d, KT, stride=16), :]
-            right = wide[pl.ds(4 * a + 2 * d + 1, KT, stride=16), :]
-            value = jnp.where(live, jnp.where(odd > 0, right, left), 0.0)
-            ref[a * KT : (a + 1) * KT, :] = value.astype(BF16)
+    pick_rows(1, count_ref, odd, foot_ref, packet_ref, wide)
+    odd_ref[...] = odd
+    pick_rows(0, count_ref, odd, foot_ref, upper_ref, wide)
 
 
 def register_kernel(shift_ref, movie_ref, out_ref, image, laid, load_sem, store_sem):
@@ -185,19 +192,29 @@
     return jnp.dot(rows, group, preferred_element_type=F32, precision=lax.Precision.HIGHEST)
 
 
-def denom_kernel(place_ref, upper_ref, packet_ref, trace_ref, tiles_ref, field, sums):
+def denom_kernel(
+    place_ref, upper_ref, packet_ref, trace_ref, tiles_ref, field, sums
+):
     expand(upper_ref, packet_ref, tiles_ref)
     rebuild(place_ref, tiles_ref, trace_ref, field)
     tiles_ref[TILES * PR : TILES * PR + NH, :] = project(place_ref, tiles_ref, field, sums)
+
+
+def even_tile():
+    return lax.bitwise_and(lax.axis_index("tile"), 1) == 0
 
 
 def numer_kernel(place_ref, tiles_ref, image_ref, field_ref, sums_ref, permute_ref, sums):
     source = iota((VOX, NF * VOX), 0)
     target = iota((VOX, NF * VOX), 1)
     same = (source // PC == target // VOX) & (source % PC == target % PC)
-    frame = (target % VOX) // PC
+    same = jnp.where(same, 1.0, 0.0).astype(BF16)
+    frame = iota((16, NF * VOX), 1) % VOX // PC
     for f in range(NF):
-        permute_ref[f * VOX : (f + 1) * VOX, :] = jnp.where(same & (frame == f), 1.0, 0.0).astype(BF16)
+        mine = jnp.where(frame == f, 1.0, 0.0).astype(BF16)
+        for r in range(VOX // 16):
+            at = f * VOX + 16 * r
+            permute_ref[at : at + 16, :] = same[16 * r : 16 * r + 16, :] * mine
     groups = XC // 8
     rows = groups * PR
     step = 16
@@ -222,7 +239,10 @@
     numer = project(place_ref, tiles_ref, field_ref, sums)
     denom = tiles_ref[TILES * PR : TILES * PR + NH, :]
     value = jnp.where(iota((NH, VOX), 1) % PC < PC // 2, numer, denom)
-    sums_ref[...] = value
+    upper, lower = value[:KT, :], value[KT:, :]
+    even = even_tile()
+    sums_ref[:KT, :] = jnp.where(even, lower, upper)
+    sums_ref[KT:, :] = jnp.where(even, upper, lower)
 
 
 def fold(products_ref):
@@ -257,10 +277,15 @@
 
 
 def lower_kernel(
-    place_ref, spot_ref, packet_ref, tiles_ref, image_ref, old_ref, mine_ref, below_ref, above_ref,
+    place_ref, spot_ref, packet_ref, tiles_ref, image_ref, old_ref, mine_ref, near_ref, far_ref,
     trace_ref, field_ref, out_ref, product_n, product_d,
 ):
-    sums = mine_ref[...] + jnp.concatenate([below_ref[...], above_ref[...]], axis=0)
+    even = even_tile()
+    first_mine, second_mine = mine_ref[:KT, :], mine_ref[KT:, :]
+    near, far = near_ref[...], far_ref[...]
+    upper = jnp.where(even, second_mine + near, first_mine + far)
+    lower = jnp.where(even, first_mine + far, second_mine + near)
+    sums = jnp.concatenate([upper, lower], axis=0)
     first = iota((NH, VOX), 1) % PC < PC // 2
     numer = jnp.where(first, sums, pltpu.roll(sums, PC // 2, 1))
     denom = jnp.where(first, pltpu.roll(sums, VOX - PC // 2, 1), sums)
@@ -306,15 +331,13 @@
     above = lax.ppermute(mine, "tile", down)
     theirs = lax.ppermute(mine, "nrn", cross)
 
-    upper, packet, odd = call(
-        rows_kernel,
-        [shape(NA * KT, BF16), shape(NA * KT + KT, BF16), shape(KT, jnp.int32)],
-        [smem(), vmem(), vmem()],
-        scratch=[pltpu.VMEM((KT * 16, VOX), F32)], name="rows", limit=4,
-    )(
-        counts, pltpu.with_memory_space_constraint(blocks.T, pltpu.HBM),
-        pltpu.with_memory_space_constraint(footprints.reshape(-1, VOX), pltpu.HBM),
-    )
+    hbm = pltpu.with_memory_space_constraint
+    block_rows = hbm(blocks.T, pltpu.HBM)
+    foot_rows = hbm(footprints.reshape(-1, VOX), pltpu.HBM)
+    wide = pltpu.VMEM((KT * 16, VOX), F32)
+    packet, upper, odd = call(
+        rows_kernel, [shape(NA * KT + KT, BF16), pltpu.HBM((NA * KT, VOX), BF16), shape(KT, jnp.int32)], [smem(), vmem(), vmem()], scratch=[wide], name="rows", limit=4,
+    )(counts, block_rows, foot_rows)
     packet_in = lax.ppermute(packet, "tile", down)
 
     height, width = movie.shape[2:]
@@ -326,7 +349,7 @@
             pltpu.SemaphoreType.DMA((5,)), pltpu.SemaphoreType.DMA((5,)),
         ],
         out_specs=outside, name="register", limit=12,
-    )(shifts[0, 0], pltpu.with_memory_space_constraint(movie[0, 0], pltpu.HBM))
+    )(hbm(shifts[0, 0], pltpu.HBM), hbm(movie[0, 0], pltpu.HBM))
     sent, packet_in, above, theirs = lax.optimization_barrier((sent, packet_in, above, theirs))
     images = lax.all_to_all(
         sent.reshape(tiles * 2, XC, VOX), ("tile", "nrn"), split_axis=0, concat_axis=0, tiled=True
@@ -366,8 +389,10 @@
         return [(2 * i + c, 2 * j + 1 - c) for i, j in pairs for c in (0, 1)]
 
     partial = partial + lax.ppermute(partial, "nrn", cross)
-    from_above = lax.ppermute(partial[:KT], "tile", down)
-    from_below = lax.ppermute(partial[KT:], "tile", up)
+    near = [(i, i ^ 1) for i in range(tiles)]
+    far = [(i, (i - 1 + 2 * (i % 2)) % tiles) for i in range(tiles)]
+    from_far = lax.ppermute(partial[:KT], "tile", far)
+    from_near = lax.ppermute(partial[KT:], "tile", near)
 
     product = pltpu.VMEM((NA * KT * PR, VOX), F32)
     new, rebuilt, lower_new = call(
@@ -375,7 +400,7 @@
         [shape(NH, F32), pltpu.VMEM((2 * FIELD * PR, VOX), F32), shape(NA * KT, BF16)],
         [smem()] * 2 + [vmem()] * 7,
         scratch=[product, product], name="lower", limit=8,
-    )(place, spot, packet_in, tiles_e, image_field, old, partial, from_below, from_above)
+    )(place, spot, packet_in, tiles_e, image_field, old, partial, from_near, from_far)
     lower_back = lax.ppermute(lower_new, "tile", up)
     lower_other = lax.ppermute(lower_new, everyone, other_core(up))
     upper_new, upper_sent = call(

time: 114 us -> 109 us (0.956)
  starting transfers between devices: 33.4 us -> 22.9 us
  waiting for transfers between devices: 52.4 us -> 58.1 us
  local copies, waits for them, and re-layouts: 2.41 us -> 1.12 us
    ppermute x1, starting transfers between devices: 8.26 us -> 2.83 us  [shards(): lower_other = lax.ppermute(lower_new, everyone, other_core(up))]
    ppermute x2, waiting for transfers between devices: 1.48 us -> 6.24 us  [the longest x1 6.24 us: shards(): from_far = lax.ppermute(partial[:KT], 'tile', far)]
    ppermute x2, starting transfers between devices: 6.97 us -> 2.22 us  [the longest x1 1.48 us: shards(): from_far = lax.ppermute(partial[:KT], 'tile', far)]
    unnamed x10 -> x6, local copies, waits for them, and re-layouts: 2.19 us -> 0.9 us
  transfers between devices with their start and end apart: 11 -> 11, of which waited for: 7 -> 7; matrix products, arithmetic and copies ran while one was open for 1% -> 1% of each run, Pallas kernels for 9% -> 10%
where the time goes in v2:
time: 109 us; the launch traced here: 108 us
  waiting for transfers between devices  58.1 us (53%)
  Pallas kernels  23.8 us (22%)
  starting transfers between devices  22.9 us (21%)
  between operations  1.4 us (1%)
  local copies, waits for them, and re-layouts  1.12 us (1%)
  other arithmetic  1.12 us (1%)
    all_to_all x1, waiting for transfers between devices, shards(): lax.all_to_all(sent.reshape(tiles * 2, XC, VOX), ('tile', 'nrn'), split_a...  44.3 us
    all_to_all x1, starting transfers between devices, shards(): lax.all_to_all(sent.reshape(tiles * 2, XC, VOX), ('tile', 'nrn'), split_a...  9.87 us
    ppermute x1, waiting for transfers between devices, shards(): from_far = lax.ppermute(partial[:KT], 'tile', far)  6.24 us
    pallas_call x1, Pallas kernels, shards(): call(numer_kernel, [pltpu.VMEM(((FIELD + PADF) * PR, VOX), F32), shape(NH...  5.26 us
    pallas_call x1, Pallas kernels, shards(): call(register_kernel, shape(tiles * 2 * XC, BF16), [smem(), outside], scr...  5.15 us
    ppermute x1, waiting for transfers between devices, shards(): above = lax.ppermute(mine, 'tile', down)  4.76 us
    pallas_call x1, Pallas kernels, shards(): call(lower_kernel, [shape(NH, F32), pltpu.VMEM((2 * FIELD * PR, VOX), F32...  4.35 us
    pallas_call x1, Pallas kernels, shards(): call(denom_kernel, pltpu.VMEM((TILES * PR + NH, VOX), F32), [smem()] + [v...  3.76 us
  transfers between devices with their start and end apart: 11, of which 7 were waited for; matrix products, arithmetic and copies ran while one was open for 1% of the time, Pallas kernels for 10%

profile of v2, /device:TPU:1, one launch (start us, length us, event | category | flops | bytes accessed | tf_op | source)
XLA Modules:
  0.0 108.5 jit_solution(13002352830667576556)
XLA Ops:
  1.3 2.1 %rows.1 = (bf16[480,128]{1,0:T(8,128)(2,1)S(1)}, bf16[384,128]{1,0:T(8,128)(2,1)}, s32[96,128]{1,0:T(8,128)S(1)}) custom-call(s32[1]{0:T(128)S(6)} %copy.12.count_ref, s32[16,96]{1,0:T(8,128)} %bitcast.24, bf16[1536,128]{1,0:T(8,128)(2,1)} %bitcast.20), custom_call_target="tpu_custom_call" | custom-call | tf_op jit(solution)/shard_map/rows/pallas_call | solution.py:338
  3.4 2.0 %collective-permute-start = (bf16[480,128]{1,0:T(8,128)(2,1)S(1)}, bf16[480,128]{1,0:T(8,128)(2,1)S(1)}, u32[]{:S(2)}, u32[]{:S(2)}) collective-permute-start(bf16[480,128]{1,0:T(8,128)(2,1)S(1)} %get-tuple-element.16), channel_id=1, source_target_pairs={{0,2},{2,4},{4,6},{6,8},{8,10},{10,12},{12,14},{14,16},{16,18},{18... | collective-permute-start | bytes 368648 | tf_op jit(solution)/shard_map/ppermute | solution.py:341
  5.4 1.2 %collective-permute-start.2 = (f32[96,4]{0,1:T(4,128)}, f32[96,4]{0,1:T(4,128)S(1)}, u32[]{:S(2)}, u32[]{:S(2)}) collective-permute-start(f32[96,4]{0,1:T(4,128)} %bitcast.25), channel_id=1, source_target_pairs={{0,1},{1,0},{2,3},{3,2},{4,5},{5,4},{6,7},{7,6},{8,9},{9,8},{10,11... | collective-permute-start | bytes 4616 | tf_op jit(solution)/shard_map/ppermute | solution.py:332
  6.6 1.0 collective-permute-start.1
  7.6 0.0 copy-start.2
  7.6 5.2 %register.1 = bf16[8192,128]{1,0:T(8,128)(2,1)} custom-call(s32[2]{0:T(128)} %bitcast.32, bf16[1024,1024]{1,0:T(8,128)(2,1)} %bitcast.18), custom_call_target="tpu_custom_call" | custom-call | tf_op jit(solution)/shard_map/register/pallas_call | solution.py:345
  12.7 0.0 collective-permute-done.2
  12.7 4.8 %collective-permute-done.1 = f32[96,4]{0,1:T(4,128)S(1)} collective-permute-done((f32[96,4]{0,1:T(4,128)}, f32[96,4]{0,1:T(4,128)S(1)}, u32[]{:S(2)}, u32[]{:S(2)}) %collective-permute-start.1) | collective-permute-done | bytes 1568 | tf_op jit(solution)/shard_map/ppermute | solution.py:331
  17.5 0.0 collective-permute-done.packet_ref
  17.5 9.9 %all-to-all-start = ((bf16[256,32,128]{2,1,0:T(8,128)(2,1)}), bf16[256,32,128]{2,1,0:T(8,128)(2,1)}, u32[]{:S(2)}, u32[]{:S(2)}) async-start(bf16[256,32,128]{2,1,0:T(8,128)(2,1)} %bitcast.10), calls=%async_computation | async-start | bytes 4194304 | tf_op jit(solution)/shard_map/all_to_all | solution.py:354
  27.4 0.2 add_reduce_fusion.1
  27.6 2.3 %collective-permute-start.3 = (f32[96,4]{0,1:T(4,128)S(1)}, f32[96,4]{0,1:T(4,128)S(1)}, u32[]{:S(2)}, u32[]{:S(2)}) collective-permute-start(f32[96,4]{0,1:T(4,128)S(1)} %collective-permute-done.1), channel_id=1, source_target_pairs={{0,1},{1,0},{2,3},{3,2},{4,5},{5,4},{6,7},{7,6},{8,9},{9,8},{10,11... | collective-permute-start | bytes 4616 | tf_op jit(solution)/shard_map/ppermute | solution.py:359
  29.9 0.2 select_reduce_fusion
  30.1 0.1 pad_add_fusion
  30.1 0.6 collective-permute-done.3
  30.7 0.0 copy-done.2
  30.7 0.1 fusion.1
  30.8 0.1 copy.9.trace_ref.old_ref
  30.9 0.0 copy-start
  30.9 0.9 copy-done
  31.8 3.8 %denominator.1.tiles_ref = f32[6336,128]{1,0:T(8,128)S(1)} custom-call(s32[192]{0:T(256)S(1)} %get-tuple-element.37.place_ref, bf16[384,128]{1,0:T(8,128)(2,1)S(1)} %copy-done, bf16[480,128]{1,0:T(8,128)(2,1)S(1)} %collective-permute-done.packet_ref, f32[192,128]{1,0:T(8,128)S(1)} %copy.9.trace_ref.old_ref), custom_call_target="tpu_custom_call" | custom-call | tf_op jit(solution)/shard_map/denominator/pallas_call | solution.py:374
  35.6 44.3 %all-to-all-done = bf16[256,32,128]{2,1,0:T(8,128)(2,1)} async-done(((bf16[256,32,128]{2,1,0:T(8,128)(2,1)}), bf16[256,32,128]{2,1,0:T(8,128)(2,1)}, u32[]{:S(2)}, u32[]{:S(2)}) %all-to-all-start) | async-done | bytes 2097184 | tf_op jit(solution)/shard_map/all_to_all | solution.py:354
  79.9 5.3 %numerator.1 = (f32[9216,128]{1,0:T(8,128)S(1)}, f32[192,128]{1,0:T(8,128)S(1)}) custom-call(s32[192]{0:T(256)S(1)} %get-tuple-element.36.place_ref.spot_ref, f32[6336,128]{1,0:T(8,128)S(1)} %denominator.1.tiles_ref, bf16[8192,128]{1,0:T(8,128)(2,1)} %bitcast.11.image_ref), custom_call_target="tpu_custom_call" | custom-call | tf_op jit(solution)/shard_map/numerator/pallas_call | solution.py:379
  85.2 0.9 collective-permute-start.4
  86.1 0.9 collective-permute-done.4
  87.1 1.5 %collective-permute-start.6 = (f32[96,128]{1,0:T(8,128)S(1)}, f32[96,128]{1,0:T(8,128)S(1)}, u32[]{:S(2)}, u32[]{:S(2)}) collective-permute-start(f32[96,128]{1,0:T(8,128)S(1)} %get-tuple-element.32), channel_id=1, source_target_pairs={{0,254},{2,4},{4,2},{6,8},{8,6},{10,12},{12,10},{14,16},{16,14},{1... | collective-permute-start | bytes 147464 | tf_op jit(solution)/shard_map/ppermute | solution.py:394
  88.5 0.7 collective-permute-start.5
  89.3 6.2 %collective-permute-done.6.far_ref = f32[96,128]{1,0:T(8,128)S(1)} collective-permute-done((f32[96,128]{1,0:T(8,128)S(1)}, f32[96,128]{1,0:T(8,128)S(1)}, u32[]{:S(2)}, u32[]{:S(2)}) %collective-permute-start.6) | collective-permute-done | bytes 49184 | tf_op jit(solution)/shard_map/ppermute | solution.py:394
  95.5 0.0 collective-permute-done.5.near_ref
  95.5 0.0 copy-start.1
  95.5 4.4 %lower.1 = (f32[192,128]{1,0:T(8,128)S(1)}, f32[16384,128]{1,0:T(8,128)S(1)}, bf16[384,128]{1,0:T(8,128)(2,1)}) custom-call(s32[192]{0:T(256)S(1)} %get-tuple-element.37.place_ref, s32[192]{0:T(256)S(1)} %get-tuple-element.36.place_ref.spot_ref, bf16[480,128]{1,0:T(8,128)(2,1)S(1)} %collective-permute-done.packet_ref, f32[6336,128]{1,0:T(8,128)S(1)} %denominator.1.tiles_ref, ...), custom_call_target="tpu_custom_call" | custom-call | tf_op jit(solution)/shard_map/lower/pallas_call | solution.py:398
  99.9 2.8 %collective-permute-start.9 = (bf16[384,128]{1,0:T(8,128)(2,1)}, bf16[384,128]{1,0:T(8,128)(2,1)S(1)}, u32[]{:S(2)}, u32[]{:S(2)}) collective-permute-start(bf16[384,128]{1,0:T(8,128)(2,1)} %get-tuple-element.28), channel_id=1, source_target_pairs={{2,1},{3,0},{4,3},{5,2},{6,5},{7,4},{8,7},{9,6},{10,9},{11,8},{12,... | collective-permute-start | bytes 294920 | tf_op jit(solution)/shard_map/ppermute | solution.py:405
  102.7 0.0 collective-permute-start.7
  102.7 0.0 copy-done.1
  102.7 2.1 %upper.1 = (bf16[384,128]{1,0:T(8,128)(2,1)S(1)}, bf16[384,128]{1,0:T(8,128)(2,1)S(1)}) custom-call(s32[192]{0:T(256)S(1)} %get-tuple-element.37.place_ref, s32[192]{0:T(256)S(1)} %get-tuple-element.36.place_ref.spot_ref, bf16[384,128]{1,0:T(8,128)(2,1)S(1)} %copy-done.1, f32[9216,128]{1,0:T(8,128)S(1)} %get-tuple-element.22.image_ref, ...), custom_call_target="tpu_custom_call" | custom-call | tf_op jit(solution)/shard_map/upper/pallas_call | solution.py:406
  104.8 0.1 copy.11
  104.9 0.5 collective-permute-start.8
  105.4 0.6 broadcast_select_fusion
  106.0 0.4 collective-permute-done.8.upper_other
  106.4 0.0 collective-permute-done.9.lower_other
  106.4 0.9 collective-permute-done.7.lower_ref
  107.3 1.2 %merge.1 = bf16[1536,128]{1,0:T(8,128)(2,1)} custom-call(s32[96,128]{1,0:T(8,128)S(1)} %get-tuple-element.25.odd_ref, bf16[384,128]{1,0:T(8,128)(2,1)S(1)} %get-tuple-element.27.upper_ref, bf16[384,128]{1,0:T(8,128)(2,1)S(1)} %collective-permute-done.7.lower_ref, bf16[384,128]{1,0:T(8,128)(2,1)S(1)} %collective-permute-done.8.upper_other, ...), custom_call_target="tpu_custom_call" | custom-call | tf_op jit(solution)/shard_map/merge/pallas_call | solution.py:411
  (8 shorter events, 0.1 us)
Async XLA Ops:
  3.4 14.1 %collective-permute-start = (bf16[480,128]{1,0:T(8,128)(2,1)S(1)}, bf16[480,128]{1,0:T(8,128)(2,1)S(1)}, u32[]{:S(2)}, u32[]{:S(2)}) collective-permute-start(bf16[480,128]{1,0:T(8,128)(2,1)S(1)} %get-tuple-element.16), channel_id=1, source_target_pairs={{0,2},{2,4},{4,6},{6,8},{8,10},{10,12},{12,14},{14,16},{16,18},{18... | collective-permute-start | bytes 368648 | tf_op jit(solution)/shard_map/ppermute | solution.py:341
  5.4 7.3 %collective-permute-start.2 = (f32[96,4]{0,1:T(4,128)}, f32[96,4]{0,1:T(4,128)S(1)}, u32[]{:S(2)}, u32[]{:S(2)}) collective-permute-start(f32[96,4]{0,1:T(4,128)} %bitcast.25), channel_id=1, source_target_pairs={{0,1},{1,0},{2,3},{3,2},{4,5},{5,4},{6,7},{7,6},{8,9},{9,8},{10,11... | collective-permute-start | bytes 4616 | tf_op jit(solution)/shard_map/ppermute | solution.py:332
  6.6 10.9 %collective-permute-start.1 = (f32[96,4]{0,1:T(4,128)}, f32[96,4]{0,1:T(4,128)S(1)}, u32[]{:S(2)}, u32[]{:S(2)}) collective-permute-start(f32[96,4]{0,1:T(4,128)} %bitcast.26), channel_id=1, source_target_pairs={{0,2},{2,4},{4,6},{6,8},{8,10},{10,12},{12,14},{14,16},{16,18},{18... | collective-permute-start | bytes 4616 | tf_op jit(solution)/shard_map/ppermute | solution.py:331
  7.6 23.1 %copy-start.2 = (f32[1,96,4]{1,2,0:T(4,128)S(1)}, f32[1,96,4]{1,2,0:T(4,128)}, u32[]{:S(2)}) copy-start(f32[1,96,4]{1,2,0:T(4,128)} %param.10) | copy-start | bytes 4612
  17.5 62.4 %all-to-all-start = ((bf16[256,32,128]{2,1,0:T(8,128)(2,1)}), bf16[256,32,128]{2,1,0:T(8,128)(2,1)}, u32[]{:S(2)}, u32[]{:S(2)}) async-start(bf16[256,32,128]{2,1,0:T(8,128)(2,1)} %bitcast.10), calls=%async_computation | async-start | bytes 4194304 | tf_op jit(solution)/shard_map/all_to_all | solution.py:354
  27.6 3.1 %collective-permute-start.3 = (f32[96,4]{0,1:T(4,128)S(1)}, f32[96,4]{0,1:T(4,128)S(1)}, u32[]{:S(2)}, u32[]{:S(2)}) collective-permute-start(f32[96,4]{0,1:T(4,128)S(1)} %collective-permute-done.1), channel_id=1, source_target_pairs={{0,1},{1,0},{2,3},{3,2},{4,5},{5,4},{6,7},{7,6},{8,9},{9,8},{10,11... | collective-permute-start | bytes 4616 | tf_op jit(solution)/shard_map/ppermute | solution.py:359
  30.9 0.9 copy-start
  85.2 1.9 %collective-permute-start.4 = (f32[192,128]{1,0:T(8,128)S(1)}, f32[192,128]{1,0:T(8,128)S(1)}, u32[]{:S(2)}, u32[]{:S(2)}) collective-permute-start(f32[192,128]{1,0:T(8,128)S(1)} %get-tuple-element.23), channel_id=1, source_target_pairs={{0,1},{1,0},{2,3},{3,2},{4,5},{5,4},{6,7},{7,6},{8,9},{9,8},{10,11... | collective-permute-start | bytes 294920 | tf_op jit(solution)/shard_map/ppermute | solution.py:391
  87.1 8.5 %collective-permute-start.6 = (f32[96,128]{1,0:T(8,128)S(1)}, f32[96,128]{1,0:T(8,128)S(1)}, u32[]{:S(2)}, u32[]{:S(2)}) collective-permute-start(f32[96,128]{1,0:T(8,128)S(1)} %get-tuple-element.32), channel_id=1, source_target_pairs={{0,254},{2,4},{4,2},{6,8},{8,6},{10,12},{12,10},{14,16},{16,14},{1... | collective-permute-start | bytes 147464 | tf_op jit(solution)/shard_map/ppermute | solution.py:394
  88.5 7.0 %collective-permute-start.5 = (f32[96,128]{1,0:T(8,128)S(1)}, f32[96,128]{1,0:T(8,128)S(1)}, u32[]{:S(2)}, u32[]{:S(2)}) collective-permute-start(f32[96,128]{1,0:T(8,128)S(1)} %get-tuple-element.33), channel_id=1, source_target_pairs={{0,2},{2,0},{4,6},{6,4},{8,10},{10,8},{12,14},{14,12},{16,18},{18,... | collective-permute-start | bytes 147464 | tf_op jit(solution)/shard_map/ppermute | solution.py:395
  95.5 7.2 %copy-start.1 = (bf16[384,128]{1,0:T(8,128)(2,1)S(1)}, bf16[384,128]{1,0:T(8,128)(2,1)}, u32[]{:S(2)}) copy-start(bf16[384,128]{1,0:T(8,128)(2,1)} %get-tuple-element.18.upper_ref) | copy-start | bytes 294916
  99.9 6.5 %collective-permute-start.9 = (bf16[384,128]{1,0:T(8,128)(2,1)}, bf16[384,128]{1,0:T(8,128)(2,1)S(1)}, u32[]{:S(2)}, u32[]{:S(2)}) collective-permute-start(bf16[384,128]{1,0:T(8,128)(2,1)} %get-tuple-element.28), channel_id=1, source_target_pairs={{2,1},{3,0},{4,3},{5,2},{6,5},{7,4},{8,7},{9,6},{10,9},{11,8},{12,... | collective-permute-start | bytes 294920 | tf_op jit(solution)/shard_map/ppermute | solution.py:405
  102.7 4.6 %collective-permute-start.7 = (bf16[384,128]{1,0:T(8,128)(2,1)}, bf16[384,128]{1,0:T(8,128)(2,1)S(1)}, u32[]{:S(2)}, u32[]{:S(2)}) collective-permute-start(bf16[384,128]{1,0:T(8,128)(2,1)} %get-tuple-element.28), channel_id=1, source_target_pairs={{2,0},{4,2},{6,4},{8,6},{10,8},{12,10},{14,12},{16,14},{18,16},{20... | collective-permute-start | bytes 294920 | tf_op jit(solution)/shard_map/ppermute | solution.py:404
  104.9 1.5 %collective-permute-start.8 = (bf16[384,128]{1,0:T(8,128)(2,1)S(1)}, bf16[384,128]{1,0:T(8,128)(2,1)S(1)}, u32[]{:S(2)}, u32[]{:S(2)}) collective-permute-start(bf16[384,128]{1,0:T(8,128)(2,1)S(1)} %get-tuple-element.29), channel_id=1, source_target_pairs={{0,1},{1,0},{2,3},{3,2},{4,5},{5,4},{6,7},{7,6},{8,9},{9,8},{10,11... | collective-permute-start | bytes 294920 | tf_op jit(solution)/shard_map/ppermute | solution.py:410

commit v3 on v2

--- a/solution.py
+++ b/solution.py
@@ -9,6 +9,7 @@
 PR = 8
 PC = 16
 VOX = PR * PC
+CHUNKS = 2
 BAND = 224
 NF = 8
 KT = 96
@@ -37,7 +38,7 @@
     return pl.BlockSpec(memory_space=pltpu.SMEM)
 
 
-def call(kernel, out_shape, in_specs, scratch=(), name=None, limit=24, out_specs=None):
+def call(kernel, out_shape, in_specs, scratch=(), name=None, limit=24, out_specs=None, aliases=None):
     if out_specs is None:
         out_specs = [vmem() for _ in out_shape] if isinstance(out_shape, (list, tuple)) else vmem()
     return pl.pallas_call(
@@ -46,6 +47,7 @@
         in_specs=in_specs,
         out_specs=out_specs,
         scratch_shapes=list(scratch),
+        input_output_aliases=aliases or {},
         compiler_params=pltpu.CompilerParams(vmem_limit_bytes=limit * MIB),
         name=name,
     )
@@ -76,11 +78,15 @@
         out_ref[a * KT : (a + 1) * KT, :] = value.astype(BF16)
 
 
-def rows_kernel(count_ref, block_ref, foot_ref, packet_ref, upper_ref, odd_ref, wide):
+def rows_kernel(count_ref, block_ref, foot_ref, packet_ref, wide):
     plane, place, odd = places(block_ref)
     info = jnp.where(iota((KT, VOX), 1) < 64, plane, place.astype(F32))
     packet_ref[NA * KT : NA * KT + KT, :] = info.astype(BF16)
     pick_rows(1, count_ref, odd, foot_ref, packet_ref, wide)
+
+
+def own_rows_kernel(count_ref, block_ref, foot_ref, packet_ref, upper_ref, odd_ref, wide):
+    odd = places(block_ref)[2]
     odd_ref[...] = odd
     pick_rows(0, count_ref, odd, foot_ref, upper_ref, wide)
 
@@ -156,13 +162,15 @@
     lax.fori_loop(0, rows // step, body, 0)
 
 
-def rebuild(place_ref, tiles_ref, trace_ref, field_ref):
+def clear(field_ref):
     zero(field_ref, 0, FIELD * PR)
 
     @pl.when(lax.axis_index("tile") == 0)
     def _():
         zero(field_ref, FIELD * PR, FIELD * PR)
 
+
+def rebuild(place_ref, tiles_ref, trace_ref, field_ref):
     def body(n, carry):
         trace = jnp.broadcast_to(trace_ref[pl.ds(n, 1), :], (PR, VOX))
         base = place_ref[n]
@@ -196,6 +204,7 @@
     place_ref, upper_ref, packet_ref, trace_ref, tiles_ref, field, sums
 ):
     expand(upper_ref, packet_ref, tiles_ref)
+    clear(field)
     rebuild(place_ref, tiles_ref, trace_ref, field)
     tiles_ref[TILES * PR : TILES * PR + NH, :] = project(place_ref, tiles_ref, field, sums)
 
@@ -205,6 +214,10 @@
 
 
 def numer_kernel(place_ref, tiles_ref, image_ref, field_ref, sums_ref, permute_ref, sums):
+    groups = XC // 8
+    rows = groups * PR
+    step = Z // CHUNKS
+    chunk = step * NF * rows
     source = iota((VOX, NF * VOX), 0)
     target = iota((VOX, NF * VOX), 1)
     same = (source // PC == target // VOX) & (source % PC == target % PC)
@@ -215,26 +228,19 @@
         for r in range(VOX // 16):
             at = f * VOX + 16 * r
             permute_ref[at : at + 16, :] = same[16 * r : 16 * r + 16, :] * mine
-    groups = XC // 8
-    rows = groups * PR
-    step = 16
-
-    def body(k, carry):
-        base = pl.multiple_of(k * (step * NF * rows), step * NF * rows)
-        image = image_ref[pl.ds(base, step * NF * rows), :]
+    for k in range(CHUNKS):
         lhs = []
         for z in range(step):
-            start = z * NF * rows
-            lhs.append(jnp.concatenate([image[start + f * rows : start + (f + 1) * rows, :] for f in range(NF)], axis=1))
+            start = k * chunk + z * NF * rows
+            frames = [image_ref[start + f * rows : start + (f + 1) * rows, :] for f in range(NF)]
+            lhs.append(jnp.concatenate(frames, axis=1))
         out = jnp.dot(jnp.concatenate(lhs, axis=0), permute_ref[...], preferred_element_type=F32)
         for z in range(step):
             for g in range(groups):
                 for x in range(8):
                     at = z * rows + g * PR
-                    tile_at(field_ref, (k * step + z) * XC + g * 8 + x)[...] = out[at : at + PR, x * VOX : (x + 1) * VOX]
-        return carry
-
-    lax.fori_loop(0, Z // step, body, 0)
+                    to = ((k * step + z) * XC + g * 8 + x) * PR
+                    field_ref[to : to + PR, :] = out[at : at + PR, x * VOX : (x + 1) * VOX]
     field_ref[FIELD * PR : (FIELD + PADF) * PR, :] = jnp.zeros((PADF * PR, VOX), F32)
     numer = project(place_ref, tiles_ref, field_ref, sums)
     denom = tiles_ref[TILES * PR : TILES * PR + NH, :]
@@ -245,13 +251,25 @@
     sums_ref[KT:, :] = jnp.where(even, upper, lower)
 
 
-def fold(products_ref):
+def stage_kernel(spot_ref, image_ref, found_ref, field_ref):
+    for d in range(2):
+        def body(k, carry):
+            spot = spot_ref[d * KT + k]
+            for a in range(NA):
+                tile_at(found_ref, (d * NA + a) * KT + k)[...] = tile_at(image_ref, spot + a * XC)[...]
+            return carry
+
+        lax.fori_loop(0, KT, body, 0, unroll=8)
+    clear(field_ref)
+
+
+def fold(start, tiles_ref, traces):
     lane_in = iota((2 * VOX, VOX), 0) % VOX
     lane_out = iota((2 * VOX, VOX), 1)
     total = None
     for i in range(PR):
         pick = jnp.where((lane_out // PC == i) & (lane_out % PC == lane_in % PC), 1.0, 0.0).astype(BF16)
-        rows = products_ref[pl.ds(i, NA * KT, stride=PR), :]
+        rows = tiles_ref[pl.ds(start * PR + i, NA * KT, stride=PR), :] * traces
         high = rows.astype(BF16)
         low = (rows - high.astype(F32)).astype(BF16)
         part = jnp.dot(jnp.concatenate([high, low], axis=1), pick, preferred_element_type=F32)
@@ -259,26 +277,22 @@
     return total
 
 
-def renew(start, place_ref, spot_ref, rows_ref, image_ref, field_ref, trace_ref, product_n, product_d):
+def renew(d, place_ref, rows_ref, found_ref, field_ref, trace_ref, rebuilt):
     def body(k, carry):
-        n = start + k
-        trace = jnp.broadcast_to(trace_ref[pl.ds(n, 1), :], (PR, VOX))
-        base = place_ref[n]
-        spot = spot_ref[n]
+        base = place_ref[d * KT + k]
         for a in range(NA):
-            m = a * KT + k
-            tile_at(product_n, m)[...] = tile_at(image_ref, spot + a * XC)[...] * trace
-            tile_at(product_d, m)[...] = tile_at(field_ref, base + a * XC)[...] * trace
+            tile_at(rebuilt, a * KT + k)[...] = tile_at(field_ref, base + a * XC)[...]
         return carry
 
     lax.fori_loop(0, KT, body, 0, unroll=8)
-    ratio = fold(product_n) / (fold(product_d) + EPSILON)
+    traces = jnp.concatenate([trace_ref[d * KT : (d + 1) * KT, :]] * NA, axis=0)
+    ratio = fold(d * NA * KT, found_ref, traces) / (fold(0, rebuilt, traces) + EPSILON)
     return (rows_ref[0 : NA * KT, :].astype(F32) * ratio).astype(BF16)
 
 
 def lower_kernel(
-    place_ref, spot_ref, packet_ref, tiles_ref, image_ref, old_ref, mine_ref, near_ref, far_ref,
-    trace_ref, field_ref, out_ref, product_n, product_d,
+    place_ref, packet_ref, tiles_ref, found_ref, old_ref, mine_ref, near_ref, far_ref, cleared_ref,
+    trace_ref, field_ref, out_ref, rebuilt,
 ):
     even = even_tile()
     first_mine, second_mine = mine_ref[:KT, :], mine_ref[KT:, :]
@@ -291,15 +305,11 @@
     denom = jnp.where(first, pltpu.roll(sums, VOX - PC // 2, 1), sums)
     trace_ref[...] = old_ref[...] * numer / (denom + EPSILON)
     rebuild(place_ref, tiles_ref, trace_ref, field_ref)
-    out_ref[...] = renew(
-        KT, place_ref, spot_ref, packet_ref, image_ref, field_ref, trace_ref, product_n, product_d
-    )
-
-
-def upper_kernel(
-    place_ref, spot_ref, upper_ref, image_ref, field_ref, trace_ref, out_ref, sent_ref, product_n, product_d
-):
-    value = renew(0, place_ref, spot_ref, upper_ref, image_ref, field_ref, trace_ref, product_n, product_d)
+    out_ref[...] = renew(1, place_ref, packet_ref, found_ref, field_ref, trace_ref, rebuilt)
+
+
+def upper_kernel(place_ref, upper_ref, found_ref, field_ref, trace_ref, out_ref, sent_ref, rebuilt):
+    value = renew(0, place_ref, upper_ref, found_ref, field_ref, trace_ref, rebuilt)
     out_ref[...] = value
     sent_ref[...] = value
 
@@ -335,8 +345,8 @@
     block_rows = hbm(blocks.T, pltpu.HBM)
     foot_rows = hbm(footprints.reshape(-1, VOX), pltpu.HBM)
     wide = pltpu.VMEM((KT * 16, VOX), F32)
-    packet, upper, odd = call(
-        rows_kernel, [shape(NA * KT + KT, BF16), pltpu.HBM((NA * KT, VOX), BF16), shape(KT, jnp.int32)], [smem(), vmem(), vmem()], scratch=[wide], name="rows", limit=4,
+    packet = call(
+        rows_kernel, shape(NA * KT + KT, BF16), [smem(), vmem(), vmem()], scratch=[wide], name="rows", limit=4,
     )(counts, block_rows, foot_rows)
     packet_in = lax.ppermute(packet, "tile", down)
 
@@ -355,6 +365,11 @@
         sent.reshape(tiles * 2, XC, VOX), ("tile", "nrn"), split_axis=0, concat_axis=0, tiled=True
     ).reshape(-1, VOX)
 
+    upper, odd = call(
+        own_rows_kernel, [pltpu.HBM((NA * KT, VOX), BF16), shape(KT, jnp.int32)],
+        [smem(), vmem(), vmem(), pl.BlockSpec(memory_space=pl.ANY)], scratch=[wide], name="own_rows", limit=4,
+    )(counts, block_rows, foot_rows, packet_in)
+
     both = jnp.concatenate([mine, above], axis=0)
     other = jnp.concatenate([theirs, lax.ppermute(above, "nrn", cross)], axis=0)
     frames = jnp.stack([jnp.where(core == 0, both, other), jnp.where(core == 0, other, both)], axis=-1)
@@ -378,9 +393,10 @@
     tiles_e = in_vmem(tiles_e, pltpu.VMEM)
     image_field, partial = call(
         numer_kernel, [pltpu.VMEM(((FIELD + PADF) * PR, VOX), F32), shape(NH, F32)],
-        [smem()] + [vmem()] * 2,
-        scratch=[pltpu.VMEM((NF * VOX, NF * VOX), BF16), sums], name="numerator", limit=12,
-    )(spot, tiles_e, images)
+        [smem(), vmem(), vmem()],
+        scratch=[pltpu.VMEM((NF * VOX, NF * VOX), BF16), sums],
+        name="numerator", limit=12,
+    )(spot, tiles_e, in_vmem(images, pltpu.VMEM))
     image_field = in_vmem(image_field, pltpu.VMEM)
 
     everyone = ("tile", "nrn")
@@ -394,19 +410,25 @@
     from_far = lax.ppermute(partial[:KT], "tile", far)
     from_near = lax.ppermute(partial[KT:], "tile", near)
 
-    product = pltpu.VMEM((NA * KT * PR, VOX), F32)
+    image_field, _ = lax.optimization_barrier((image_field, partial))
+    found, cleared = call(
+        stage_kernel, [pltpu.VMEM((TILES * PR, VOX), F32), pltpu.VMEM((2 * FIELD * PR, VOX), F32)],
+        [smem(), vmem()], name="stage", limit=4,
+    )(spot, in_vmem(image_field, pltpu.VMEM))
+    found, cleared = in_vmem(found, pltpu.VMEM), in_vmem(cleared, pltpu.VMEM)
+    half = pltpu.VMEM((NA * KT * PR, VOX), F32)
     new, rebuilt, lower_new = call(
         lower_kernel,
         [shape(NH, F32), pltpu.VMEM((2 * FIELD * PR, VOX), F32), shape(NA * KT, BF16)],
-        [smem()] * 2 + [vmem()] * 7,
-        scratch=[product, product], name="lower", limit=8,
-    )(place, spot, packet_in, tiles_e, image_field, old, partial, from_near, from_far)
+        [smem()] + [vmem()] * 8,
+        scratch=[half], name="lower", limit=8, aliases={8: 1},
+    )(place, packet_in, tiles_e, found, old, partial, from_near, from_far, cleared)
     lower_back = lax.ppermute(lower_new, "tile", up)
     lower_other = lax.ppermute(lower_new, everyone, other_core(up))
     upper_new, upper_sent = call(
-        upper_kernel, [shape(NA * KT, BF16)] * 2, [smem()] * 2 + [vmem()] * 4,
-        scratch=[product, product], name="upper", limit=8,
-    )(place, spot, upper, image_field, in_vmem(rebuilt, pltpu.VMEM), new)
+        upper_kernel, [shape(NA * KT, BF16)] * 2, [smem()] + [vmem()] * 4,
+        scratch=[half], name="upper", limit=8,
+    )(place, upper, found, in_vmem(rebuilt, pltpu.VMEM), new)
     upper_other = lax.ppermute(upper_sent, "nrn", cross)
     merged = call(
         merge_kernel, shape(KT * 16, BF16), [vmem()] * 5,

time: 109 us -> 107 us (0.982)
  waiting for transfers between devices: 58.1 us -> 54.3 us
  Pallas kernels: 23.8 us -> 25.6 us
    pallas_call x2 -> x4, Pallas kernels: 4.15 us -> 7.02 us  [the longest x1 1.92 us: shards(): call(own_rows_kernel, [pltpu.HBM((NA * KT, VOX), BF16), shape(KT, jnp.int...]
    ppermute x1, waiting for transfers between devices: 6.24 us -> 4.34 us  [shards(): from_far = lax.ppermute(partial[:KT], 'tile', far)]
    all_to_all x1, waiting for transfers between devices: 44.3 us -> 42.9 us  [shards(): lax.all_to_all(sent.reshape(tiles * 2, XC, VOX), ('tile', 'nrn'), split_a...]
  transfers between devices with their start and end apart: 11 -> 11, of which waited for: 7 -> 6; matrix products, arithmetic and copies ran while one was open for 1% -> 1% of each run, Pallas kernels for 10% -> 14%
where the time goes in v3:
time: 107 us
  waiting for transfers between devices  54.3 us (51%)
  Pallas kernels  25.6 us (24%)
  starting transfers between devices  23.1 us (22%)
  between operations  1.43 us (1%)
  local copies, waits for them, and re-layouts  1.13 us (1%)
  other arithmetic  1.12 us (1%)
    all_to_all x1, waiting for transfers between devices, shards(): lax.all_to_all(sent.reshape(tiles * 2, XC, VOX), ('tile', 'nrn'), split_a...  42.9 us
    all_to_all x1, starting transfers between devices, shards(): lax.all_to_all(sent.reshape(tiles * 2, XC, VOX), ('tile', 'nrn'), split_a...  9.74 us
    pallas_call x1, Pallas kernels, shards(): call(numer_kernel, [pltpu.VMEM(((FIELD + PADF) * PR, VOX), F32), shape(NH...  5.05 us
    pallas_call x1, Pallas kernels, shards(): call(register_kernel, shape(tiles * 2 * XC, BF16), [smem(), outside], scr...  5.01 us
    ppermute x1, waiting for transfers between devices, shards(): above = lax.ppermute(mine, 'tile', down)  4.89 us
    ppermute x1, waiting for transfers between devices, shards(): from_far = lax.ppermute(partial[:KT], 'tile', far)  4.34 us
    pallas_call x1, Pallas kernels, shards(): call(denom_kernel, pltpu.VMEM((TILES * PR + NH, VOX), F32), [smem()] + [v...  3.75 us
    pallas_call x1, Pallas kernels, shards(): call(lower_kernel, [shape(NH, F32), pltpu.VMEM((2 * FIELD * PR, VOX), F32...  3.59 us
  transfers between devices with their start and end apart: 11, of which 6 were waited for; matrix products, arithmetic and copies ran while one was open for 1% of the time, Pallas kernels for 14%

profile of v3, /device:TPU:1, one launch (start us, length us, event | category | flops | bytes accessed | tf_op | source)
XLA Modules:
  0.0 106.7 jit_solution(7370640261877631101)
XLA Ops:
  1.3 1.3 %rows.1 = bf16[480,128]{1,0:T(8,128)(2,1)S(1)} custom-call(s32[1]{0:T(128)S(6)} %copy.14.count_ref, s32[16,96]{1,0:T(8,128)} %bitcast.24, bf16[1536,128]{1,0:T(8,128)(2,1)} %bitcast.19), custom_call_target="tpu_custom_call" | custom-call | tf_op jit(solution)/shard_map/rows/pallas_call | solution.py:348
  2.6 2.1 %collective-permute-start = (bf16[480,128]{1,0:T(8,128)(2,1)S(1)}, bf16[480,128]{1,0:T(8,128)(2,1)S(1)}, u32[]{:S(2)}, u32[]{:S(2)}) collective-permute-start(bf16[480,128]{1,0:T(8,128)(2,1)S(1)} %rows.1), channel_id=1, source_target_pairs={{0,2},{2,4},{4,6},{6,8},{8,10},{10,12},{12,14},{14,16},{16,18},{18... | collective-permute-start | bytes 368648 | tf_op jit(solution)/shard_map/ppermute | solution.py:351
  4.7 1.3 %collective-permute-start.2 = (f32[96,4]{0,1:T(4,128)}, f32[96,4]{0,1:T(4,128)S(1)}, u32[]{:S(2)}, u32[]{:S(2)}) collective-permute-start(f32[96,4]{0,1:T(4,128)} %bitcast.27), channel_id=1, source_target_pairs={{0,1},{1,0},{2,3},{3,2},{4,5},{5,4},{6,7},{7,6},{8,9},{9,8},{10,11... | collective-permute-start | bytes 4616 | tf_op jit(solution)/shard_map/ppermute | solution.py:342
  6.0 0.9 collective-permute-start.1
  6.9 5.0 %register.1 = bf16[8192,128]{1,0:T(8,128)(2,1)} custom-call(s32[2]{0:T(128)} %bitcast.34, bf16[1024,1024]{1,0:T(8,128)(2,1)} %bitcast.18), custom_call_target="tpu_custom_call" | custom-call | tf_op jit(solution)/shard_map/register/pallas_call | solution.py:355
  11.9 0.0 copy-start.2
  11.9 0.0 collective-permute-done.2
  11.9 4.9 %collective-permute-done.1 = f32[96,4]{0,1:T(4,128)S(1)} collective-permute-done((f32[96,4]{0,1:T(4,128)}, f32[96,4]{0,1:T(4,128)S(1)}, u32[]{:S(2)}, u32[]{:S(2)}) %collective-permute-start.1) | collective-permute-done | bytes 1568 | tf_op jit(solution)/shard_map/ppermute | solution.py:341
  16.8 0.0 collective-permute-done.packet_ref
  16.8 9.7 %all-to-all-start = ((bf16[256,32,128]{2,1,0:T(8,128)(2,1)}), bf16[256,32,128]{2,1,0:T(8,128)(2,1)}, u32[]{:S(2)}, u32[]{:S(2)}) async-start(bf16[256,32,128]{2,1,0:T(8,128)(2,1)} %bitcast.10), calls=%async_computation | async-start | bytes 4194304 | tf_op jit(solution)/shard_map/all_to_all | solution.py:364
  26.6 0.2 add_reduce_fusion.1
  26.8 2.3 %collective-permute-start.3 = (f32[96,4]{0,1:T(4,128)S(1)}, f32[96,4]{0,1:T(4,128)S(1)}, u32[]{:S(2)}, u32[]{:S(2)}) collective-permute-start(f32[96,4]{0,1:T(4,128)S(1)} %collective-permute-done.1), channel_id=1, source_target_pairs={{0,1},{1,0},{2,3},{3,2},{4,5},{5,4},{6,7},{7,6},{8,9},{9,8},{10,11... | collective-permute-start | bytes 4616 | tf_op jit(solution)/shard_map/ppermute | solution.py:374
  29.1 0.2 select_reduce_fusion
  29.3 0.1 pad_add_fusion
  29.3 1.9 %own_rows.1 = (bf16[384,128]{1,0:T(8,128)(2,1)}, s32[96,128]{1,0:T(8,128)S(1)}) custom-call(s32[1]{0:T(128)S(6)} %copy.14.count_ref, s32[16,96]{1,0:T(8,128)} %bitcast.25, bf16[1536,128]{1,0:T(8,128)(2,1)} %bitcast.20, bf16[480,128]{1,0:T(8,128)(2,1)S(1)} %collective-permute-done.packet_ref), custom_call_target="tpu_custom_call" | custom-call | tf_op jit(solution)/shard_map/own_rows/pallas_call | solution.py:368
  31.3 0.0 collective-permute-done.3
  31.3 0.0 copy-done.2
  31.3 0.1 fusion.1
  31.4 0.1 copy.10.trace_ref.old_ref
  31.5 0.0 copy-start
  31.5 0.9 copy-done
  32.4 3.8 %denominator.1.tiles_ref = f32[6336,128]{1,0:T(8,128)S(1)} custom-call(s32[192]{0:T(256)S(1)} %get-tuple-element.41.place_ref, bf16[384,128]{1,0:T(8,128)(2,1)S(1)} %copy-done, bf16[480,128]{1,0:T(8,128)(2,1)S(1)} %collective-permute-done.packet_ref, f32[192,128]{1,0:T(8,128)S(1)} %copy.10.trace_ref.old_ref), custom_call_target="tpu_custom_call" | custom-call | tf_op jit(solution)/shard_map/denominator/pallas_call | solution.py:389
  36.1 42.9 %all-to-all-done = bf16[256,32,128]{2,1,0:T(8,128)(2,1)} async-done(((bf16[256,32,128]{2,1,0:T(8,128)(2,1)}), bf16[256,32,128]{2,1,0:T(8,128)(2,1)}, u32[]{:S(2)}, u32[]{:S(2)}) %all-to-all-start) | async-done | bytes 2097184 | tf_op jit(solution)/shard_map/all_to_all | solution.py:364
  79.1 5.1 %numerator.1 = (f32[9216,128]{1,0:T(8,128)S(1)}, f32[192,128]{1,0:T(8,128)S(1)}) custom-call(s32[192]{0:T(256)S(1)} %get-tuple-element.40.place_ref.spot_ref, f32[6336,128]{1,0:T(8,128)S(1)} %denominator.1.tiles_ref, bf16[8192,128]{1,0:T(8,128)(2,1)} %bitcast.11.image_ref), custom_call_target="tpu_custom_call" | custom-call | tf_op jit(solution)/shard_map/numerator/pallas_call | solution.py:394
  84.2 0.9 collective-permute-start.4
  85.1 0.9 collective-permute-done.4
  86.0 1.5 %collective-permute-start.6 = (f32[96,128]{1,0:T(8,128)S(1)}, f32[96,128]{1,0:T(8,128)S(1)}, u32[]{:S(2)}, u32[]{:S(2)}) collective-permute-start(f32[96,128]{1,0:T(8,128)S(1)} %get-tuple-element.36), channel_id=1, source_target_pairs={{0,254},{2,4},{4,2},{6,8},{8,6},{10,12},{12,10},{14,16},{16,14},{1... | collective-permute-start | bytes 147464 | tf_op jit(solution)/shard_map/ppermute | solution.py:410
  87.5 0.7 collective-permute-start.5
  88.3 1.9 %stage.1 = (f32[6144,128]{1,0:T(8,128)S(1)}, f32[16384,128]{1,0:T(8,128)S(1)}) custom-call(s32[192]{0:T(256)S(1)} %get-tuple-element.40.place_ref.spot_ref, f32[9216,128]{1,0:T(8,128)S(1)} %get-tuple-element.25.image_ref), custom_call_target="tpu_custom_call" | custom-call | tf_op jit(solution)/shard_map/stage/pallas_call | solution.py:414
  90.2 4.3 %collective-permute-done.6.far_ref = f32[96,128]{1,0:T(8,128)S(1)} collective-permute-done((f32[96,128]{1,0:T(8,128)S(1)}, f32[96,128]{1,0:T(8,128)S(1)}, u32[]{:S(2)}, u32[]{:S(2)}) %collective-permute-start.6) | collective-permute-done | bytes 49184 | tf_op jit(solution)/shard_map/ppermute | solution.py:410
  94.5 0.0 collective-permute-done.5.near_ref
  94.5 0.0 copy-start.1
  94.5 3.6 %lower.1 = (f32[192,128]{1,0:T(8,128)S(1)}, f32[16384,128]{1,0:T(8,128)S(1)}, bf16[384,128]{1,0:T(8,128)(2,1)}) custom-call(s32[192]{0:T(256)S(1)} %get-tuple-element.41.place_ref, bf16[480,128]{1,0:T(8,128)(2,1)S(1)} %collective-permute-done.packet_ref, f32[6336,128]{1,0:T(8,128)S(1)} %denominator.1.tiles_ref, ...), custom_call_target="tpu_custom_call", output_to_operand_aliasing={{1}: (8, {})} | custom-call | tf_op jit(solution)/shard_map/lower/pallas_call | solution.py:420
  98.1 3.1 %collective-permute-start.9 = (bf16[384,128]{1,0:T(8,128)(2,1)}, bf16[384,128]{1,0:T(8,128)(2,1)S(1)}, u32[]{:S(2)}, u32[]{:S(2)}) collective-permute-start(bf16[384,128]{1,0:T(8,128)(2,1)} %get-tuple-element.32), channel_id=1, source_target_pairs={{2,1},{3,0},{4,3},{5,2},{6,5},{7,4},{8,7},{9,6},{10,9},{11,8},{12,... | collective-permute-start | bytes 294920 | tf_op jit(solution)/shard_map/ppermute | solution.py:427
  101.2 0.0 collective-permute-start.7
  101.2 0.0 copy-done.1
  101.2 1.9 %upper.1 = (bf16[384,128]{1,0:T(8,128)(2,1)S(1)}, bf16[384,128]{1,0:T(8,128)(2,1)S(1)}) custom-call(s32[192]{0:T(256)S(1)} %get-tuple-element.41.place_ref, bf16[384,128]{1,0:T(8,128)(2,1)S(1)} %copy-done.1, f32[6144,128]{1,0:T(8,128)S(1)} %get-tuple-element.26.found_ref, f32[16384,128]{1,0:T(8,128)S(1)} %get-tuple-element.30.field_ref, ...), custom_call_target="tpu_custom_call" | custom-call | tf_op jit(solution)/shard_map/upper/pallas_call | solution.py:428
  103.1 0.1 copy.12
  103.2 0.5 collective-permute-start.8
  103.7 0.6 broadcast_select_fusion
  104.3 0.4 collective-permute-done.8.upper_other
  104.7 0.0 collective-permute-done.9.lower_other
  104.7 0.8 collective-permute-done.7.lower_ref
  105.5 1.2 %merge.1 = bf16[1536,128]{1,0:T(8,128)(2,1)} custom-call(s32[96,128]{1,0:T(8,128)S(1)} %get-tuple-element.29.odd_ref, bf16[384,128]{1,0:T(8,128)(2,1)S(1)} %get-tuple-element.31.upper_ref, bf16[384,128]{1,0:T(8,128)(2,1)S(1)} %collective-permute-done.7.lower_ref, bf16[384,128]{1,0:T(8,128)(2,1)S(1)} %collective-permute-done.8.upper_other, ...), custom_call_target="tpu_custom_call" | custom-call | tf_op jit(solution)/shard_map/merge/pallas_call | solution.py:433
  (8 shorter events, 0.1 us)
Async XLA Ops:
  2.6 14.2 %collective-permute-start = (bf16[480,128]{1,0:T(8,128)(2,1)S(1)}, bf16[480,128]{1,0:T(8,128)(2,1)S(1)}, u32[]{:S(2)}, u32[]{:S(2)}) collective-permute-start(bf16[480,128]{1,0:T(8,128)(2,1)S(1)} %rows.1), channel_id=1, source_target_pairs={{0,2},{2,4},{4,6},{6,8},{8,10},{10,12},{12,14},{14,16},{16,18},{18... | collective-permute-start | bytes 368648 | tf_op jit(solution)/shard_map/ppermute | solution.py:351
  4.7 7.2 %collective-permute-start.2 = (f32[96,4]{0,1:T(4,128)}, f32[96,4]{0,1:T(4,128)S(1)}, u32[]{:S(2)}, u32[]{:S(2)}) collective-permute-start(f32[96,4]{0,1:T(4,128)} %bitcast.27), channel_id=1, source_target_pairs={{0,1},{1,0},{2,3},{3,2},{4,5},{5,4},{6,7},{7,6},{8,9},{9,8},{10,11... | collective-permute-start | bytes 4616 | tf_op jit(solution)/shard_map/ppermute | solution.py:342
  6.0 10.8 %collective-permute-start.1 = (f32[96,4]{0,1:T(4,128)}, f32[96,4]{0,1:T(4,128)S(1)}, u32[]{:S(2)}, u32[]{:S(2)}) collective-permute-start(f32[96,4]{0,1:T(4,128)} %bitcast.28), channel_id=1, source_target_pairs={{0,2},{2,4},{4,6},{6,8},{8,10},{10,12},{12,14},{14,16},{16,18},{18... | collective-permute-start | bytes 4616 | tf_op jit(solution)/shard_map/ppermute | solution.py:341
  11.9 19.4 %copy-start.2 = (f32[1,96,4]{1,2,0:T(4,128)S(1)}, f32[1,96,4]{1,2,0:T(4,128)}, u32[]{:S(2)}) copy-start(f32[1,96,4]{1,2,0:T(4,128)} %param.10) | copy-start | bytes 4612
  16.8 62.3 %all-to-all-start = ((bf16[256,32,128]{2,1,0:T(8,128)(2,1)}), bf16[256,32,128]{2,1,0:T(8,128)(2,1)}, u32[]{:S(2)}, u32[]{:S(2)}) async-start(bf16[256,32,128]{2,1,0:T(8,128)(2,1)} %bitcast.10), calls=%async_computation | async-start | bytes 4194304 | tf_op jit(solution)/shard_map/all_to_all | solution.py:364
  26.8 4.5 %collective-permute-start.3 = (f32[96,4]{0,1:T(4,128)S(1)}, f32[96,4]{0,1:T(4,128)S(1)}, u32[]{:S(2)}, u32[]{:S(2)}) collective-permute-start(f32[96,4]{0,1:T(4,128)S(1)} %collective-permute-done.1), channel_id=1, source_target_pairs={{0,1},{1,0},{2,3},{3,2},{4,5},{5,4},{6,7},{7,6},{8,9},{9,8},{10,11... | collective-permute-start | bytes 4616 | tf_op jit(solution)/shard_map/ppermute | solution.py:374
  31.5 0.9 copy-start
  84.2 1.9 %collective-permute-start.4 = (f32[192,128]{1,0:T(8,128)S(1)}, f32[192,128]{1,0:T(8,128)S(1)}, u32[]{:S(2)}, u32[]{:S(2)}) collective-permute-start(f32[192,128]{1,0:T(8,128)S(1)} %get-tuple-element.24), channel_id=1, source_target_pairs={{0,1},{1,0},{2,3},{3,2},{4,5},{5,4},{6,7},{7,6},{8,9},{9,8},{10,11... | collective-permute-start | bytes 294920 | tf_op jit(solution)/shard_map/ppermute | solution.py:407
  86.0 8.5 %collective-permute-start.6 = (f32[96,128]{1,0:T(8,128)S(1)}, f32[96,128]{1,0:T(8,128)S(1)}, u32[]{:S(2)}, u32[]{:S(2)}) collective-permute-start(f32[96,128]{1,0:T(8,128)S(1)} %get-tuple-element.36), channel_id=1, source_target_pairs={{0,254},{2,4},{4,2},{6,8},{8,6},{10,12},{12,10},{14,16},{16,14},{1... | collective-permute-start | bytes 147464 | tf_op jit(solution)/shard_map/ppermute | solution.py:410
  87.5 7.0 %collective-permute-start.5 = (f32[96,128]{1,0:T(8,128)S(1)}, f32[96,128]{1,0:T(8,128)S(1)}, u32[]{:S(2)}, u32[]{:S(2)}) collective-permute-start(f32[96,128]{1,0:T(8,128)S(1)} %get-tuple-element.37), channel_id=1, source_target_pairs={{0,2},{2,0},{4,6},{6,4},{8,10},{10,8},{12,14},{14,12},{16,18},{18,... | collective-permute-start | bytes 147464 | tf_op jit(solution)/shard_map/ppermute | solution.py:411
  94.5 6.7 %copy-start.1 = (bf16[384,128]{1,0:T(8,128)(2,1)S(1)}, bf16[384,128]{1,0:T(8,128)(2,1)}, u32[]{:S(2)}) copy-start(bf16[384,128]{1,0:T(8,128)(2,1)} %get-tuple-element.19.upper_ref) | copy-start | bytes 294916
  98.1 6.6 %collective-permute-start.9 = (bf16[384,128]{1,0:T(8,128)(2,1)}, bf16[384,128]{1,0:T(8,128)(2,1)S(1)}, u32[]{:S(2)}, u32[]{:S(2)}) collective-permute-start(bf16[384,128]{1,0:T(8,128)(2,1)} %get-tuple-element.32), channel_id=1, source_target_pairs={{2,1},{3,0},{4,3},{5,2},{6,5},{7,4},{8,7},{9,6},{10,9},{11,8},{12,... | collective-permute-start | bytes 294920 | tf_op jit(solution)/shard_map/ppermute | solution.py:427
  101.2 4.3 %collective-permute-start.7 = (bf16[384,128]{1,0:T(8,128)(2,1)}, bf16[384,128]{1,0:T(8,128)(2,1)S(1)}, u32[]{:S(2)}, u32[]{:S(2)}) collective-permute-start(bf16[384,128]{1,0:T(8,128)(2,1)} %get-tuple-element.32), channel_id=1, source_target_pairs={{2,0},{4,2},{6,4},{8,6},{10,8},{12,10},{14,12},{16,14},{18,16},{20... | collective-permute-start | bytes 294920 | tf_op jit(solution)/shard_map/ppermute | solution.py:426
  103.2 1.4 %collective-permute-start.8 = (bf16[384,128]{1,0:T(8,128)(2,1)S(1)}, bf16[384,128]{1,0:T(8,128)(2,1)S(1)}, u32[]{:S(2)}, u32[]{:S(2)}) collective-permute-start(bf16[384,128]{1,0:T(8,128)(2,1)S(1)} %get-tuple-element.33), channel_id=1, source_target_pairs={{0,1},{1,0},{2,3},{3,2},{4,5},{5,4},{6,7},{7,6},{8,9},{9,8},{10,11... | collective-permute-start | bytes 294920 | tf_op jit(solution)/shard_map/ppermute | solution.py:432

commit v4 on v3

--- a/solution.py
+++ b/solution.py
@@ -9,6 +9,7 @@
 PR = 8
 PC = 16
 VOX = PR * PC
+ROWS = 16
 CHUNKS = 2
 BAND = 224
 NF = 8
@@ -209,6 +210,33 @@
     tiles_ref[TILES * PR : TILES * PR + NH, :] = project(place_ref, tiles_ref, field, sums)
 
 
+def pack(rows):
+    slot = iota((ROWS, VOX), 1) % 8
+    packed = jnp.zeros((ROWS, VOX), F32)
+    for j in range(KT // ROWS):
+        packed = jnp.where(slot == j, rows[j * ROWS : (j + 1) * ROWS, :], packed)
+    return packed
+
+
+def unpack(packed, spread):
+    high = packed.astype(BF16)
+    rest = packed - high.astype(F32)
+    middle = rest.astype(BF16)
+    low = (rest - middle.astype(F32)).astype(BF16)
+    wide = jnp.dot(jnp.concatenate([high, middle, low], axis=0), spread, preferred_element_type=F32)
+    wide = wide[: 2 * ROWS] + wide[2 * ROWS : 4 * ROWS] + wide[4 * ROWS :]
+    slots = KT // ROWS
+    parts = []
+    for kind in range(2):
+        rows = []
+        for d in range(2):
+            for j in range(slots):
+                at = (kind * slots + j) * VOX
+                rows.append(wide[d * ROWS : (d + 1) * ROWS, at : at + VOX])
+        parts.append(jnp.concatenate(rows, axis=0))
+    return parts
+
+
 def even_tile():
     return lax.bitwise_and(lax.axis_index("tile"), 1) == 0
 
@@ -245,13 +273,21 @@
     numer = project(place_ref, tiles_ref, field_ref, sums)
     denom = tiles_ref[TILES * PR : TILES * PR + NH, :]
     value = jnp.where(iota((NH, VOX), 1) % PC < PC // 2, numer, denom)
-    upper, lower = value[:KT, :], value[KT:, :]
+    upper, lower = pack(value[:KT, :]), pack(value[KT:, :])
     even = even_tile()
-    sums_ref[:KT, :] = jnp.where(even, lower, upper)
-    sums_ref[KT:, :] = jnp.where(even, upper, lower)
-
-
-def stage_kernel(spot_ref, image_ref, found_ref, field_ref):
+    sums_ref[:ROWS, :] = jnp.where(even, lower, upper)
+    sums_ref[ROWS:, :] = jnp.where(even, upper, lower)
+
+
+def stage_kernel(spot_ref, image_ref, found_ref, field_ref, spread_ref):
+    source = iota((VOX, VOX), 0)
+    group = source // PC == iota((VOX, VOX), 1) // PC
+    slots = KT // ROWS
+    for kind in range(2):
+        for j in range(slots):
+            at = (kind * slots + j) * VOX
+            pick = group & (source % PC == kind * 8 + j)
+            spread_ref[:, at : at + VOX] = jnp.where(pick, 1.0, 0.0).astype(BF16)
     for d in range(2):
         def body(k, carry):
             spot = spot_ref[d * KT + k]
@@ -291,18 +327,15 @@
 
 
 def lower_kernel(
-    place_ref, packet_ref, tiles_ref, found_ref, old_ref, mine_ref, near_ref, far_ref, cleared_ref,
+    place_ref, packet_ref, tiles_ref, found_ref, old_ref, mine_ref, near_ref, far_ref, spread_ref, cleared_ref,
     trace_ref, field_ref, out_ref, rebuilt,
 ):
     even = even_tile()
-    first_mine, second_mine = mine_ref[:KT, :], mine_ref[KT:, :]
-    near, far = near_ref[...], far_ref[...]
-    upper = jnp.where(even, second_mine + near, first_mine + far)
-    lower = jnp.where(even, first_mine + far, second_mine + near)
-    sums = jnp.concatenate([upper, lower], axis=0)
-    first = iota((NH, VOX), 1) % PC < PC // 2
-    numer = jnp.where(first, sums, pltpu.roll(sums, PC // 2, 1))
-    denom = jnp.where(first, pltpu.roll(sums, VOX - PC // 2, 1), sums)
+    first = mine_ref[:ROWS, :] + far_ref[...]
+    second = mine_ref[ROWS:, :] + near_ref[...]
+    upper = jnp.where(even, second, first)
+    lower = jnp.where(even, first, second)
+    numer, denom = unpack(jnp.concatenate([upper, lower], axis=0), spread_ref[...])
     trace_ref[...] = old_ref[...] * numer / (denom + EPSILON)
     rebuild(place_ref, tiles_ref, trace_ref, field_ref)
     out_ref[...] = renew(1, place_ref, packet_ref, found_ref, field_ref, trace_ref, rebuilt)
@@ -392,7 +425,7 @@
     )(place, upper, packet_in, old)
     tiles_e = in_vmem(tiles_e, pltpu.VMEM)
     image_field, partial = call(
-        numer_kernel, [pltpu.VMEM(((FIELD + PADF) * PR, VOX), F32), shape(NH, F32)],
+        numer_kernel, [pltpu.VMEM(((FIELD + PADF) * PR, VOX), F32), shape(2 * ROWS, F32)],
         [smem(), vmem(), vmem()],
         scratch=[pltpu.VMEM((NF * VOX, NF * VOX), BF16), sums],
         name="numerator", limit=12,
@@ -407,22 +440,26 @@
     partial = partial + lax.ppermute(partial, "nrn", cross)
     near = [(i, i ^ 1) for i in range(tiles)]
     far = [(i, (i - 1 + 2 * (i % 2)) % tiles) for i in range(tiles)]
-    from_far = lax.ppermute(partial[:KT], "tile", far)
-    from_near = lax.ppermute(partial[KT:], "tile", near)
+    from_far = lax.ppermute(partial[:ROWS], "tile", far)
+    from_near = lax.ppermute(partial[ROWS:], "tile", near)
 
     image_field, _ = lax.optimization_barrier((image_field, partial))
-    found, cleared = call(
-        stage_kernel, [pltpu.VMEM((TILES * PR, VOX), F32), pltpu.VMEM((2 * FIELD * PR, VOX), F32)],
+    found, cleared, spread = call(
+        stage_kernel,
+        [
+            pltpu.VMEM((TILES * PR, VOX), F32), pltpu.VMEM((2 * FIELD * PR, VOX), F32),
+            pltpu.VMEM((VOX, 2 * KT // ROWS * VOX), BF16),
+        ],
         [smem(), vmem()], name="stage", limit=4,
     )(spot, in_vmem(image_field, pltpu.VMEM))
-    found, cleared = in_vmem(found, pltpu.VMEM), in_vmem(cleared, pltpu.VMEM)
+    found, cleared, spread = [in_vmem(v, pltpu.VMEM) for v in (found, cleared, spread)]
     half = pltpu.VMEM((NA * KT * PR, VOX), F32)
     new, rebuilt, lower_new = call(
         lower_kernel,
         [shape(NH, F32), pltpu.VMEM((2 * FIELD * PR, VOX), F32), shape(NA * KT, BF16)],
-        [smem()] + [vmem()] * 8,
-        scratch=[half], name="lower", limit=8, aliases={8: 1},
-    )(place, packet_in, tiles_e, found, old, partial, from_near, from_far, cleared)
+        [smem()] + [vmem()] * 9,
+        scratch=[half], name="lower", limit=8, aliases={9: 1},
+    )(place, packet_in, tiles_e, found, old, partial, from_near, from_far, spread, cleared)
     lower_back = lax.ppermute(lower_new, "tile", up)
     lower_other = lax.ppermute(lower_new, everyone, other_core(up))
     upper_new, upper_sent = call(

time: 107 us -> 106 us (level)
  no operation moved by 1% of the time
where the time goes in v4:
time: 106 us
  waiting for transfers between devices  53.6 us (51%)
  Pallas kernels  25.8 us (24%)
  starting transfers between devices  23.1 us (22%)
  between operations  1.42 us (1%)
  local copies, waits for them, and re-layouts  1.12 us (1%)
  other arithmetic  1.1 us (1%)
    all_to_all x1, waiting for transfers between devices, shards(): lax.all_to_all(sent.reshape(tiles * 2, XC, VOX), ('tile', 'nrn'), split_a...  42.9 us
    all_to_all x1, starting transfers between devices, shards(): lax.all_to_all(sent.reshape(tiles * 2, XC, VOX), ('tile', 'nrn'), split_a...  9.74 us
    pallas_call x1, Pallas kernels, shards(): call(numer_kernel, [pltpu.VMEM(((FIELD + PADF) * PR, VOX), F32), shape(2...  5.07 us
    pallas_call x1, Pallas kernels, shards(): call(register_kernel, shape(tiles * 2 * XC, BF16), [smem(), outside], scr...  5.01 us
    ppermute x1, waiting for transfers between devices, shards(): above = lax.ppermute(mine, 'tile', down)  4.89 us
    ppermute x1, waiting for transfers between devices, shards(): from_far = lax.ppermute(partial[:ROWS], 'tile', far)  3.85 us
    pallas_call x1, Pallas kernels, shards(): call(denom_kernel, pltpu.VMEM((TILES * PR + NH, VOX), F32), [smem()] + [v...  3.77 us
    pallas_call x1, Pallas kernels, shards(): call(lower_kernel, [shape(NH, F32), pltpu.VMEM((2 * FIELD * PR, VOX), F32...  3.7 us
  transfers between devices with their start and end apart: 11, of which 6 were waited for; matrix products, arithmetic and copies ran while one was open for 1% of the time, Pallas kernels for 14%

profile of v4, /device:TPU:1, one launch (start us, length us, event | category | flops | bytes accessed | tf_op | source)
XLA Modules:
  0.0 106.2 jit_solution(2543140755246789076)
XLA Ops:
  1.3 1.3 %rows.1 = bf16[480,128]{1,0:T(8,128)(2,1)S(1)} custom-call(s32[1]{0:T(128)S(6)} %copy.14.count_ref, s32[16,96]{1,0:T(8,128)} %bitcast.24, bf16[1536,128]{1,0:T(8,128)(2,1)} %bitcast.19), custom_call_target="tpu_custom_call" | custom-call | tf_op jit(solution)/shard_map/rows/pallas_call | solution.py:381
  2.6 2.1 %collective-permute-start = (bf16[480,128]{1,0:T(8,128)(2,1)S(1)}, bf16[480,128]{1,0:T(8,128)(2,1)S(1)}, u32[]{:S(2)}, u32[]{:S(2)}) collective-permute-start(bf16[480,128]{1,0:T(8,128)(2,1)S(1)} %rows.1), channel_id=1, source_target_pairs={{0,2},{2,4},{4,6},{6,8},{8,10},{10,12},{12,14},{14,16},{16,18},{18... | collective-permute-start | bytes 368648 | tf_op jit(solution)/shard_map/ppermute | solution.py:384
  4.7 1.3 %collective-permute-start.2 = (f32[96,4]{0,1:T(4,128)}, f32[96,4]{0,1:T(4,128)S(1)}, u32[]{:S(2)}, u32[]{:S(2)}) collective-permute-start(f32[96,4]{0,1:T(4,128)} %bitcast.27), channel_id=1, source_target_pairs={{0,1},{1,0},{2,3},{3,2},{4,5},{5,4},{6,7},{7,6},{8,9},{9,8},{10,11... | collective-permute-start | bytes 4616 | tf_op jit(solution)/shard_map/ppermute | solution.py:375
  6.0 0.9 collective-permute-start.1
  6.9 5.0 %register.1 = bf16[8192,128]{1,0:T(8,128)(2,1)} custom-call(s32[2]{0:T(128)} %bitcast.34, bf16[1024,1024]{1,0:T(8,128)(2,1)} %bitcast.18), custom_call_target="tpu_custom_call" | custom-call | tf_op jit(solution)/shard_map/register/pallas_call | solution.py:388
  11.9 0.0 copy-start.2
  11.9 0.0 collective-permute-done.2
  11.9 4.9 %collective-permute-done.1 = f32[96,4]{0,1:T(4,128)S(1)} collective-permute-done((f32[96,4]{0,1:T(4,128)}, f32[96,4]{0,1:T(4,128)S(1)}, u32[]{:S(2)}, u32[]{:S(2)}) %collective-permute-start.1) | collective-permute-done | bytes 1568 | tf_op jit(solution)/shard_map/ppermute | solution.py:374
  16.8 0.0 collective-permute-done.packet_ref
  16.8 9.7 %all-to-all-start = ((bf16[256,32,128]{2,1,0:T(8,128)(2,1)}), bf16[256,32,128]{2,1,0:T(8,128)(2,1)}, u32[]{:S(2)}, u32[]{:S(2)}) async-start(bf16[256,32,128]{2,1,0:T(8,128)(2,1)} %bitcast.10), calls=%async_computation | async-start | bytes 4194304 | tf_op jit(solution)/shard_map/all_to_all | solution.py:397
  26.6 0.2 add_reduce_fusion.1
  26.8 2.3 %collective-permute-start.3 = (f32[96,4]{0,1:T(4,128)S(1)}, f32[96,4]{0,1:T(4,128)S(1)}, u32[]{:S(2)}, u32[]{:S(2)}) collective-permute-start(f32[96,4]{0,1:T(4,128)S(1)} %collective-permute-done.1), channel_id=1, source_target_pairs={{0,1},{1,0},{2,3},{3,2},{4,5},{5,4},{6,7},{7,6},{8,9},{9,8},{10,11... | collective-permute-start | bytes 4616 | tf_op jit(solution)/shard_map/ppermute | solution.py:407
  29.1 0.2 select_reduce_fusion
  29.3 0.1 pad_add_fusion
  29.3 1.9 %own_rows.1 = (bf16[384,128]{1,0:T(8,128)(2,1)}, s32[96,128]{1,0:T(8,128)S(1)}) custom-call(s32[1]{0:T(128)S(6)} %copy.14.count_ref, s32[16,96]{1,0:T(8,128)} %bitcast.25, bf16[1536,128]{1,0:T(8,128)(2,1)} %bitcast.20, bf16[480,128]{1,0:T(8,128)(2,1)S(1)} %collective-permute-done.packet_ref), custom_call_target="tpu_custom_call" | custom-call | tf_op jit(solution)/shard_map/own_rows/pallas_call | solution.py:401
  31.3 0.0 collective-permute-done.3
  31.3 0.0 copy-done.2
  31.3 0.1 fusion.1
  31.4 0.1 copy.10.trace_ref.old_ref
  31.5 0.0 copy-start
  31.5 0.9 copy-done
  32.4 3.8 %denominator.1.tiles_ref = f32[6336,128]{1,0:T(8,128)S(1)} custom-call(s32[192]{0:T(256)S(1)} %get-tuple-element.43.place_ref, bf16[384,128]{1,0:T(8,128)(2,1)S(1)} %copy-done, bf16[480,128]{1,0:T(8,128)(2,1)S(1)} %collective-permute-done.packet_ref, f32[192,128]{1,0:T(8,128)S(1)} %copy.10.trace_ref.old_ref), custom_call_target="tpu_custom_call" | custom-call | tf_op jit(solution)/shard_map/denominator/pallas_call | solution.py:422
  36.2 42.9 %all-to-all-done = bf16[256,32,128]{2,1,0:T(8,128)(2,1)} async-done(((bf16[256,32,128]{2,1,0:T(8,128)(2,1)}), bf16[256,32,128]{2,1,0:T(8,128)(2,1)}, u32[]{:S(2)}, u32[]{:S(2)}) %all-to-all-start) | async-done | bytes 2097184 | tf_op jit(solution)/shard_map/all_to_all | solution.py:397
  79.1 5.1 %numerator.1 = (f32[9216,128]{1,0:T(8,128)S(1)}, f32[32,128]{1,0:T(8,128)S(1)}) custom-call(s32[192]{0:T(256)S(1)} %get-tuple-element.42.place_ref.spot_ref, f32[6336,128]{1,0:T(8,128)S(1)} %denominator.1.tiles_ref, bf16[8192,128]{1,0:T(8,128)(2,1)} %bitcast.11.image_ref), custom_call_target="tpu_custom_call" | custom-call | tf_op jit(solution)/shard_map/numerator/pallas_call | solution.py:427
  84.2 0.9 collective-permute-start.4
  85.1 0.8 collective-permute-done.4
  85.9 1.4 %collective-permute-start.6 = (f32[16,128]{1,0:T(8,128)S(1)}, f32[16,128]{1,0:T(8,128)S(1)}, u32[]{:S(2)}, u32[]{:S(2)}) collective-permute-start(f32[16,128]{1,0:T(8,128)S(1)} %get-tuple-element.38), channel_id=1, source_target_pairs={{0,254},{2,4},{4,2},{6,8},{8,6},{10,12},{12,10},{14,16},{16,14},{1... | collective-permute-start | bytes 24584 | tf_op jit(solution)/shard_map/ppermute | solution.py:443
  87.3 0.7 collective-permute-start.5
  88.0 2.0 %stage.1 = (f32[6144,128]{1,0:T(8,128)S(1)}, f32[16384,128]{1,0:T(8,128)S(1)}, bf16[128,1536]{1,0:T(8,128)(2,1)S(1)}) custom-call(s32[192]{0:T(256)S(1)} %get-tuple-element.42.place_ref.spot_ref, f32[9216,128]{1,0:T(8,128)S(1)} %get-tuple-element.26.image_ref), custom_call_target="tpu_custom_call" | custom-call | tf_op jit(solution)/shard_map/stage/pallas_call | solution.py:447
  90.0 3.9 %collective-permute-done.6.far_ref = f32[16,128]{1,0:T(8,128)S(1)} collective-permute-done((f32[16,128]{1,0:T(8,128)S(1)}, f32[16,128]{1,0:T(8,128)S(1)}, u32[]{:S(2)}, u32[]{:S(2)}) %collective-permute-start.6) | collective-permute-done | bytes 8224 | tf_op jit(solution)/shard_map/ppermute | solution.py:443
  93.9 0.0 collective-permute-done.5.near_ref
  93.9 0.0 copy-start.1
  93.9 3.7 %lower.1 = (f32[192,128]{1,0:T(8,128)S(1)}, f32[16384,128]{1,0:T(8,128)S(1)}, bf16[384,128]{1,0:T(8,128)(2,1)}) custom-call(s32[192]{0:T(256)S(1)} %get-tuple-element.43.place_ref, bf16[480,128]{1,0:T(8,128)(2,1)S(1)} %collective-permute-done.packet_ref, f32[6336,128]{1,0:T(8,128)S(1)} %denominator.1.tiles_ref, ...), custom_call_target="tpu_custom_call", output_to_operand_aliasing={{1}: (9, {})} | custom-call | tf_op jit(solution)/shard_map/lower/pallas_call | solution.py:457
  97.6 3.2 %collective-permute-start.9 = (bf16[384,128]{1,0:T(8,128)(2,1)}, bf16[384,128]{1,0:T(8,128)(2,1)S(1)}, u32[]{:S(2)}, u32[]{:S(2)}) collective-permute-start(bf16[384,128]{1,0:T(8,128)(2,1)} %get-tuple-element.34), channel_id=1, source_target_pairs={{2,1},{3,0},{4,3},{5,2},{6,5},{7,4},{8,7},{9,6},{10,9},{11,8},{12,... | collective-permute-start | bytes 294920 | tf_op jit(solution)/shard_map/ppermute | solution.py:464
  100.8 0.0 collective-permute-start.7
  100.8 0.0 copy-done.1
  100.8 1.9 %upper.1 = (bf16[384,128]{1,0:T(8,128)(2,1)S(1)}, bf16[384,128]{1,0:T(8,128)(2,1)S(1)}) custom-call(s32[192]{0:T(256)S(1)} %get-tuple-element.43.place_ref, bf16[384,128]{1,0:T(8,128)(2,1)S(1)} %copy-done.1, f32[6144,128]{1,0:T(8,128)S(1)} %get-tuple-element.27.found_ref, f32[16384,128]{1,0:T(8,128)S(1)} %get-tuple-element.32.field_ref, ...), custom_call_target="tpu_custom_call" | custom-call | tf_op jit(solution)/shard_map/upper/pallas_call | solution.py:465
  102.7 0.1 copy.12
  102.8 0.5 collective-permute-start.8
  103.3 0.6 broadcast_select_fusion
  103.9 0.4 collective-permute-done.8.upper_other
  104.2 0.0 collective-permute-done.9.lower_other
  104.2 0.7 collective-permute-done.7.lower_ref
  105.0 1.2 %merge.1 = bf16[1536,128]{1,0:T(8,128)(2,1)} custom-call(s32[96,128]{1,0:T(8,128)S(1)} %get-tuple-element.31.odd_ref, bf16[384,128]{1,0:T(8,128)(2,1)S(1)} %get-tuple-element.33.upper_ref, bf16[384,128]{1,0:T(8,128)(2,1)S(1)} %collective-permute-done.7.lower_ref, bf16[384,128]{1,0:T(8,128)(2,1)S(1)} %collective-permute-done.8.upper_other, ...), custom_call_target="tpu_custom_call" | custom-call | tf_op jit(solution)/shard_map/merge/pallas_call | solution.py:470
  (8 shorter events, 0.1 us)
Async XLA Ops:
  2.6 14.2 %collective-permute-start = (bf16[480,128]{1,0:T(8,128)(2,1)S(1)}, bf16[480,128]{1,0:T(8,128)(2,1)S(1)}, u32[]{:S(2)}, u32[]{:S(2)}) collective-permute-start(bf16[480,128]{1,0:T(8,128)(2,1)S(1)} %rows.1), channel_id=1, source_target_pairs={{0,2},{2,4},{4,6},{6,8},{8,10},{10,12},{12,14},{14,16},{16,18},{18... | collective-permute-start | bytes 368648 | tf_op jit(solution)/shard_map/ppermute | solution.py:384
  4.7 7.2 %collective-permute-start.2 = (f32[96,4]{0,1:T(4,128)}, f32[96,4]{0,1:T(4,128)S(1)}, u32[]{:S(2)}, u32[]{:S(2)}) collective-permute-start(f32[96,4]{0,1:T(4,128)} %bitcast.27), channel_id=1, source_target_pairs={{0,1},{1,0},{2,3},{3,2},{4,5},{5,4},{6,7},{7,6},{8,9},{9,8},{10,11... | collective-permute-start | bytes 4616 | tf_op jit(solution)/shard_map/ppermute | solution.py:375
  6.0 10.8 %collective-permute-start.1 = (f32[96,4]{0,1:T(4,128)}, f32[96,4]{0,1:T(4,128)S(1)}, u32[]{:S(2)}, u32[]{:S(2)}) collective-permute-start(f32[96,4]{0,1:T(4,128)} %bitcast.28), channel_id=1, source_target_pairs={{0,2},{2,4},{4,6},{6,8},{8,10},{10,12},{12,14},{14,16},{16,18},{18... | collective-permute-start | bytes 4616 | tf_op jit(solution)/shard_map/ppermute | solution.py:374
  11.9 19.4 %copy-start.2 = (f32[1,96,4]{1,2,0:T(4,128)S(1)}, f32[1,96,4]{1,2,0:T(4,128)}, u32[]{:S(2)}) copy-start(f32[1,96,4]{1,2,0:T(4,128)} %param.10) | copy-start | bytes 4612
  16.8 62.3 %all-to-all-start = ((bf16[256,32,128]{2,1,0:T(8,128)(2,1)}), bf16[256,32,128]{2,1,0:T(8,128)(2,1)}, u32[]{:S(2)}, u32[]{:S(2)}) async-start(bf16[256,32,128]{2,1,0:T(8,128)(2,1)} %bitcast.10), calls=%async_computation | async-start | bytes 4194304 | tf_op jit(solution)/shard_map/all_to_all | solution.py:397
  26.8 4.5 %collective-permute-start.3 = (f32[96,4]{0,1:T(4,128)S(1)}, f32[96,4]{0,1:T(4,128)S(1)}, u32[]{:S(2)}, u32[]{:S(2)}) collective-permute-start(f32[96,4]{0,1:T(4,128)S(1)} %collective-permute-done.1), channel_id=1, source_target_pairs={{0,1},{1,0},{2,3},{3,2},{4,5},{5,4},{6,7},{7,6},{8,9},{9,8},{10,11... | collective-permute-start | bytes 4616 | tf_op jit(solution)/shard_map/ppermute | solution.py:407
  31.5 0.9 copy-start
  84.2 1.8 %collective-permute-start.4 = (f32[32,128]{1,0:T(8,128)S(1)}, f32[32,128]{1,0:T(8,128)S(1)}, u32[]{:S(2)}, u32[]{:S(2)}) collective-permute-start(f32[32,128]{1,0:T(8,128)S(1)} %get-tuple-element.25), channel_id=1, source_target_pairs={{0,1},{1,0},{2,3},{3,2},{4,5},{5,4},{6,7},{7,6},{8,9},{9,8},{10,11... | collective-permute-start | bytes 49160 | tf_op jit(solution)/shard_map/ppermute | solution.py:440
  85.9 7.9 %collective-permute-start.6 = (f32[16,128]{1,0:T(8,128)S(1)}, f32[16,128]{1,0:T(8,128)S(1)}, u32[]{:S(2)}, u32[]{:S(2)}) collective-permute-start(f32[16,128]{1,0:T(8,128)S(1)} %get-tuple-element.38), channel_id=1, source_target_pairs={{0,254},{2,4},{4,2},{6,8},{8,6},{10,12},{12,10},{14,16},{16,14},{1... | collective-permute-start | bytes 24584 | tf_op jit(solution)/shard_map/ppermute | solution.py:443
  87.3 6.5 %collective-permute-start.5 = (f32[16,128]{1,0:T(8,128)S(1)}, f32[16,128]{1,0:T(8,128)S(1)}, u32[]{:S(2)}, u32[]{:S(2)}) collective-permute-start(f32[16,128]{1,0:T(8,128)S(1)} %get-tuple-element.39), channel_id=1, source_target_pairs={{0,2},{2,0},{4,6},{6,4},{8,10},{10,8},{12,14},{14,12},{16,18},{18,... | collective-permute-start | bytes 24584 | tf_op jit(solution)/shard_map/ppermute | solution.py:444
  93.9 6.9 %copy-start.1 = (bf16[384,128]{1,0:T(8,128)(2,1)S(1)}, bf16[384,128]{1,0:T(8,128)(2,1)}, u32[]{:S(2)}) copy-start(bf16[384,128]{1,0:T(8,128)(2,1)} %get-tuple-element.20.upper_ref) | copy-start | bytes 294916
  97.6 6.7 %collective-permute-start.9 = (bf16[384,128]{1,0:T(8,128)(2,1)}, bf16[384,128]{1,0:T(8,128)(2,1)S(1)}, u32[]{:S(2)}, u32[]{:S(2)}) collective-permute-start(bf16[384,128]{1,0:T(8,128)(2,1)} %get-tuple-element.34), channel_id=1, source_target_pairs={{2,1},{3,0},{4,3},{5,2},{6,5},{7,4},{8,7},{9,6},{10,9},{11,8},{12,... | collective-permute-start | bytes 294920 | tf_op jit(solution)/shard_map/ppermute | solution.py:464
  100.8 4.2 %collective-permute-start.7 = (bf16[384,128]{1,0:T(8,128)(2,1)}, bf16[384,128]{1,0:T(8,128)(2,1)S(1)}, u32[]{:S(2)}, u32[]{:S(2)}) collective-permute-start(bf16[384,128]{1,0:T(8,128)(2,1)} %get-tuple-element.34), channel_id=1, source_target_pairs={{2,0},{4,2},{6,4},{8,6},{10,8},{12,10},{14,12},{16,14},{18,16},{20... | collective-permute-start | bytes 294920 | tf_op jit(solution)/shard_map/ppermute | solution.py:463
  102.8 1.5 %collective-permute-start.8 = (bf16[384,128]{1,0:T(8,128)(2,1)S(1)}, bf16[384,128]{1,0:T(8,128)(2,1)S(1)}, u32[]{:S(2)}, u32[]{:S(2)}) collective-permute-start(bf16[384,128]{1,0:T(8,128)(2,1)S(1)} %get-tuple-element.35), channel_id=1, source_target_pairs={{0,1},{1,0},{2,3},{3,2},{4,5},{5,4},{6,7},{7,6},{8,9},{9,8},{10,11... | collective-permute-start | bytes 294920 | tf_op jit(solution)/shard_map/ppermute | solution.py:469

commit v5 on v4

--- a/solution.py
+++ b/solution.py
@@ -432,11 +432,6 @@
     )(spot, tiles_e, in_vmem(images, pltpu.VMEM))
     image_field = in_vmem(image_field, pltpu.VMEM)
 
-    everyone = ("tile", "nrn")
-
-    def other_core(pairs):
-        return [(2 * i + c, 2 * j + 1 - c) for i, j in pairs for c in (0, 1)]
-
     partial = partial + lax.ppermute(partial, "nrn", cross)
     near = [(i, i ^ 1) for i in range(tiles)]
     far = [(i, (i - 1 + 2 * (i % 2)) % tiles) for i in range(tiles)]
@@ -461,12 +456,12 @@
         scratch=[half], name="lower", limit=8, aliases={9: 1},
     )(place, packet_in, tiles_e, found, old, partial, from_near, from_far, spread, cleared)
     lower_back = lax.ppermute(lower_new, "tile", up)
-    lower_other = lax.ppermute(lower_new, everyone, other_core(up))
     upper_new, upper_sent = call(
         upper_kernel, [shape(NA * KT, BF16)] * 2, [smem()] + [vmem()] * 4,
         scratch=[half], name="upper", limit=8,
     )(place, upper, found, in_vmem(rebuilt, pltpu.VMEM), new)
     upper_other = lax.ppermute(upper_sent, "nrn", cross)
+    lower_other = lax.ppermute(lower_back, "nrn", cross)
     merged = call(
         merge_kernel, shape(KT * 16, BF16), [vmem()] * 5,
         scratch=[pltpu.VMEM((KT * 16, VOX), F32)], name="merge", limit=4,

time: 106 us -> 106 us (level)
    ppermute x1, starting transfers between devices: 3.21 us -> 0.71 us  [shards(): lower_other = lax.ppermute(lower_back, 'nrn', cross)]
    ppermute x1, starting transfers between devices: 0.01 us -> 1.76 us  [shards(): lower_back = lax.ppermute(lower_new, 'tile', up)]
    ppermute x1, starting transfers between devices: 0.51 us -> 1.93 us  [shards(): upper_other = lax.ppermute(upper_sent, 'nrn', cross)]
  transfers between devices with their start and end apart: 11 -> 11, of which waited for: 6 -> 5; matrix products, arithmetic and copies ran while one was open for 1% -> 1% of each run, Pallas kernels for 14% -> 14%
where the time goes in v5:
time: 106 us
  waiting for transfers between devices  52.9 us (50%)
  Pallas kernels  25.8 us (24%)
  starting transfers between devices  23.8 us (22%)
  between operations  1.42 us (1%)
  local copies, waits for them, and re-layouts  1.12 us (1%)
  other arithmetic  1.1 us (1%)
    all_to_all x1, waiting for transfers between devices, shards(): lax.all_to_all(sent.reshape(tiles * 2, XC, VOX), ('tile', 'nrn'), split_a...  42.9 us
    all_to_all x1, starting transfers between devices, shards(): lax.all_to_all(sent.reshape(tiles * 2, XC, VOX), ('tile', 'nrn'), split_a...  9.74 us
    pallas_call x1, Pallas kernels, shards(): call(numer_kernel, [pltpu.VMEM(((FIELD + PADF) * PR, VOX), F32), shape(2...  5.06 us
    pallas_call x1, Pallas kernels, shards(): call(register_kernel, shape(tiles * 2 * XC, BF16), [smem(), outside], scr...  5.01 us
    ppermute x1, waiting for transfers between devices, shards(): above = lax.ppermute(mine, 'tile', down)  4.89 us
    ppermute x1, waiting for transfers between devices, shards(): from_far = lax.ppermute(partial[:ROWS], 'tile', far)  3.84 us
    pallas_call x1, Pallas kernels, shards(): call(denom_kernel, pltpu.VMEM((TILES * PR + NH, VOX), F32), [smem()] + [v...  3.76 us
    pallas_call x1, Pallas kernels, shards(): call(lower_kernel, [shape(NH, F32), pltpu.VMEM((2 * FIELD * PR, VOX), F32...  3.69 us
  transfers between devices with their start and end apart: 11, of which 5 were waited for; matrix products, arithmetic and copies ran while one was open for 1% of the time, Pallas kernels for 14%

profile of v5, /device:TPU:1, one launch (start us, length us, event | category | flops | bytes accessed | tf_op | source)
XLA Modules:
  0.0 106.1 jit_solution(13113489841553423878)
XLA Ops:
  1.3 1.3 %rows.1 = bf16[480,128]{1,0:T(8,128)(2,1)S(1)} custom-call(s32[1]{0:T(128)S(6)} %copy.14.count_ref, s32[16,96]{1,0:T(8,128)} %bitcast.24, bf16[1536,128]{1,0:T(8,128)(2,1)} %bitcast.19), custom_call_target="tpu_custom_call" | custom-call | tf_op jit(solution)/shard_map/rows/pallas_call | solution.py:381
  2.6 2.1 %collective-permute-start = (bf16[480,128]{1,0:T(8,128)(2,1)S(1)}, bf16[480,128]{1,0:T(8,128)(2,1)S(1)}, u32[]{:S(2)}, u32[]{:S(2)}) collective-permute-start(bf16[480,128]{1,0:T(8,128)(2,1)S(1)} %rows.1), channel_id=1, source_target_pairs={{0,2},{2,4},{4,6},{6,8},{8,10},{10,12},{12,14},{14,16},{16,18},{18... | collective-permute-start | bytes 368648 | tf_op jit(solution)/shard_map/ppermute | solution.py:384
  4.7 1.3 %collective-permute-start.2 = (f32[96,4]{0,1:T(4,128)}, f32[96,4]{0,1:T(4,128)S(1)}, u32[]{:S(2)}, u32[]{:S(2)}) collective-permute-start(f32[96,4]{0,1:T(4,128)} %bitcast.27), channel_id=1, source_target_pairs={{0,1},{1,0},{2,3},{3,2},{4,5},{5,4},{6,7},{7,6},{8,9},{9,8},{10,11... | collective-permute-start | bytes 4616 | tf_op jit(solution)/shard_map/ppermute | solution.py:375
  6.0 0.9 collective-permute-start.1
  6.9 5.0 %register.1 = bf16[8192,128]{1,0:T(8,128)(2,1)} custom-call(s32[2]{0:T(128)} %bitcast.34, bf16[1024,1024]{1,0:T(8,128)(2,1)} %bitcast.18), custom_call_target="tpu_custom_call" | custom-call | tf_op jit(solution)/shard_map/register/pallas_call | solution.py:388
  11.9 0.0 copy-start.2
  11.9 0.0 collective-permute-done.2
  11.9 4.9 %collective-permute-done.1 = f32[96,4]{0,1:T(4,128)S(1)} collective-permute-done((f32[96,4]{0,1:T(4,128)}, f32[96,4]{0,1:T(4,128)S(1)}, u32[]{:S(2)}, u32[]{:S(2)}) %collective-permute-start.1) | collective-permute-done | bytes 1568 | tf_op jit(solution)/shard_map/ppermute | solution.py:374
  16.8 0.0 collective-permute-done.packet_ref
  16.8 9.7 %all-to-all-start = ((bf16[256,32,128]{2,1,0:T(8,128)(2,1)}), bf16[256,32,128]{2,1,0:T(8,128)(2,1)}, u32[]{:S(2)}, u32[]{:S(2)}) async-start(bf16[256,32,128]{2,1,0:T(8,128)(2,1)} %bitcast.10), calls=%async_computation | async-start | bytes 4194304 | tf_op jit(solution)/shard_map/all_to_all | solution.py:397
  26.6 0.2 add_reduce_fusion.1
  26.8 2.3 %collective-permute-start.3 = (f32[96,4]{0,1:T(4,128)S(1)}, f32[96,4]{0,1:T(4,128)S(1)}, u32[]{:S(2)}, u32[]{:S(2)}) collective-permute-start(f32[96,4]{0,1:T(4,128)S(1)} %collective-permute-done.1), channel_id=1, source_target_pairs={{0,1},{1,0},{2,3},{3,2},{4,5},{5,4},{6,7},{7,6},{8,9},{9,8},{10,11... | collective-permute-start | bytes 4616 | tf_op jit(solution)/shard_map/ppermute | solution.py:407
  29.1 0.2 select_reduce_fusion
  29.3 0.1 pad_add_fusion
  29.3 1.9 %own_rows.1 = (bf16[384,128]{1,0:T(8,128)(2,1)}, s32[96,128]{1,0:T(8,128)S(1)}) custom-call(s32[1]{0:T(128)S(6)} %copy.14.count_ref, s32[16,96]{1,0:T(8,128)} %bitcast.25, bf16[1536,128]{1,0:T(8,128)(2,1)} %bitcast.20, bf16[480,128]{1,0:T(8,128)(2,1)S(1)} %collective-permute-done.packet_ref), custom_call_target="tpu_custom_call" | custom-call | tf_op jit(solution)/shard_map/own_rows/pallas_call | solution.py:401
  31.3 0.0 collective-permute-done.3
  31.3 0.0 copy-done.2
  31.3 0.1 fusion.1
  31.4 0.1 copy.10.trace_ref.old_ref
  31.5 0.0 copy-start
  31.5 0.9 copy-done
  32.4 3.8 %denominator.1.tiles_ref = f32[6336,128]{1,0:T(8,128)S(1)} custom-call(s32[192]{0:T(256)S(1)} %get-tuple-element.43.place_ref, bf16[384,128]{1,0:T(8,128)(2,1)S(1)} %copy-done, bf16[480,128]{1,0:T(8,128)(2,1)S(1)} %collective-permute-done.packet_ref, f32[192,128]{1,0:T(8,128)S(1)} %copy.10.trace_ref.old_ref), custom_call_target="tpu_custom_call" | custom-call | tf_op jit(solution)/shard_map/denominator/pallas_call | solution.py:422
  36.2 42.9 %all-to-all-done = bf16[256,32,128]{2,1,0:T(8,128)(2,1)} async-done(((bf16[256,32,128]{2,1,0:T(8,128)(2,1)}), bf16[256,32,128]{2,1,0:T(8,128)(2,1)}, u32[]{:S(2)}, u32[]{:S(2)}) %all-to-all-start) | async-done | bytes 2097184 | tf_op jit(solution)/shard_map/all_to_all | solution.py:397
  79.1 5.1 %numerator.1 = (f32[9216,128]{1,0:T(8,128)S(1)}, f32[32,128]{1,0:T(8,128)S(1)}) custom-call(s32[192]{0:T(256)S(1)} %get-tuple-element.42.place_ref.spot_ref, f32[6336,128]{1,0:T(8,128)S(1)} %denominator.1.tiles_ref, bf16[8192,128]{1,0:T(8,128)(2,1)} %bitcast.11.image_ref), custom_call_target="tpu_custom_call" | custom-call | tf_op jit(solution)/shard_map/numerator/pallas_call | solution.py:427
  84.2 0.9 collective-permute-start.4
  85.1 0.8 collective-permute-done.4
  85.9 1.4 %collective-permute-start.6 = (f32[16,128]{1,0:T(8,128)S(1)}, f32[16,128]{1,0:T(8,128)S(1)}, u32[]{:S(2)}, u32[]{:S(2)}) collective-permute-start(f32[16,128]{1,0:T(8,128)S(1)} %get-tuple-element.38), channel_id=1, source_target_pairs={{0,254},{2,4},{4,2},{6,8},{8,6},{10,12},{12,10},{14,16},{16,14},{1... | collective-permute-start | bytes 24584 | tf_op jit(solution)/shard_map/ppermute | solution.py:438
  87.3 0.7 collective-permute-start.5
  88.0 2.0 %stage.1 = (f32[6144,128]{1,0:T(8,128)S(1)}, f32[16384,128]{1,0:T(8,128)S(1)}, bf16[128,1536]{1,0:T(8,128)(2,1)S(1)}) custom-call(s32[192]{0:T(256)S(1)} %get-tuple-element.42.place_ref.spot_ref, f32[9216,128]{1,0:T(8,128)S(1)} %get-tuple-element.26.image_ref), custom_call_target="tpu_custom_call" | custom-call | tf_op jit(solution)/shard_map/stage/pallas_call | solution.py:442
  90.0 3.8 %collective-permute-done.6.far_ref = f32[16,128]{1,0:T(8,128)S(1)} collective-permute-done((f32[16,128]{1,0:T(8,128)S(1)}, f32[16,128]{1,0:T(8,128)S(1)}, u32[]{:S(2)}, u32[]{:S(2)}) %collective-permute-start.6) | collective-permute-done | bytes 8224 | tf_op jit(solution)/shard_map/ppermute | solution.py:438
  93.9 0.0 collective-permute-done.5.near_ref
  93.9 0.0 copy-start.1
  93.9 3.7 %lower.1 = (f32[192,128]{1,0:T(8,128)S(1)}, f32[16384,128]{1,0:T(8,128)S(1)}, bf16[384,128]{1,0:T(8,128)(2,1)}) custom-call(s32[192]{0:T(256)S(1)} %get-tuple-element.43.place_ref, bf16[480,128]{1,0:T(8,128)(2,1)S(1)} %collective-permute-done.packet_ref, f32[6336,128]{1,0:T(8,128)S(1)} %denominator.1.tiles_ref, ...), custom_call_target="tpu_custom_call", output_to_operand_aliasing={{1}: (9, {})} | custom-call | tf_op jit(solution)/shard_map/lower/pallas_call | solution.py:452
  97.6 1.8 %collective-permute-start.7 = (bf16[384,128]{1,0:T(8,128)(2,1)}, bf16[384,128]{1,0:T(8,128)(2,1)S(1)}, u32[]{:S(2)}, u32[]{:S(2)}) collective-permute-start(bf16[384,128]{1,0:T(8,128)(2,1)} %get-tuple-element.34), channel_id=1, source_target_pairs={{2,0},{4,2},{6,4},{8,6},{10,8},{12,10},{14,12},{16,14},{18,16},{20... | collective-permute-start | bytes 294920 | tf_op jit(solution)/shard_map/ppermute | solution.py:458
  99.3 0.0 copy-done.1
  99.3 1.9 %upper.1 = (bf16[384,128]{1,0:T(8,128)(2,1)S(1)}, bf16[384,128]{1,0:T(8,128)(2,1)S(1)}) custom-call(s32[192]{0:T(256)S(1)} %get-tuple-element.43.place_ref, bf16[384,128]{1,0:T(8,128)(2,1)S(1)} %copy-done.1, f32[6144,128]{1,0:T(8,128)S(1)} %get-tuple-element.27.found_ref, f32[16384,128]{1,0:T(8,128)S(1)} %get-tuple-element.32.field_ref, ...), custom_call_target="tpu_custom_call" | custom-call | tf_op jit(solution)/shard_map/upper/pallas_call | solution.py:459
  101.2 0.1 copy.12
  101.3 1.9 %collective-permute-start.8 = (bf16[384,128]{1,0:T(8,128)(2,1)S(1)}, bf16[384,128]{1,0:T(8,128)(2,1)S(1)}, u32[]{:S(2)}, u32[]{:S(2)}) collective-permute-start(bf16[384,128]{1,0:T(8,128)(2,1)S(1)} %get-tuple-element.35), channel_id=1, source_target_pairs={{0,1},{1,0},{2,3},{3,2},{4,5},{5,4},{6,7},{7,6},{8,9},{9,8},{10,11... | collective-permute-start | bytes 294920 | tf_op jit(solution)/shard_map/ppermute | solution.py:463
  103.3 0.0 collective-permute-done.7.lower_ref
  103.3 0.7 collective-permute-start.9
  104.0 0.6 broadcast_select_fusion
  104.6 0.0 collective-permute-done.8.upper_other
  104.6 0.4 collective-permute-done.9.lower_other
  104.9 1.2 %merge.1 = bf16[1536,128]{1,0:T(8,128)(2,1)} custom-call(s32[96,128]{1,0:T(8,128)S(1)} %get-tuple-element.31.odd_ref, bf16[384,128]{1,0:T(8,128)(2,1)S(1)} %get-tuple-element.33.upper_ref, bf16[384,128]{1,0:T(8,128)(2,1)S(1)} %collective-permute-done.7.lower_ref, bf16[384,128]{1,0:T(8,128)(2,1)S(1)} %collective-permute-done.8.upper_other, ...), custom_call_target="tpu_custom_call" | custom-call | tf_op jit(solution)/shard_map/merge/pallas_call | solution.py:465
  (8 shorter events, 0.1 us)
Async XLA Ops:
  2.6 14.2 %collective-permute-start = (bf16[480,128]{1,0:T(8,128)(2,1)S(1)}, bf16[480,128]{1,0:T(8,128)(2,1)S(1)}, u32[]{:S(2)}, u32[]{:S(2)}) collective-permute-start(bf16[480,128]{1,0:T(8,128)(2,1)S(1)} %rows.1), channel_id=1, source_target_pairs={{0,2},{2,4},{4,6},{6,8},{8,10},{10,12},{12,14},{14,16},{16,18},{18... | collective-permute-start | bytes 368648 | tf_op jit(solution)/shard_map/ppermute | solution.py:384
  4.7 7.2 %collective-permute-start.2 = (f32[96,4]{0,1:T(4,128)}, f32[96,4]{0,1:T(4,128)S(1)}, u32[]{:S(2)}, u32[]{:S(2)}) collective-permute-start(f32[96,4]{0,1:T(4,128)} %bitcast.27), channel_id=1, source_target_pairs={{0,1},{1,0},{2,3},{3,2},{4,5},{5,4},{6,7},{7,6},{8,9},{9,8},{10,11... | collective-permute-start | bytes 4616 | tf_op jit(solution)/shard_map/ppermute | solution.py:375
  6.0 10.8 %collective-permute-start.1 = (f32[96,4]{0,1:T(4,128)}, f32[96,4]{0,1:T(4,128)S(1)}, u32[]{:S(2)}, u32[]{:S(2)}) collective-permute-start(f32[96,4]{0,1:T(4,128)} %bitcast.28), channel_id=1, source_target_pairs={{0,2},{2,4},{4,6},{6,8},{8,10},{10,12},{12,14},{14,16},{16,18},{18... | collective-permute-start | bytes 4616 | tf_op jit(solution)/shard_map/ppermute | solution.py:374
  11.9 19.4 %copy-start.2 = (f32[1,96,4]{1,2,0:T(4,128)S(1)}, f32[1,96,4]{1,2,0:T(4,128)}, u32[]{:S(2)}) copy-start(f32[1,96,4]{1,2,0:T(4,128)} %param.10) | copy-start | bytes 4612
  16.8 62.3 %all-to-all-start = ((bf16[256,32,128]{2,1,0:T(8,128)(2,1)}), bf16[256,32,128]{2,1,0:T(8,128)(2,1)}, u32[]{:S(2)}, u32[]{:S(2)}) async-start(bf16[256,32,128]{2,1,0:T(8,128)(2,1)} %bitcast.10), calls=%async_computation | async-start | bytes 4194304 | tf_op jit(solution)/shard_map/all_to_all | solution.py:397
  26.8 4.5 %collective-permute-start.3 = (f32[96,4]{0,1:T(4,128)S(1)}, f32[96,4]{0,1:T(4,128)S(1)}, u32[]{:S(2)}, u32[]{:S(2)}) collective-permute-start(f32[96,4]{0,1:T(4,128)S(1)} %collective-permute-done.1), channel_id=1, source_target_pairs={{0,1},{1,0},{2,3},{3,2},{4,5},{5,4},{6,7},{7,6},{8,9},{9,8},{10,11... | collective-permute-start | bytes 4616 | tf_op jit(solution)/shard_map/ppermute | solution.py:407
  31.5 0.9 copy-start
  84.2 1.8 %collective-permute-start.4 = (f32[32,128]{1,0:T(8,128)S(1)}, f32[32,128]{1,0:T(8,128)S(1)}, u32[]{:S(2)}, u32[]{:S(2)}) collective-permute-start(f32[32,128]{1,0:T(8,128)S(1)} %get-tuple-element.25), channel_id=1, source_target_pairs={{0,1},{1,0},{2,3},{3,2},{4,5},{5,4},{6,7},{7,6},{8,9},{9,8},{10,11... | collective-permute-start | bytes 49160 | tf_op jit(solution)/shard_map/ppermute | solution.py:435
  85.9 7.9 %collective-permute-start.6 = (f32[16,128]{1,0:T(8,128)S(1)}, f32[16,128]{1,0:T(8,128)S(1)}, u32[]{:S(2)}, u32[]{:S(2)}) collective-permute-start(f32[16,128]{1,0:T(8,128)S(1)} %get-tuple-element.38), channel_id=1, source_target_pairs={{0,254},{2,4},{4,2},{6,8},{8,6},{10,12},{12,10},{14,16},{16,14},{1... | collective-permute-start | bytes 24584 | tf_op jit(solution)/shard_map/ppermute | solution.py:438
  87.3 6.6 %collective-permute-start.5 = (f32[16,128]{1,0:T(8,128)S(1)}, f32[16,128]{1,0:T(8,128)S(1)}, u32[]{:S(2)}, u32[]{:S(2)}) collective-permute-start(f32[16,128]{1,0:T(8,128)S(1)} %get-tuple-element.39), channel_id=1, source_target_pairs={{0,2},{2,0},{4,6},{6,4},{8,10},{10,8},{12,14},{14,12},{16,18},{18,... | collective-permute-start | bytes 24584 | tf_op jit(solution)/shard_map/ppermute | solution.py:439
  93.9 5.5 %copy-start.1 = (bf16[384,128]{1,0:T(8,128)(2,1)S(1)}, bf16[384,128]{1,0:T(8,128)(2,1)}, u32[]{:S(2)}) copy-start(bf16[384,128]{1,0:T(8,128)(2,1)} %get-tuple-element.20.upper_ref) | copy-start | bytes 294916
  97.6 5.7 %collective-permute-start.7 = (bf16[384,128]{1,0:T(8,128)(2,1)}, bf16[384,128]{1,0:T(8,128)(2,1)S(1)}, u32[]{:S(2)}, u32[]{:S(2)}) collective-permute-start(bf16[384,128]{1,0:T(8,128)(2,1)} %get-tuple-element.34), channel_id=1, source_target_pairs={{2,0},{4,2},{6,4},{8,6},{10,8},{12,10},{14,12},{16,14},{18,16},{20... | collective-permute-start | bytes 294920 | tf_op jit(solution)/shard_map/ppermute | solution.py:458
  101.3 3.2 %collective-permute-start.8 = (bf16[384,128]{1,0:T(8,128)(2,1)S(1)}, bf16[384,128]{1,0:T(8,128)(2,1)S(1)}, u32[]{:S(2)}, u32[]{:S(2)}) collective-permute-start(bf16[384,128]{1,0:T(8,128)(2,1)S(1)} %get-tuple-element.35), channel_id=1, source_target_pairs={{0,1},{1,0},{2,3},{3,2},{4,5},{5,4},{6,7},{7,6},{8,9},{9,8},{10,11... | collective-permute-start | bytes 294920 | tf_op jit(solution)/shard_map/ppermute | solution.py:463
  103.3 1.7 %collective-permute-start.9 = (bf16[384,128]{1,0:T(8,128)(2,1)S(1)}, bf16[384,128]{1,0:T(8,128)(2,1)S(1)}, u32[]{:S(2)}, u32[]{:S(2)}) collective-permute-start(bf16[384,128]{1,0:T(8,128)(2,1)S(1)} %collective-permute-done.7.lower_ref), channel_id=1, source_target_pairs={{0,1},{1,0},{2,3},{3,2},{4,5},{5,4},{6,7},{7,6},{8,9},{9,8},{10,11... | collective-permute-start | bytes 294920 | tf_op jit(solution)/shard_map/ppermute | solution.py:464

commit v6 on v4

--- a/solution.py
+++ b/solution.py
@@ -181,7 +181,7 @@
             tile_at(field_ref, base + a * XC)[...] = held[a] + added[a]
         return carry
 
-    lax.fori_loop(0, NH, body, 0, unroll=8)
+    lax.fori_loop(0, NH, body, 0, unroll=16)
 
 
 def project(place_ref, tiles_ref, field_ref, sums_ref):
@@ -193,7 +193,7 @@
         tile_at(sums_ref, n)[...] = total
         return carry
 
-    lax.fori_loop(0, NH, body, 0, unroll=8)
+    lax.fori_loop(0, NH, body, 0, unroll=16)
     rows = sums_ref[pl.ds(0, NH, stride=PR), :]
     for i in range(1, PR):
         rows = rows + sums_ref[pl.ds(i, NH, stride=PR), :]
@@ -295,7 +295,7 @@
                 tile_at(found_ref, (d * NA + a) * KT + k)[...] = tile_at(image_ref, spot + a * XC)[...]
             return carry
 
-        lax.fori_loop(0, KT, body, 0, unroll=8)
+        lax.fori_loop(0, KT, body, 0, unroll=16)
     clear(field_ref)
 
 
@@ -320,7 +320,7 @@
             tile_at(rebuilt, a * KT + k)[...] = tile_at(field_ref, base + a * XC)[...]
         return carry
 
-    lax.fori_loop(0, KT, body, 0, unroll=8)
+    lax.fori_loop(0, KT, body, 0, unroll=16)
     traces = jnp.concatenate([trace_ref[d * KT : (d + 1) * KT, :]] * NA, axis=0)
     ratio = fold(d * NA * KT, found_ref, traces) / (fold(0, rebuilt, traces) + EPSILON)
     return (rows_ref[0 : NA * KT, :].astype(F32) * ratio).astype(BF16)

time: 106 us -> 106 us (level)
  no operation moved by 1% of the time
where the time goes in v6:
time: 106 us
  waiting for transfers between devices  53.8 us (51%)
  Pallas kernels  25.6 us (24%)
  starting transfers between devices  23 us (22%)
  between operations  1.42 us (1%)
  local copies, waits for them, and re-layouts  1.12 us (1%)
  other arithmetic  1.1 us (1%)
    all_to_all x1, waiting for transfers between devices, shards(): lax.all_to_all(sent.reshape(tiles * 2, XC, VOX), ('tile', 'nrn'), split_a...  43 us
    all_to_all x1, starting transfers between devices, shards(): lax.all_to_all(sent.reshape(tiles * 2, XC, VOX), ('tile', 'nrn'), split_a...  9.74 us
    pallas_call x1, Pallas kernels, shards(): call(numer_kernel, [pltpu.VMEM(((FIELD + PADF) * PR, VOX), F32), shape(2...  5.03 us
    pallas_call x1, Pallas kernels, shards(): call(register_kernel, shape(tiles * 2 * XC, BF16), [smem(), outside], scr...  5.01 us
    ppermute x1, waiting for transfers between devices, shards(): above = lax.ppermute(mine, 'tile', down)  4.89 us
    ppermute x1, waiting for transfers between devices, shards(): from_far = lax.ppermute(partial[:ROWS], 'tile', far)  3.92 us
    pallas_call x1, Pallas kernels, shards(): call(denom_kernel, pltpu.VMEM((TILES * PR + NH, VOX), F32), [smem()] + [v...  3.7 us
    pallas_call x1, Pallas kernels, shards(): call(lower_kernel, [shape(NH, F32), pltpu.VMEM((2 * FIELD * PR, VOX), F32...  3.64 us
  transfers between devices with their start and end apart: 11, of which 6 were waited for; matrix products, arithmetic and copies ran while one was open for 1% of the time, Pallas kernels for 14%

profile of v6, /device:TPU:1, one launch (start us, length us, event | category | flops | bytes accessed | tf_op | source)
XLA Modules:
  0.0 106.1 jit_solution(2275637474925787513)
XLA Ops:
  1.3 1.3 %rows.1 = bf16[480,128]{1,0:T(8,128)(2,1)S(1)} custom-call(s32[1]{0:T(128)S(6)} %copy.14.count_ref, s32[16,96]{1,0:T(8,128)} %bitcast.24, bf16[1536,128]{1,0:T(8,128)(2,1)} %bitcast.19), custom_call_target="tpu_custom_call" | custom-call | tf_op jit(solution)/shard_map/rows/pallas_call | solution.py:381
  2.6 2.1 %collective-permute-start = (bf16[480,128]{1,0:T(8,128)(2,1)S(1)}, bf16[480,128]{1,0:T(8,128)(2,1)S(1)}, u32[]{:S(2)}, u32[]{:S(2)}) collective-permute-start(bf16[480,128]{1,0:T(8,128)(2,1)S(1)} %rows.1), channel_id=1, source_target_pairs={{0,2},{2,4},{4,6},{6,8},{8,10},{10,12},{12,14},{14,16},{16,18},{18... | collective-permute-start | bytes 368648 | tf_op jit(solution)/shard_map/ppermute | solution.py:384
  4.7 1.3 %collective-permute-start.2 = (f32[96,4]{0,1:T(4,128)}, f32[96,4]{0,1:T(4,128)S(1)}, u32[]{:S(2)}, u32[]{:S(2)}) collective-permute-start(f32[96,4]{0,1:T(4,128)} %bitcast.27), channel_id=1, source_target_pairs={{0,1},{1,0},{2,3},{3,2},{4,5},{5,4},{6,7},{7,6},{8,9},{9,8},{10,11... | collective-permute-start | bytes 4616 | tf_op jit(solution)/shard_map/ppermute | solution.py:375
  6.0 0.9 collective-permute-start.1
  6.9 5.0 %register.1 = bf16[8192,128]{1,0:T(8,128)(2,1)} custom-call(s32[2]{0:T(128)} %bitcast.34, bf16[1024,1024]{1,0:T(8,128)(2,1)} %bitcast.18), custom_call_target="tpu_custom_call" | custom-call | tf_op jit(solution)/shard_map/register/pallas_call | solution.py:388
  11.9 0.0 copy-start.2
  11.9 0.0 collective-permute-done.2
  11.9 4.9 %collective-permute-done.1 = f32[96,4]{0,1:T(4,128)S(1)} collective-permute-done((f32[96,4]{0,1:T(4,128)}, f32[96,4]{0,1:T(4,128)S(1)}, u32[]{:S(2)}, u32[]{:S(2)}) %collective-permute-start.1) | collective-permute-done | bytes 1568 | tf_op jit(solution)/shard_map/ppermute | solution.py:374
  16.8 0.0 collective-permute-done.packet_ref
  16.8 9.7 %all-to-all-start = ((bf16[256,32,128]{2,1,0:T(8,128)(2,1)}), bf16[256,32,128]{2,1,0:T(8,128)(2,1)}, u32[]{:S(2)}, u32[]{:S(2)}) async-start(bf16[256,32,128]{2,1,0:T(8,128)(2,1)} %bitcast.10), calls=%async_computation | async-start | bytes 4194304 | tf_op jit(solution)/shard_map/all_to_all | solution.py:397
  26.6 0.2 add_reduce_fusion.1
  26.8 2.3 %collective-permute-start.3 = (f32[96,4]{0,1:T(4,128)S(1)}, f32[96,4]{0,1:T(4,128)S(1)}, u32[]{:S(2)}, u32[]{:S(2)}) collective-permute-start(f32[96,4]{0,1:T(4,128)S(1)} %collective-permute-done.1), channel_id=1, source_target_pairs={{0,1},{1,0},{2,3},{3,2},{4,5},{5,4},{6,7},{7,6},{8,9},{9,8},{10,11... | collective-permute-start | bytes 4616 | tf_op jit(solution)/shard_map/ppermute | solution.py:407
  29.1 0.2 select_reduce_fusion
  29.3 0.1 pad_add_fusion
  29.3 1.9 %own_rows.1 = (bf16[384,128]{1,0:T(8,128)(2,1)}, s32[96,128]{1,0:T(8,128)S(1)}) custom-call(s32[1]{0:T(128)S(6)} %copy.14.count_ref, s32[16,96]{1,0:T(8,128)} %bitcast.25, bf16[1536,128]{1,0:T(8,128)(2,1)} %bitcast.20, bf16[480,128]{1,0:T(8,128)(2,1)S(1)} %collective-permute-done.packet_ref), custom_call_target="tpu_custom_call" | custom-call | tf_op jit(solution)/shard_map/own_rows/pallas_call | solution.py:401
  31.3 0.0 collective-permute-done.3
  31.3 0.0 copy-done.2
  31.3 0.1 fusion.1
  31.4 0.1 copy.10.trace_ref.old_ref
  31.5 0.0 copy-start
  31.5 0.9 copy-done
  32.4 3.7 %denominator.1.tiles_ref = f32[6336,128]{1,0:T(8,128)S(1)} custom-call(s32[192]{0:T(256)S(1)} %get-tuple-element.43.place_ref, bf16[384,128]{1,0:T(8,128)(2,1)S(1)} %copy-done, bf16[480,128]{1,0:T(8,128)(2,1)S(1)} %collective-permute-done.packet_ref, f32[192,128]{1,0:T(8,128)S(1)} %copy.10.trace_ref.old_ref), custom_call_target="tpu_custom_call" | custom-call | tf_op jit(solution)/shard_map/denominator/pallas_call | solution.py:422
  36.1 43.0 %all-to-all-done = bf16[256,32,128]{2,1,0:T(8,128)(2,1)} async-done(((bf16[256,32,128]{2,1,0:T(8,128)(2,1)}), bf16[256,32,128]{2,1,0:T(8,128)(2,1)}, u32[]{:S(2)}, u32[]{:S(2)}) %all-to-all-start) | async-done | bytes 2097184 | tf_op jit(solution)/shard_map/all_to_all | solution.py:397
  79.1 5.0 %numerator.1 = (f32[9216,128]{1,0:T(8,128)S(1)}, f32[32,128]{1,0:T(8,128)S(1)}) custom-call(s32[192]{0:T(256)S(1)} %get-tuple-element.42.place_ref.spot_ref, f32[6336,128]{1,0:T(8,128)S(1)} %denominator.1.tiles_ref, bf16[8192,128]{1,0:T(8,128)(2,1)} %bitcast.11.image_ref), custom_call_target="tpu_custom_call" | custom-call | tf_op jit(solution)/shard_map/numerator/pallas_call | solution.py:427
  84.1 0.9 collective-permute-start.4
  85.0 0.8 collective-permute-done.4
  85.9 1.4 %collective-permute-start.6 = (f32[16,128]{1,0:T(8,128)S(1)}, f32[16,128]{1,0:T(8,128)S(1)}, u32[]{:S(2)}, u32[]{:S(2)}) collective-permute-start(f32[16,128]{1,0:T(8,128)S(1)} %get-tuple-element.38), channel_id=1, source_target_pairs={{0,254},{2,4},{4,2},{6,8},{8,6},{10,12},{12,10},{14,16},{16,14},{1... | collective-permute-start | bytes 24584 | tf_op jit(solution)/shard_map/ppermute | solution.py:443
  87.3 0.7 collective-permute-start.5
  88.0 1.9 %stage.1 = (f32[6144,128]{1,0:T(8,128)S(1)}, f32[16384,128]{1,0:T(8,128)S(1)}, bf16[128,1536]{1,0:T(8,128)(2,1)S(1)}) custom-call(s32[192]{0:T(256)S(1)} %get-tuple-element.42.place_ref.spot_ref, f32[9216,128]{1,0:T(8,128)S(1)} %get-tuple-element.26.image_ref), custom_call_target="tpu_custom_call" | custom-call | tf_op jit(solution)/shard_map/stage/pallas_call | solution.py:447
  89.9 3.9 %collective-permute-done.6.far_ref = f32[16,128]{1,0:T(8,128)S(1)} collective-permute-done((f32[16,128]{1,0:T(8,128)S(1)}, f32[16,128]{1,0:T(8,128)S(1)}, u32[]{:S(2)}, u32[]{:S(2)}) %collective-permute-start.6) | collective-permute-done | bytes 8224 | tf_op jit(solution)/shard_map/ppermute | solution.py:443
  93.8 0.0 collective-permute-done.5.near_ref
  93.8 0.0 copy-start.1
  93.8 3.6 %lower.1 = (f32[192,128]{1,0:T(8,128)S(1)}, f32[16384,128]{1,0:T(8,128)S(1)}, bf16[384,128]{1,0:T(8,128)(2,1)}) custom-call(s32[192]{0:T(256)S(1)} %get-tuple-element.43.place_ref, bf16[480,128]{1,0:T(8,128)(2,1)S(1)} %collective-permute-done.packet_ref, f32[6336,128]{1,0:T(8,128)S(1)} %denominator.1.tiles_ref, ...), custom_call_target="tpu_custom_call", output_to_operand_aliasing={{1}: (9, {})} | custom-call | tf_op jit(solution)/shard_map/lower/pallas_call | solution.py:457
  97.5 3.2 %collective-permute-start.9 = (bf16[384,128]{1,0:T(8,128)(2,1)}, bf16[384,128]{1,0:T(8,128)(2,1)S(1)}, u32[]{:S(2)}, u32[]{:S(2)}) collective-permute-start(bf16[384,128]{1,0:T(8,128)(2,1)} %get-tuple-element.34), channel_id=1, source_target_pairs={{2,1},{3,0},{4,3},{5,2},{6,5},{7,4},{8,7},{9,6},{10,9},{11,8},{12,... | collective-permute-start | bytes 294920 | tf_op jit(solution)/shard_map/ppermute | solution.py:464
  100.7 0.0 collective-permute-start.7
  100.7 0.0 copy-done.1
  100.7 1.9 %upper.1 = (bf16[384,128]{1,0:T(8,128)(2,1)S(1)}, bf16[384,128]{1,0:T(8,128)(2,1)S(1)}) custom-call(s32[192]{0:T(256)S(1)} %get-tuple-element.43.place_ref, bf16[384,128]{1,0:T(8,128)(2,1)S(1)} %copy-done.1, f32[6144,128]{1,0:T(8,128)S(1)} %get-tuple-element.27.found_ref, f32[16384,128]{1,0:T(8,128)S(1)} %get-tuple-element.32.field_ref, ...), custom_call_target="tpu_custom_call" | custom-call | tf_op jit(solution)/shard_map/upper/pallas_call | solution.py:465
  102.5 0.1 copy.12
  102.6 0.5 collective-permute-start.8
  103.2 0.6 broadcast_select_fusion
  103.7 0.4 collective-permute-done.8.upper_other
  104.1 0.0 collective-permute-done.9.lower_other
  104.1 0.8 collective-permute-done.7.lower_ref
  104.9 1.2 %merge.1 = bf16[1536,128]{1,0:T(8,128)(2,1)} custom-call(s32[96,128]{1,0:T(8,128)S(1)} %get-tuple-element.31.odd_ref, bf16[384,128]{1,0:T(8,128)(2,1)S(1)} %get-tuple-element.33.upper_ref, bf16[384,128]{1,0:T(8,128)(2,1)S(1)} %collective-permute-done.7.lower_ref, bf16[384,128]{1,0:T(8,128)(2,1)S(1)} %collective-permute-done.8.upper_other, ...), custom_call_target="tpu_custom_call" | custom-call | tf_op jit(solution)/shard_map/merge/pallas_call | solution.py:470
  (8 shorter events, 0.1 us)
Async XLA Ops:
  2.6 14.2 %collective-permute-start = (bf16[480,128]{1,0:T(8,128)(2,1)S(1)}, bf16[480,128]{1,0:T(8,128)(2,1)S(1)}, u32[]{:S(2)}, u32[]{:S(2)}) collective-permute-start(bf16[480,128]{1,0:T(8,128)(2,1)S(1)} %rows.1), channel_id=1, source_target_pairs={{0,2},{2,4},{4,6},{6,8},{8,10},{10,12},{12,14},{14,16},{16,18},{18... | collective-permute-start | bytes 368648 | tf_op jit(solution)/shard_map/ppermute | solution.py:384
  4.7 7.2 %collective-permute-start.2 = (f32[96,4]{0,1:T(4,128)}, f32[96,4]{0,1:T(4,128)S(1)}, u32[]{:S(2)}, u32[]{:S(2)}) collective-permute-start(f32[96,4]{0,1:T(4,128)} %bitcast.27), channel_id=1, source_target_pairs={{0,1},{1,0},{2,3},{3,2},{4,5},{5,4},{6,7},{7,6},{8,9},{9,8},{10,11... | collective-permute-start | bytes 4616 | tf_op jit(solution)/shard_map/ppermute | solution.py:375
  6.0 10.8 %collective-permute-start.1 = (f32[96,4]{0,1:T(4,128)}, f32[96,4]{0,1:T(4,128)S(1)}, u32[]{:S(2)}, u32[]{:S(2)}) collective-permute-start(f32[96,4]{0,1:T(4,128)} %bitcast.28), channel_id=1, source_target_pairs={{0,2},{2,4},{4,6},{6,8},{8,10},{10,12},{12,14},{14,16},{16,18},{18... | collective-permute-start | bytes 4616 | tf_op jit(solution)/shard_map/ppermute | solution.py:374
  11.9 19.4 %copy-start.2 = (f32[1,96,4]{1,2,0:T(4,128)S(1)}, f32[1,96,4]{1,2,0:T(4,128)}, u32[]{:S(2)}) copy-start(f32[1,96,4]{1,2,0:T(4,128)} %param.10) | copy-start | bytes 4612
  16.8 62.3 %all-to-all-start = ((bf16[256,32,128]{2,1,0:T(8,128)(2,1)}), bf16[256,32,128]{2,1,0:T(8,128)(2,1)}, u32[]{:S(2)}, u32[]{:S(2)}) async-start(bf16[256,32,128]{2,1,0:T(8,128)(2,1)} %bitcast.10), calls=%async_computation | async-start | bytes 4194304 | tf_op jit(solution)/shard_map/all_to_all | solution.py:397
  26.8 4.5 %collective-permute-start.3 = (f32[96,4]{0,1:T(4,128)S(1)}, f32[96,4]{0,1:T(4,128)S(1)}, u32[]{:S(2)}, u32[]{:S(2)}) collective-permute-start(f32[96,4]{0,1:T(4,128)S(1)} %collective-permute-done.1), channel_id=1, source_target_pairs={{0,1},{1,0},{2,3},{3,2},{4,5},{5,4},{6,7},{7,6},{8,9},{9,8},{10,11... | collective-permute-start | bytes 4616 | tf_op jit(solution)/shard_map/ppermute | solution.py:407
  31.5 0.9 copy-start
  84.1 1.8 %collective-permute-start.4 = (f32[32,128]{1,0:T(8,128)S(1)}, f32[32,128]{1,0:T(8,128)S(1)}, u32[]{:S(2)}, u32[]{:S(2)}) collective-permute-start(f32[32,128]{1,0:T(8,128)S(1)} %get-tuple-element.25), channel_id=1, source_target_pairs={{0,1},{1,0},{2,3},{3,2},{4,5},{5,4},{6,7},{7,6},{8,9},{9,8},{10,11... | collective-permute-start | bytes 49160 | tf_op jit(solution)/shard_map/ppermute | solution.py:440
  85.9 7.9 %collective-permute-start.6 = (f32[16,128]{1,0:T(8,128)S(1)}, f32[16,128]{1,0:T(8,128)S(1)}, u32[]{:S(2)}, u32[]{:S(2)}) collective-permute-start(f32[16,128]{1,0:T(8,128)S(1)} %get-tuple-element.38), channel_id=1, source_target_pairs={{0,254},{2,4},{4,2},{6,8},{8,6},{10,12},{12,10},{14,16},{16,14},{1... | collective-permute-start | bytes 24584 | tf_op jit(solution)/shard_map/ppermute | solution.py:443
  87.3 6.5 %collective-permute-start.5 = (f32[16,128]{1,0:T(8,128)S(1)}, f32[16,128]{1,0:T(8,128)S(1)}, u32[]{:S(2)}, u32[]{:S(2)}) collective-permute-start(f32[16,128]{1,0:T(8,128)S(1)} %get-tuple-element.39), channel_id=1, source_target_pairs={{0,2},{2,0},{4,6},{6,4},{8,10},{10,8},{12,14},{14,12},{16,18},{18,... | collective-permute-start | bytes 24584 | tf_op jit(solution)/shard_map/ppermute | solution.py:444
  93.8 6.8 %copy-start.1 = (bf16[384,128]{1,0:T(8,128)(2,1)S(1)}, bf16[384,128]{1,0:T(8,128)(2,1)}, u32[]{:S(2)}) copy-start(bf16[384,128]{1,0:T(8,128)(2,1)} %get-tuple-element.20.upper_ref) | copy-start | bytes 294916
  97.5 6.6 %collective-permute-start.9 = (bf16[384,128]{1,0:T(8,128)(2,1)}, bf16[384,128]{1,0:T(8,128)(2,1)S(1)}, u32[]{:S(2)}, u32[]{:S(2)}) collective-permute-start(bf16[384,128]{1,0:T(8,128)(2,1)} %get-tuple-element.34), channel_id=1, source_target_pairs={{2,1},{3,0},{4,3},{5,2},{6,5},{7,4},{8,7},{9,6},{10,9},{11,8},{12,... | collective-permute-start | bytes 294920 | tf_op jit(solution)/shard_map/ppermute | solution.py:464
  100.7 4.2 %collective-permute-start.7 = (bf16[384,128]{1,0:T(8,128)(2,1)}, bf16[384,128]{1,0:T(8,128)(2,1)S(1)}, u32[]{:S(2)}, u32[]{:S(2)}) collective-permute-start(bf16[384,128]{1,0:T(8,128)(2,1)} %get-tuple-element.34), channel_id=1, source_target_pairs={{2,0},{4,2},{6,4},{8,6},{10,8},{12,10},{14,12},{16,14},{18,16},{20... | collective-permute-start | bytes 294920 | tf_op jit(solution)/shard_map/ppermute | solution.py:463
  102.6 1.4 %collective-permute-start.8 = (bf16[384,128]{1,0:T(8,128)(2,1)S(1)}, bf16[384,128]{1,0:T(8,128)(2,1)S(1)}, u32[]{:S(2)}, u32[]{:S(2)}) collective-permute-start(bf16[384,128]{1,0:T(8,128)(2,1)S(1)} %get-tuple-element.35), channel_id=1, source_target_pairs={{0,1},{1,0},{2,3},{3,2},{4,5},{5,4},{6,7},{7,6},{8,9},{9,8},{10,11... | collective-permute-start | bytes 294920 | tf_op jit(solution)/shard_map/ppermute | solution.py:469
